TPU v7x, 32 devices: a whole 2x2x4 slice. The times are simulated.
32 devices in a mesh: wide: 8 (over y, x, core), narrow: 4 (over z).
Axes of the slice: x: 2, y: 2, z: 4, core: 2. Of those that a mesh axis runs over, the one named last changes fastest.
Arguments:
- layer_input: bfloat16 [2, 8, 256, 2048], P(None, 'wide', 'narrow'), may hold values from -6 to 6
- document_lengths: int32 [2, 8, 4], P(None, 'wide'), may hold values from 1 to 128, 256 in all within a row
- attn_gain: bfloat16 [2048], replicated, may hold values from 0.5 to 1.5
- w_query: bfloat16 [2048, 2048], P(None, 'narrow'), may hold values from -0.125 to 0.125
- w_key: bfloat16 [2048, 1024], P(None, 'narrow'), may hold values from -0.125 to 0.125
- w_value: bfloat16 [2048, 1024], P(None, 'narrow'), may hold values from -0.125 to 0.125
- query_gain: bfloat16 [128], replicated, may hold values from 1 to 2.5
- key_gain: bfloat16 [128], replicated, may hold values from 1 to 2.5
- w_out: bfloat16 [2048, 2048], P('narrow'), may hold values from -0.75 to 0.75
- mlp_gain: bfloat16 [2048], replicated, may hold values from 0.5 to 1.5
- w_gate: bfloat16 [2048, 6144], P(None, 'narrow'), may hold values from -0.125 to 0.125
- w_up: bfloat16 [2048, 6144], P(None, 'narrow'), may hold values from -0.125 to 0.125
- w_down: bfloat16 [6144, 2048], P('narrow'), may hold values from -0.078125 to 0.078125
- output_cotangent: bfloat16 [2, 8, 256, 2048], P(None, 'wide', 'narrow'), may hold values from -6 to 6
Outputs:
- layer_out: float32 [2, 8, 256, 2048], P(None, 'wide', 'narrow')
- in_grad: float32 [2, 8, 256, 2048], P(None, 'wide', 'narrow')
- attn_gain_grad: float32 [2048], replicated
- w_query_grad: float32 [2048, 2048], P('wide', 'narrow')
- w_key_grad: float32 [2048, 1024], P('wide', 'narrow')
- w_value_grad: float32 [2048, 1024], P('wide', 'narrow')
- query_gain_grad: float32 [128], replicated
- key_gain_grad: float32 [128], replicated
- w_out_grad: float32 [2048, 2048], P('narrow', 'wide')
- mlp_gain_grad: float32 [2048], replicated
- w_gate_grad: float32 [2048, 6144], P('wide', 'narrow')
- w_up_grad: float32 [2048, 6144], P('wide', 'narrow')
- w_down_grad: float32 [6144, 2048], P('narrow', 'wide')
Inputs may be any that keep to these rules, and one draw needn't show every extreme that they name: `document_lengths`: each row's 4 document lengths sum to 256, and in every row the longest is exactly 128.
All inputs are finite; a program needn't handle non-finite values.
Results may differ from a plain program's by a relative error of at most 0.013.
The roundings to bfloat16 on the way count: a program that leaves them out, or rounds other values in their place, can miss the bound.
Values may be sent and summed in bfloat16 or wider, within the bound.
A program may use at most 192 MiB of HBM per device.

v0:
```python
import jax
import jax.numpy as jnp
from jax import lax
from jax.sharding import PartitionSpec as P

norm_eps = 1e-06
masked_score = -1e30


def rms_scale(values):
    return lax.rsqrt(jnp.mean(values * values, axis=-1, keepdims=True) + norm_eps)


def rms_back(grad_in, normed_hat, scale_rows):
    return scale_rows * (
        grad_in - normed_hat * jnp.mean(grad_in * normed_hat, axis=-1, keepdims=True)
    )


def doc_layout(lengths, seq_len):
    doc_ends = jnp.cumsum(lengths)
    starts = doc_ends - lengths
    places = lax.iota(jnp.int32, seq_len)
    segment = jnp.sum((places[:, None] >= doc_ends[None, :]).astype(jnp.int32), axis=1)
    member = segment[:, None] == lax.iota(jnp.int32, lengths.shape[0])[None, :]
    doc_first = jnp.sum(jnp.where(member, starts[None, :], 0), axis=1)
    allowed = (segment[:, None] == segment[None, :]) & (places[None, :] <= places[:, None])
    return (places - doc_first, allowed)


def rope_tables(inside, head_dim):
    half_dim = head_dim // 2
    frequency = jnp.power(1000000.0, -2.0 * lax.iota(jnp.float32, half_dim) / head_dim)
    angles = inside.astype(jnp.float32)[:, None] * frequency[None, :]
    return (jnp.cos(angles), jnp.sin(angles))


def rotate(values, cos_table, sine_table):
    half_dim = values.shape[-1] // 2
    first_half = values[..., :half_dim]
    second = values[..., half_dim:]
    cos_wide = cos_table[:, None, :]
    sine_wide = sine_table[:, None, :]
    return jnp.concatenate(
        [first_half * cos_wide - second * sine_wide, second * cos_wide + first_half * sine_wide],
        axis=-1,
    )


def contract_rows(left_side, right_side):
    return lax.dot_general(
        left_side, right_side, (((0,), (0,)), ((), ())), preferred_element_type=jnp.float32
    )


def contract_cols(left_side, right_side):
    return lax.dot_general(
        left_side, right_side, (((1,), (1,)), ((), ())), preferred_element_type=jnp.float32
    )


def row_product(source, weight):
    return jnp.dot(source, weight, preferred_element_type=jnp.float32)


def row_back_product(source, weight):
    return contract_cols(source, weight)


def attention_scores(grouped, key_rot, allowed, score_scale):
    raw_scores = (
        jnp.einsum("tkgd,ukd->kgtu", grouped, key_rot, preferred_element_type=jnp.float32)
        * score_scale
    )
    return jnp.where(allowed[None, None], raw_scores, masked_score)


def local(
    layer_input,
    document_lengths,
    attn_gain,
    w_query,
    w_key,
    w_value,
    query_gain,
    key_gain,
    w_out,
    mlp_gain,
    w_gate,
    w_up,
    w_down,
    output_cotangent,
):
    shard_rows = layer_input.shape[2]
    seq_len = shard_rows * lax.axis_size("narrow")
    head_dim = query_gain.shape[0]
    query_cols = w_query.shape[1]
    key_cols = w_key.shape[1]
    query_heads = query_cols // head_dim
    kv_local = key_cols // head_dim
    group_size = query_cols // key_cols
    ff_cols = w_gate.shape[1]
    score_scale = head_dim ** (-0.5)
    w_qkv = jnp.concatenate([w_query, w_key, w_value], axis=1)
    w_both = jnp.concatenate([w_gate, w_up], axis=1)
    attn_gain_f = attn_gain.astype(jnp.float32)
    query_gain_f = query_gain.astype(jnp.float32)
    key_gain_f = key_gain.astype(jnp.float32)
    mlp_gain_f = mlp_gain.astype(jnp.float32)
    totals = None
    small_totals = None
    outputs_list = []
    in_grads = []
    for micro_step in range(layer_input.shape[0]):
        rows_in = layer_input[micro_step, 0].astype(jnp.float32)
        inside, allowed = doc_layout(document_lengths[micro_step, 0], seq_len)
        cos_table, sine_table = rope_tables(inside, head_dim)
        scale_one = rms_scale(rows_in)
        hat_one = rows_in * scale_one
        normed = (hat_one * attn_gain_f).astype(jnp.bfloat16)
        normed_full = lax.all_gather(normed, "narrow", axis=0, tiled=True)
        projected = jnp.dot(normed_full, w_qkv, preferred_element_type=jnp.float32)
        query_raw = projected[:, :query_cols].reshape(seq_len, query_heads, head_dim)
        key_raw = projected[:, query_cols : query_cols + key_cols].reshape(
            seq_len, kv_local, head_dim
        )
        value_rows = (
            projected[:, query_cols + key_cols :]
            .astype(jnp.bfloat16)
            .reshape(seq_len, kv_local, head_dim)
        )
        query_scale = rms_scale(query_raw)
        query_hat = query_raw * query_scale
        query_rot = rotate(query_hat * query_gain_f, cos_table, sine_table).astype(jnp.bfloat16)
        key_scale = rms_scale(key_raw)
        key_hat = key_raw * key_scale
        key_rot = rotate(key_hat * key_gain_f, cos_table, sine_table).astype(jnp.bfloat16)
        grouped = query_rot.reshape(seq_len, kv_local, group_size, head_dim)
        scores = attention_scores(grouped, key_rot, allowed, score_scale)
        top_score = jnp.max(scores, axis=-1, keepdims=True)
        exponent = jnp.exp(scores - top_score)
        total_mass = jnp.sum(exponent, axis=-1, keepdims=True)
        log_mass = top_score + jnp.log(total_mass)
        prob_low = (exponent / total_mass).astype(jnp.bfloat16)
        attn_mix = jnp.einsum(
            "kgtu,ukd->tkgd", prob_low, value_rows, preferred_element_type=jnp.float32
        )
        attn_mix = attn_mix.reshape(seq_len, query_cols).astype(jnp.bfloat16)
        attn_branch = lax.psum_scatter(
            row_product(attn_mix, w_out), "narrow", scatter_dimension=0, tiled=True
        )
        middle = rows_in + attn_branch
        scale_two = rms_scale(middle)
        hat_two = middle * scale_two
        normed_two = (hat_two * mlp_gain_f).astype(jnp.bfloat16)
        normed_two_full = lax.all_gather(normed_two, "narrow", axis=0, tiled=True)
        gate_up = jnp.dot(normed_two_full, w_both, preferred_element_type=jnp.float32)
        gate_pre = gate_up[:, :ff_cols]
        up_proj = gate_up[:, ff_cols:]
        sigmoid_gate = jax.nn.sigmoid(gate_pre)
        silu_gate = gate_pre * sigmoid_gate
        activated = (silu_gate * up_proj).astype(jnp.bfloat16)
        mlp_branch = lax.psum_scatter(
            row_product(activated, w_down).astype(jnp.bfloat16),
            "narrow",
            scatter_dimension=0,
            tiled=True,
        ).astype(jnp.float32)
        outputs_list.append(middle + mlp_branch)
        cot_rows = output_cotangent[micro_step, 0]
        cot_full = lax.all_gather(cot_rows, "narrow", axis=0, tiled=True)
        grad_down = contract_rows(activated, cot_full)
        d_act = contract_cols(cot_full, w_down)
        d_gate = d_act * up_proj * sigmoid_gate * (1.0 + gate_pre * (1.0 - sigmoid_gate))
        d_up = d_act * silu_gate
        d_both = jnp.concatenate([d_gate, d_up], axis=1).astype(jnp.bfloat16)
        grad_both = contract_rows(normed_two_full, d_both)
        d_normed_two = lax.psum_scatter(
            row_back_product(d_both, w_both), "narrow", scatter_dimension=0, tiled=True
        )
        mlp_gain_part = jnp.sum(d_normed_two * hat_two, axis=0)
        d_middle = cot_rows.astype(jnp.float32) + rms_back(
            d_normed_two * mlp_gain_f, hat_two, scale_two
        )
        d_branch = d_middle.astype(jnp.bfloat16)
        d_branch_full = lax.all_gather(d_branch, "narrow", axis=0, tiled=True)
        grad_out = contract_rows(attn_mix, d_branch_full)
        d_mix = contract_cols(d_branch_full, w_out).astype(jnp.bfloat16)
        d_mix = d_mix.reshape(seq_len, kv_local, group_size, head_dim)
        d_prob = jnp.einsum("tkgd,ukd->kgtu", d_mix, value_rows, preferred_element_type=jnp.float32)
        scores_again = attention_scores(grouped, key_rot, allowed, score_scale)
        prob_again = jnp.exp(scores_again - log_mass)
        prob_back_low = prob_again.astype(jnp.bfloat16)
        d_value = jnp.einsum(
            "kgtu,tkgd->ukd", prob_back_low, d_mix, preferred_element_type=jnp.float32
        )
        d_score = prob_again * (d_prob - jnp.sum(prob_again * d_prob, axis=-1, keepdims=True))
        d_score = d_score.astype(jnp.bfloat16)
        d_query = jnp.einsum("kgtu,ukd->tkgd", d_score, key_rot, preferred_element_type=jnp.float32)
        d_query = d_query.reshape(seq_len, query_heads, head_dim) * score_scale
        d_key = (
            jnp.einsum("kgtu,tkgd->ukd", d_score, grouped, preferred_element_type=jnp.float32)
            * score_scale
        )
        d_query_norm = rotate(d_query, cos_table, -sine_table)
        d_key_norm = rotate(d_key, cos_table, -sine_table)
        query_gain_part = jnp.sum(d_query_norm * query_hat, axis=(0, 1))
        key_gain_part = jnp.sum(d_key_norm * key_hat, axis=(0, 1))
        d_query_raw = rms_back(d_query_norm * query_gain_f, query_hat, query_scale)
        d_key_raw = rms_back(d_key_norm * key_gain_f, key_hat, key_scale)
        d_proj = jnp.concatenate(
            [
                d_query_raw.reshape(seq_len, query_cols),
                d_key_raw.reshape(seq_len, key_cols),
                d_value.reshape(seq_len, key_cols),
            ],
            axis=1,
        ).astype(jnp.bfloat16)
        grad_qkv = contract_rows(normed_full, d_proj)
        d_normed = lax.psum_scatter(
            row_back_product(d_proj, w_qkv), "narrow", scatter_dimension=0, tiled=True
        )
        attn_gain_part = jnp.sum(d_normed * hat_one, axis=0)
        in_grads.append(d_middle + rms_back(d_normed * attn_gain_f, hat_one, scale_one))
        grads_now = (grad_qkv, grad_both, grad_out, grad_down)
        small_now = (attn_gain_part, query_gain_part, key_gain_part, mlp_gain_part)
        if totals is None:
            totals = grads_now
            small_totals = small_now
        else:
            totals = tuple((running + extra for running, extra in zip(totals, grads_now)))
            small_totals = tuple(
                (running + extra for running, extra in zip(small_totals, small_now))
            )
    totals = (
        lax.psum_scatter(totals[0], "wide", scatter_dimension=0, tiled=True),
        lax.psum_scatter(totals[1], "wide", scatter_dimension=0, tiled=True),
        lax.psum_scatter(totals[2], "wide", scatter_dimension=1, tiled=True),
        lax.psum_scatter(totals[3], "wide", scatter_dimension=1, tiled=True),
    )
    small_sums = lax.psum(small_totals, ("wide", "narrow"))
    qkv_share, both_share, out_share, down_share = totals
    layer_out = jnp.stack(outputs_list)[:, None]
    in_grad = jnp.stack(in_grads)[:, None]
    return (
        layer_out,
        in_grad,
        small_sums[0],
        qkv_share[:, :query_cols],
        qkv_share[:, query_cols : query_cols + key_cols],
        qkv_share[:, query_cols + key_cols :],
        small_sums[1],
        small_sums[2],
        out_share,
        small_sums[3],
        both_share[:, :ff_cols],
        both_share[:, ff_cols:],
        down_share,
    )


def solution(mesh):
    in_specs = (
        P(None, "wide", "narrow", None),
        P(None, "wide", None),
        P(),
        P(None, "narrow"),
        P(None, "narrow"),
        P(None, "narrow"),
        P(),
        P(),
        P("narrow", None),
        P(),
        P(None, "narrow"),
        P(None, "narrow"),
        P("narrow", None),
        P(None, "wide", "narrow", None),
    )
    out_specs = (
        P(None, "wide", "narrow", None),
        P(None, "wide", "narrow", None),
        P(),
        P("wide", "narrow"),
        P("wide", "narrow"),
        P("wide", "narrow"),
        P(),
        P(),
        P("narrow", "wide"),
        P(),
        P("wide", "narrow"),
        P("wide", "narrow"),
        P("narrow", "wide"),
    )
    return jax.shard_map(local, mesh=mesh, in_specs=in_specs, out_specs=out_specs, check_vma=False)
```

profile of v0, /device:TPU:0, one launch (start us, length us, event | category | flops | bytes accessed | tf_op | source)
XLA Modules:
  0.0 1073.6 jit_solution(3452140487380955168)
XLA Ops:
  9.4 2.1 fusion.34
  18.1 3.2 constant_dynamic-update-slice_fusion.2
  23.4 18.8 %all-gather.11.cloned.1.call-done = bf16[256,2048]{1,0:T(8,128)(2,1)} async-done(((bf16[64,2048]{1,0:T(8,128)(2,1)}), bf16[256,2048]{1,0:T(8,128)(2,1)}) %all-gather.11.cloned.1.call-update) | async-done | bytes 1048592 | tf_op jit(solution)/shard_map/all_gather | solution.py:121
  42.3 3.8 fusion.110
  47.8 24.1 %all-gather.15.cloned.1.call-done = bf16[256,2048]{1,0:T(8,128)(2,1)} async-done(((bf16[64,2048]{1,0:T(8,128)(2,1)}), bf16[256,2048]{1,0:T(8,128)(2,1)}) %all-gather.15.cloned.1.call-update) | async-done | bytes 1048592 | tf_op jit(solution)/shard_map/all_gather | solution.py:121
  71.9 3.8 fusion.113
  82.0 2.2 multiply_multiply_fusion.1
  85.8 1.9 reshape.535
  87.7 2.0 multiply_reduce_fusion.15
  101.0 2.1 fusion.111
  112.0 2.1 fusion.114
  114.8 31.8 %reduce-scatter.13.cloned.1.call-done = f32[64,2048]{1,0:T(8,128)} async-done(((f32[256,2048]{1,0:T(8,128)}), f32[64,2048]{1,0:T(8,128)}) %reduce-scatter.13.cloned.1.call-update) | async-done | bytes 524304 | tf_op jit(solution)/shard_map/reduce_scatter | solution.py:149
  146.6 45.5 %reduce-scatter.17.cloned.1.call-done = f32[64,2048]{1,0:T(8,128)} async-done(((f32[256,2048]{1,0:T(8,128)}), f32[64,2048]{1,0:T(8,128)}) %reduce-scatter.17.cloned.1.call-update) | async-done | bytes 524304 | tf_op jit(solution)/shard_map/reduce_scatter | solution.py:149
  192.1 2.9 multiply_reduce_fusion.10
  196.7 1.9 fusion.107
  198.8 6.0 constant_dynamic-update-slice_fusion.4
  204.8 5.9 constant_dynamic-update-slice_fusion.3
  210.8 13.3 %all-gather.13.cloned.1.call-done = bf16[256,2048]{1,0:T(8,128)(2,1)} async-done(((bf16[64,2048]{1,0:T(8,128)(2,1)}), bf16[256,2048]{1,0:T(8,128)(2,1)}) %all-gather.13.cloned.1.call-update) | async-done | bytes 1048592 | tf_op jit(solution)/shard_map/all_gather | solution.py:156
  224.0 10.0 fusion.112
  234.0 19.5 %all-gather.23.cloned.1.call-done = bf16[1,1,256,2048]{3,2,1,0:T(8,128)(2,1)} async-done(((bf16[1,1,64,2048]{3,2,1,0:T(8,128)(2,1)}), bf16[1,1,256,2048]{3,2,1,0:T(8,128)(2,1)}) %all-gather.23.cloned.1.call-update) | async-done | bytes 1048592 | tf_op jit(solution)/shard_map/all_gather | solution.py:171
  253.5 7.2 multiply_convert_fusion.3
  261.9 9.4 fusion.21
  272.5 42.3 %reduce-scatter.21.cloned.1.call-done = f32[64,2048]{1,0:T(8,128)} async-done(((f32[256,2048]{1,0:T(8,128)}), f32[64,2048]{1,0:T(8,128)}) %reduce-scatter.21.cloned.1.call-update) | async-done | bytes 524304 | tf_op jit(solution)/shard_map/reduce_scatter | solution.py:178
  314.8 2.9 multiply_reduce_fusion.3
  318.9 26.2 %all-gather.17.cloned.1.call-done = bf16[256,2048]{1,0:T(8,128)(2,1)} async-done(((bf16[64,2048]{1,0:T(8,128)(2,1)}), bf16[256,2048]{1,0:T(8,128)(2,1)}) %all-gather.17.cloned.1.call-update) | async-done | bytes 1048592 | tf_op jit(solution)/shard_map/all_gather | solution.py:156
  345.1 10.0 fusion.115
  355.1 19.1 %all-gather.25.cloned.1.call-done = bf16[1,1,256,2048]{3,2,1,0:T(8,128)(2,1)} async-done(((bf16[1,1,64,2048]{3,2,1,0:T(8,128)(2,1)}), bf16[1,1,256,2048]{3,2,1,0:T(8,128)(2,1)}) %all-gather.25.cloned.1.call-update) | async-done | bytes 1048592 | tf_op jit(solution)/shard_map/all_gather | solution.py:171
  374.2 7.2 multiply_convert_fusion.1
  382.6 9.4 fusion.19
  392.1 5.8 convolution_convert_fusion
  399.1 36.4 %reduce-scatter.25.cloned.1.call-done = f32[64,2048]{1,0:T(8,128)} async-done(((f32[256,2048]{1,0:T(8,128)}), f32[64,2048]{1,0:T(8,128)}) %reduce-scatter.25.cloned.1.call-update) | async-done | bytes 524304 | tf_op jit(solution)/shard_map/reduce_scatter | solution.py:178
  435.5 2.0 multiply_reduce_fusion.2
  438.1 26.9 %reduce-scatter.19.cloned.1.call-done = bf16[64,2048]{1,0:T(8,128)(2,1)} async-done(((bf16[256,2048]{1,0:T(8,128)(2,1)}), bf16[64,2048]{1,0:T(8,128)(2,1)}) %reduce-scatter.19.cloned.1.call-update) | async-done | bytes 262160 | tf_op jit(solution)/shard_map/reduce_scatter | solution.py:163
  464.9 2.9 fusion.99
  473.6 21.0 %all-gather.19.cloned.1.call-done = bf16[256,2048]{1,0:T(8,128)(2,1)} async-done(((bf16[64,2048]{1,0:T(8,128)(2,1)}), bf16[256,2048]{1,0:T(8,128)(2,1)}) %all-gather.19.cloned.1.call-update) | async-done | bytes 1048592 | tf_op jit(solution)/shard_map/all_gather | solution.py:186
  494.6 2.7 convolution_convert_fusion.3
  497.3 1.8 copy.291
  499.1 2.3 fusion.10
  501.4 3.3 multiply_reduce_fusion.1
  504.7 19.0 %all-gather.21.cloned.1.call-done = bf16[256,2048]{1,0:T(8,128)(2,1)} async-done(((bf16[64,2048]{1,0:T(8,128)(2,1)}), bf16[256,2048]{1,0:T(8,128)(2,1)}) %all-gather.21.cloned.1.call-update) | async-done | bytes 1048592 | tf_op jit(solution)/shard_map/all_gather | solution.py:186
  523.7 2.7 convolution_convert_fusion.2
  537.8 2.4 multiply_reduce_fusion.13
  544.3 1.9 copy.285
  549.1 4.4 multiply_reduce_fusion.6
  556.5 4.8 fusion.76
  570.8 4.9 fusion.74
  575.8 5.7 convolution_convert_fusion.1
  581.6 2.3 fusion.75
  583.9 4.6 convolution_add_fusion.2
  589.7 11.6 %fusion.20 = f32[2048,3072]{1,0:T(8,128)} fusion(bf16[256,2048]{1,0:T(8,128)(2,1)S(1)} %copy-done.44, bf16[256,1536]{1,0:T(8,128)(2,1)} %copy-done.67, bf16[256,1536]{1,0:T(8,128)(2,1)} %copy-done.66), kind=kOutput, calls=%fused_computation.62 | convolution fusion | flops 3224371200 | bytes 27787264 | tf_op jit(solution)/shard_map/dot_general | solution.py:51
  601.3 16.9 %convolution_add_fusion = f32[2048,3072]{1,0:T(8,128)} fusion(f32[2048,3072]{1,0:T(8,128)} %fusion.20, bf16[256,2048]{1,0:T(8,128)(2,1)S(1)} %copy-done.40, bf16[256,1536]{1,0:T(8,128)(2,1)} %copy-done.64, bf16[256,1536]{1,0:T(8,128)(2,1)S(1)} %copy-done.63), kind=kOutput, calls=%fused_computation | convolution fusion | flops 3230662656 | bytes 52953088 | tf_op jit(solution)/shard_map/dot_general | solution.py:51
  620.3 2.8 convolution_add_fusion.3
  624.3 3.0 fusion.15
  627.3 6.5 convolution_add_fusion.1
  634.6 15.6 %reduce-scatter.27.cloned.1.call-done = f32[64,2048]{1,0:T(8,128)} async-done(((f32[256,2048]{1,0:T(8,128)}), f32[64,2048]{1,0:T(8,128)}) %reduce-scatter.27.cloned.1.call-update) | async-done | bytes 524304 | tf_op jit(solution)/shard_map/reduce_scatter | solution.py:220
  651.9 41.1 %all-reduce = (f32[2048]{0:T(1024)}, f32[128]{0:T(128)}, f32[128]{0:T(128)}, f32[2048]{0:T(1024)}) all-reduce(f32[2048]{0:T(1024)S(1)} %add.226, f32[128]{0:T(128)S(1)} %add.228, f32[128]{0:T(128)S(1)} %add.229, f32[2048]{0:T(1024)S(1)} %add.231), channel_id=1, replica_groups=mesh['wide'=8,'narrow'=4] {'wide','narrow'}, use_global_device_ids=true, to_apply=%region_38.39 | all-reduce | flops 4352 | bytes 34816 | tf_op jit(solution)/shard_map/psum | solution.py:241
  693.1 1.8 fusion.39
  697.4 56.1 %reduce-scatter.29.cloned.1.call-done = f32[256,1024]{1,0:T(8,128)} async-done(((f32[2048,1024]{1,0:T(8,128)}), f32[256,1024]{1,0:T(8,128)}) %reduce-scatter.29.cloned.1.call-update) | async-done | bytes 1048592 | tf_op jit(solution)/shard_map/reduce_scatter | solution.py:236
  753.5 1.9 slice.176
  755.4 2.0 fusion.102
  757.4 157.0 %reduce-scatter.33.cloned.1.call-done = f32[256,3072]{1,0:T(8,128)} async-done(((f32[2048,3072]{1,0:T(8,128)}), f32[256,3072]{1,0:T(8,128)}) %reduce-scatter.33.cloned.1.call-update) | async-done | bytes 3145744 | tf_op jit(solution)/shard_map/reduce_scatter | solution.py:237
  914.3 3.7 fusion.101
  918.1 51.9 %reduce-scatter.31.cloned.1.call-done = f32[512,256]{1,0:T(8,128)} async-done(((f32[512,2048]{1,0:T(8,128)}), f32[512,256]{1,0:T(8,128)}) %reduce-scatter.31.cloned.1.call-update) | async-done | bytes 524304 | tf_op jit(solution)/shard_map/reduce_scatter | solution.py:238
  970.0 96.3 %reduce-scatter.35.cloned.1.call-done = f32[1536,256]{1,0:T(8,128)} async-done(((f32[1536,2048]{1,0:T(8,128)}), f32[1536,256]{1,0:T(8,128)}) %reduce-scatter.35.cloned.1.call-update) | async-done | bytes 1572880 | tf_op jit(solution)/shard_map/reduce_scatter | solution.py:239
  (370 shorter events, 95.4 us)
Async XLA Ops:
  7.2 93.8 %copy-start = (bf16[512,2048]{1,0:T(8,128)(2,1)S(1)}, bf16[512,2048]{1,0:T(8,128)(2,1)}, u32[]{:S(2)}) copy-start(bf16[512,2048]{1,0:T(8,128)(2,1)} %param.22) | copy-start | bytes 6291460
  7.2 35.1 %all-gather.11.cloned.1.call-start = ((), (), s32[]{:S(2)}) async-start(), calls=%async_computation.12 | async-start | bytes 1310720 | tf_op jit(solution)/shard_map/all_gather | solution.py:121
  9.4 11.9 %copy-start.57 = (bf16[2048,256]{1,0:T(8,128)(2,1)S(1)}, bf16[2048,256]{1,0:T(8,128)(2,1)}, u32[]{:S(2)}) copy-start(bf16[2048,256]{1,0:T(8,128)(2,1)} %param.18) | copy-start | bytes 3145732
  11.5 60.4 %all-gather.15.cloned.1.call-start = ((), (), s32[]{:S(2)}) async-start(), calls=%async_computation.16 | async-start | bytes 1310720 | tf_op jit(solution)/shard_map/all_gather | solution.py:121
  12.2 134.4 %reduce-scatter.13.cloned.1.call-start = ((), (), s32[]{:S(2)}) async-start(), calls=%async_computation.13 | async-start | bytes 2621440 | tf_op jit(solution)/shard_map/reduce_scatter | solution.py:149
  13.0 69.0 %copy-start.98 = (f32[128]{0:T(128)}, f32[128]{0:T(128)S(1)}, u32[]{:S(2)}) copy-start(f32[128]{0:T(128)S(1)} %convert_element_type.147) | copy-start | bytes 1540
  15.6 76.6 %copy-start.102 = (f32[128]{0:T(128)}, f32[128]{0:T(128)S(1)}, u32[]{:S(2)}) copy-start(f32[128]{0:T(128)S(1)} %convert_element_type.145) | copy-start | bytes 1540
  46.0 31.4 %copy-start.20 = (f32[256,1024]{1,0:T(8,128)}, f32[256,1024]{1,0:T(8,128)S(1)}, u32[]{:S(2)}) copy-start(f32[256,1024]{1,0:T(8,128)S(1)} %fusion.110) | copy-start | bytes 3145732
  79.3 6.3 copy-start.8
  81.6 6.1 copy-start.10
  85.7 13.0 %copy-start.27 = (bf16[256,4,64]{2,0,1:T(8,128)(2,1)}, bf16[256,4,64]{2,0,1:T(8,128)(2,1)S(1)}, u32[]{:S(2)}) copy-start(bf16[256,4,64]{2,0,1:T(8,128)(2,1)S(1)} %copy.206) | copy-start | bytes 393220
  85.8 13.0 %copy-start.29 = (bf16[256,4,64]{2,0,1:T(8,128)(2,1)}, bf16[256,4,64]{2,0,1:T(8,128)(2,1)S(1)}, u32[]{:S(2)}) copy-start(bf16[256,4,64]{2,0,1:T(8,128)(2,1)S(1)} %copy.205) | copy-start | bytes 393220
  90.6 380.7 %copy-start.83 = (f32[256,2]{0,1:T(2,128)}, f32[256,2]{0,1:T(2,128)S(1)}, u32[]{:S(2)}) copy-start(f32[256,2]{0,1:T(2,128)S(1)} %add_rsqrt_fusion.3) | copy-start | bytes 6148
  103.1 89.0 %reduce-scatter.17.cloned.1.call-start = ((), (), s32[]{:S(2)}) async-start(), calls=%async_computation.17 | async-start | bytes 2621440 | tf_op jit(solution)/shard_map/reduce_scatter | solution.py:149
  103.2 5.3 copy-start.45
  114.1 110.0 %all-gather.13.cloned.1.call-start = ((), (), s32[]{:S(2)}) async-start(), calls=%async_computation.14 | async-start | bytes 1310720 | tf_op jit(solution)/shard_map/all_gather | solution.py:156
  196.6 56.9 %all-gather.23.cloned.1.call-start = ((), (), s32[]{:S(2)}) async-start(), calls=%async_computation.30 | async-start | bytes 1310720 | tf_op jit(solution)/shard_map/all_gather | solution.py:171
  198.6 116.2 %reduce-scatter.21.cloned.1.call-start = ((), (), s32[]{:S(2)}) async-start(), calls=%async_computation.20 | async-start | bytes 2621440 | tf_op jit(solution)/shard_map/reduce_scatter | solution.py:178
  271.2 73.9 %all-gather.17.cloned.1.call-start = ((), (), s32[]{:S(2)}) async-start(), calls=%async_computation.18 | async-start | bytes 1310720 | tf_op jit(solution)/shard_map/all_gather | solution.py:156
  317.7 56.5 %all-gather.25.cloned.1.call-start = ((), (), s32[]{:S(2)}) async-start(), calls=%async_computation.31 | async-start | bytes 1310720 | tf_op jit(solution)/shard_map/all_gather | solution.py:171
  318.4 117.1 %reduce-scatter.25.cloned.1.call-start = ((), (), s32[]{:S(2)}) async-start(), calls=%async_computation.23 | async-start | bytes 2621440 | tf_op jit(solution)/shard_map/reduce_scatter | solution.py:178
  392.0 72.9 %reduce-scatter.19.cloned.1.call-start = ((), (), s32[]{:S(2)}) async-start(), calls=%async_computation.19 | async-start | bytes 1310720 | tf_op jit(solution)/shard_map/reduce_scatter | solution.py:163
  397.9 96.7 %all-gather.19.cloned.1.call-start = ((), (), s32[]{:S(2)}) async-start(), calls=%async_computation.21 | async-start | bytes 1310720 | tf_op jit(solution)/shard_map/all_gather | solution.py:186
  467.9 55.8 %all-gather.21.cloned.1.call-start = ((), (), s32[]{:S(2)}) async-start(), calls=%async_computation.24 | async-start | bytes 1310720 | tf_op jit(solution)/shard_map/all_gather | solution.py:186
  468.6 166.0 %reduce-scatter.23.cloned.1.call-start = ((), (), s32[]{:S(2)}) async-start(), calls=%async_computation.22 | async-start | bytes 2621440 | tf_op jit(solution)/shard_map/reduce_scatter | solution.py:220
  532.3 5.4 copy-start.22
  532.3 5.4 copy-start.23
  532.4 5.4 copy-start.82
  532.8 8.2 copy-start.37
  536.6 5.6 copy-start.38
  543.1 6.0 copy-start.9
  543.1 6.0 copy-start.11
  547.6 5.9 copy-start.76
  549.0 5.2 copy-start.21
  549.1 5.8 copy-start.34
  549.1 6.5 copy-start.86
  556.5 5.9 copy-start.26
  561.3 7.1 copy-start.19
  561.3 7.1 copy-start.59
  561.3 8.6 copy-start.36
  561.3 88.9 %reduce-scatter.27.cloned.1.call-start = ((), (), s32[]{:S(2)}) async-start(), calls=%async_computation.25 | async-start | bytes 2621440 | tf_op jit(solution)/shard_map/reduce_scatter | solution.py:220
  575.7 117.3 %reduce-scatter.15.cloned.1.call-start = ((), (), s32[]{:S(2)}) async-start(), calls=%async_computation.15 | async-start | bytes 1310720 | tf_op jit(solution)/shard_map/reduce_scatter | solution.py:163
  575.8 5.8 copy-start.43
  575.8 5.8 copy-start.69
  581.5 172.0 %reduce-scatter.29.cloned.1.call-start = ((), (), s32[]{:S(2)}) async-start(), calls=%async_computation.26 | async-start | bytes 9437184 | tf_op jit(solution)/shard_map/reduce_scatter | solution.py:236
  588.5 12.8 %copy-start.40 = (bf16[256,2048]{1,0:T(8,128)(2,1)S(1)}, bf16[256,2048]{1,0:T(8,128)(2,1)}, u32[]{:S(2)}) copy-start(bf16[256,2048]{1,0:T(8,128)(2,1)} %all-gather.17.cloned.1.call-done) | copy-start | bytes 3145732
  588.5 12.8 %copy-start.63 = (bf16[256,1536]{1,0:T(8,128)(2,1)S(1)}, bf16[256,1536]{1,0:T(8,128)(2,1)}, u32[]{:S(2)}) copy-start(bf16[256,1536]{1,0:T(8,128)(2,1)} %copy-done.62) | copy-start | bytes 2359300
  588.5 325.8 %reduce-scatter.33.cloned.1.call-start = ((), (), s32[]{:S(2)}) async-start(), calls=%async_computation.28 | async-start | bytes 28311552 | tf_op jit(solution)/shard_map/reduce_scatter | solution.py:237
  618.3 351.7 %reduce-scatter.31.cloned.1.call-start = ((), (), s32[]{:S(2)}) async-start(), calls=%async_computation.27 | async-start | bytes 4718592 | tf_op jit(solution)/shard_map/reduce_scatter | solution.py:238
  623.1 443.2 %reduce-scatter.35.cloned.1.call-start = ((), (), s32[]{:S(2)}) async-start(), calls=%async_computation.29 | async-start | bytes 14155776 | tf_op jit(solution)/shard_map/reduce_scatter | solution.py:239
  633.8 16.4 %copy-start.4 = (bf16[2,1,64,2048]{3,2,1,0:T(8,128)(2,1)S(1)}, bf16[2,1,64,2048]{3,2,1,0:T(8,128)(2,1)}, u32[]{:S(2)}) copy-start(bf16[2,1,64,2048]{3,2,1,0:T(8,128)(2,1)} %param.14) | copy-start | bytes 1572868
  633.8 16.4 %copy-start.79 = (f32[2048]{0:T(1024)S(1)}, f32[2048]{0:T(1024)}, u32[]{:S(2)}) copy-start(f32[2048]{0:T(1024)} %copy-done.78) | copy-start | bytes 24580
  633.8 16.4 %copy-start.91 = (f32[64]{0:T(128)S(1)}, f32[64]{0:T(128)}, u32[]{:S(2)}) copy-start(f32[64]{0:T(128)} %copy-done.90) | copy-start | bytes 772
  633.8 16.4 %copy-start.93 = (f32[64]{0:T(128)S(1)}, f32[64]{0:T(128)}, u32[]{:S(2)}) copy-start(f32[64]{0:T(128)} %copy-done.92) | copy-start | bytes 772
  633.9 59.2 %copy-start.7 = (f32[64,2048]{1,0:T(8,128)S(1)}, f32[64,2048]{1,0:T(8,128)}, u32[]{:S(2)}) copy-start(f32[64,2048]{1,0:T(8,128)} %copy-done.6) | copy-start | bytes 1572868
  633.9 59.2 %copy-start.12 = (bf16[2,1,64,2048]{3,2,1,0:T(8,128)(2,1)S(1)}, bf16[2,1,64,2048]{3,2,1,0:T(8,128)(2,1)}, u32[]{:S(2)}) copy-start(bf16[2,1,64,2048]{3,2,1,0:T(8,128)(2,1)} %param.27) | copy-start | bytes 1572868
  633.9 59.2 %copy-start.15 = (f32[64,2048]{1,0:T(8,128)S(1)}, f32[64,2048]{1,0:T(8,128)}, u32[]{:S(2)}) copy-start(f32[64,2048]{1,0:T(8,128)} %reduce-scatter.21.cloned.1.call-done) | copy-start | bytes 1572868
  633.9 59.2 %copy-start.97 = (f32[64]{0:T(128)S(1)}, f32[64]{0:T(128)}, u32[]{:S(2)}) copy-start(f32[64]{0:T(128)} %copy-done.96) | copy-start | bytes 772
  633.9 59.2 %copy-start.101 = (f32[64]{0:T(128)S(1)}, f32[64]{0:T(128)}, u32[]{:S(2)}) copy-start(f32[64]{0:T(128)} %broadcast_multiply_fusion.7) | copy-start | bytes 772
  651.8 44.1 %copy-start.5 = (f32[64,2048]{1,0:T(8,128)S(1)}, f32[64,2048]{1,0:T(8,128)}, u32[]{:S(2)}) copy-start(f32[64,2048]{1,0:T(8,128)} %get-tuple-element.154) | copy-start | bytes 1572868
  651.9 44.1 %copy-start.14 = (f32[64,2048]{1,0:T(8,128)S(1)}, f32[64,2048]{1,0:T(8,128)}, u32[]{:S(2)}) copy-start(f32[64,2048]{1,0:T(8,128)} %reduce-scatter.25.cloned.1.call-done) | copy-start | bytes 1572868
  651.9 44.1 %copy-start.95 = (f32[64]{0:T(128)S(1)}, f32[64]{0:T(128)}, u32[]{:S(2)}) copy-start(f32[64]{0:T(128)} %add_rsqrt_fusion.4) | copy-start | bytes 772
  651.9 44.1 %copy-start.100 = (f32[64]{0:T(128)S(1)}, f32[64]{0:T(128)}, u32[]{:S(2)}) copy-start(f32[64]{0:T(128)} %broadcast_multiply_fusion.5) | copy-start | bytes 772
  755.4 311.0 %copy-start.1 = (bf16[512,2048]{1,0:T(8,128)(2,1)S(1)}, bf16[512,2048]{1,0:T(8,128)(2,1)}, u32[]{:S(2)}) copy-start(bf16[512,2048]{1,0:T(8,128)(2,1)} %param.22) | copy-start | bytes 6291460
  (60 other events, 140.3 us)
Sparse Core Ops, SparseCore 0:
  11.6 30.6 all-gather.10
  44.4 27.4 all-gather.14
  103.2 43.3 reduce-scatter.12
  148.8 43.1 reduce-scatter.16
  196.8 27.2 all-gather.12
  226.0 27.4 all-gather.22
  271.4 43.3 reduce-scatter.20
  317.8 27.2 all-gather.16
  346.8 27.4 all-gather.24
  392.1 43.3 reduce-scatter.24
  438.4 26.4 reduce-scatter.18
  468.0 26.5 all-gather.18
  496.3 27.4 all-gather.20
  561.4 43.3 reduce-scatter.22
  607.0 43.1 reduce-scatter.26
  653.0 27.1 reduce-scatter.14
  683.5 69.9 reduce-scatter.28
  757.4 156.8 reduce-scatter.32
  918.6 51.3 reduce-scatter.30
  973.9 92.3 reduce-scatter.34
where the time goes:
time: 1080 us; the launch traced here: 1070 us
  waiting for transfers between devices  723 us (67%)
  matrix products  156 us (14%)
  local copies, waits for them, and re-layouts  73.9 us (7%)
  other arithmetic  61.7 us (6%)
  blocking collectives  41.1 us (4%)
  between operations  16.1 us (1%)
    reduce_scatter x1, waiting for transfers between devices, local(): lax.psum_scatter(totals[1], 'wide', scatter_dimension=0, tiled=True)  157 us
    reduce_scatter x1, waiting for transfers between devices, local(): lax.psum_scatter(totals[3], 'wide', scatter_dimension=1, tiled=True)  96.3 us
    reduce_scatter x2, waiting for transfers between devices, local(): lax.psum_scatter(row_back_product(d_both, w_both), 'narrow', scatter_dime...  78.7 us
    reduce_scatter x2, waiting for transfers between devices, local(): lax.psum_scatter(row_product(attn_mix, w_out), 'narrow', scatter_dimensio...  77.3 us
    reduce_scatter x1, waiting for transfers between devices, local(): lax.psum_scatter(totals[0], 'wide', scatter_dimension=0, tiled=True)  56.1 us
    reduce_scatter x1, waiting for transfers between devices, local(): lax.psum_scatter(totals[2], 'wide', scatter_dimension=1, tiled=True)  51.9 us
    dot_general x8, matrix products, contract_rows(): lax.dot_general(left_side, right_side, (((0,), (0,)), ((), ())), preferre...  48.3 us
    dot_general x8, matrix products, contract_cols(): lax.dot_general(left_side, right_side, (((1,), (1,)), ((), ())), preferre...  48.1 us
  transfers between devices with their start and end apart: 20, of which 18 were waited for; matrix products, arithmetic and copies ran while one was open for 16% of the time, Pallas kernels for 0%

commit v1 on v0

v1 whole, which is shorter than its diff:
```python
import functools

import jax
import jax.numpy as jnp
from jax import lax
from jax.experimental import pallas as pl
from jax.experimental.pallas import tpu as pltpu
from jax.sharding import PartitionSpec as P

MESH = pl.DeviceIdType.MESH
F32 = jnp.float32
BF16 = jnp.bfloat16
norm_eps = 1e-06
masked_score = -1e30


def both(*conds):
    out = conds[0]
    for cond in conds[1:]:
        out = jnp.logical_and(out, cond)
    return out


def remote(src, dst, ssem, rsem, z):
    return pltpu.make_async_remote_copy(
        src_ref=src, dst_ref=dst, send_sem=ssem, recv_sem=rsem,
        device_id=(lax.axis_index("wide"), z), device_id_type=MESH,
    )


def line_barrier(n):
    z = lax.axis_index("narrow")
    bar = pltpu.get_barrier_semaphore()
    for step in range(1, n):
        pl.semaphore_signal(
            bar, inc=1, device_id=(lax.axis_index("wide"), lax.rem(z + step, n)), device_id_type=MESH
        )
    pl.semaphore_wait(bar, n - 1)


class Gather:
    def __init__(self, n, parts, rows, full, ssem, rsem):
        self.n, self.parts, self.rows, self.full, self.ssem, self.rsem = n, parts, rows, full, ssem, rsem
        self.z = lax.axis_index("narrow")

    def copy(self, way, hop, part, chunk):
        where = self.full.at[chunk, pl.ds(part * self.rows, self.rows)]
        z_to = self.z + 1 if way == 0 else self.z - 1
        return remote(where, where, self.ssem.at[way, hop, part], self.rsem.at[way, hop, part], z_to)

    def chunk(self, way, hop):
        return self.z - hop if way == 0 else self.z + hop

    def has(self, way, hop):
        return self.z >= hop if way == 0 else self.z + hop <= self.n - 1

    def can_send(self, way, hop):
        edge = self.z < self.n - 1 if way == 0 else self.z > 0
        return both(self.has(way, hop), edge)

    def send(self, hop, part):
        for way in (0, 1):
            if hop > 0:
                @pl.when(self.has(way, hop))
                def _():
                    self.copy(way, hop - 1, part, self.chunk(way, hop)).wait_recv()

            if hop < self.n - 1:
                @pl.when(self.can_send(way, hop))
                def _():
                    self.copy(way, hop, part, self.chunk(way, hop)).start()

    def drain(self):
        for way in (0, 1):
            for hop in range(self.n - 1):
                for part in range(self.parts):
                    @pl.when(self.can_send(way, hop))
                    def _():
                        self.copy(way, hop, part, self.chunk(way, hop)).wait_send()


class Scatter:
    def __init__(self, n, parts, partial, sbuf, rbuf, ssem, rsem):
        self.n, self.parts, self.partial = n, parts, partial
        self.sbuf, self.rbuf, self.ssem, self.rsem = sbuf, rbuf, ssem, rsem
        self.z = lax.axis_index("narrow")

    def copy(self, way, j, part):
        z_to = self.z + 1 if way == 0 else self.z - 1
        return remote(
            self.sbuf.at[way, j, part], self.rbuf.at[way, j, part],
            self.ssem.at[way, j, part], self.rsem.at[way, j, part], z_to,
        )

    def dest(self, way, j):
        return self.n - 1 - j if way == 0 else j

    def sends(self, way, j):
        return self.dest(way, j) > self.z if way == 0 else self.dest(way, j) < self.z

    def relays(self, way, j):
        inner = self.z > 0 if way == 0 else self.z < self.n - 1
        return both(self.sends(way, j), inner)

    def starts(self, way, j):
        outer = self.z == 0 if way == 0 else self.z == self.n - 1
        return both(self.sends(way, j), outer)

    def step(self, j, part):
        for way in (0, 1):
            @pl.when(self.starts(way, j))
            def _():
                self.sbuf[way, j, part] = self.partial(self.dest(way, j), part).astype(BF16)
                self.copy(way, j, part).start()

            @pl.when(self.relays(way, j))
            def _():
                self.copy(way, j, part).wait_recv()
                value = self.partial(self.dest(way, j), part) + self.rbuf[way, j, part].astype(F32)
                self.sbuf[way, j, part] = value.astype(BF16)
                self.copy(way, j, part).start()

    def final(self, part, acc_ref):
        acc_ref[part] = self.partial(self.z, part)

        @pl.when(self.z > 0)
        def _():
            j = self.n - 1 - self.z
            self.copy(0, j, part).wait_recv()
            acc_ref[part] += self.rbuf[0, j, part].astype(F32)

        @pl.when(self.z < self.n - 1)
        def _():
            j = self.z
            self.copy(1, j, part).wait_recv()
            acc_ref[part] += self.rbuf[1, j, part].astype(F32)

    def drain(self):
        for way in (0, 1):
            for j in range(self.n - 1):
                for part in range(self.parts):
                    @pl.when(self.sends(way, j))
                    def _():
                        self.copy(way, j, part).wait_send()


def rms_scale(values):
    return lax.rsqrt(jnp.mean(values * values, axis=-1, keepdims=True) + norm_eps)


def rms_back(grad_in, hat, scale_rows):
    return scale_rows * (grad_in - hat * jnp.mean(grad_in * hat, axis=-1, keepdims=True))


def gather_kernel(n, parts, rows, x_ref, gain_ref, cot_ref, normed_ref, cot_full, ssem, rsem, ssem2, rsem2):
    z = lax.axis_index("narrow")
    for part in range(parts):
        x = x_ref[part].astype(F32)
        hat = x * rms_scale(x)
        normed_ref[z, part * rows:(part + 1) * rows] = (hat * gain_ref[...].astype(F32)).astype(BF16)
        cot_full[z, part * rows:(part + 1) * rows] = cot_ref[part]
    line_barrier(n)
    one = Gather(n, parts, rows, normed_ref, ssem, rsem)
    two = Gather(n, parts, rows, cot_full, ssem2, rsem2)
    for g in (one, two):
        for hop in range(n):
            for part in range(parts):
                g.send(hop, part)
    one.drain()
    two.drain()


def mid_kernel(n, parts, rows, partial_ref, x_ref, gain_ref, middle_ref, full_ref, sbuf, rbuf, acc, ss, rs, gs, gr):
    z = lax.axis_index("narrow")
    line_barrier(n)
    scat = Scatter(n, parts, lambda d, p: partial_ref[d, p * rows:(p + 1) * rows], sbuf, rbuf, ss, rs)
    gath = Gather(n, parts, rows, full_ref, gs, gr)
    for part in range(parts + 1):
        for j in range(n - 1):
            if part < parts:
                scat.step(j, part)
            if part > 0:
                gath.send(j + 1, part - 1)
        if part < parts:
            scat.final(part, acc)
            middle = x_ref[part].astype(F32) + acc[part]
            middle_ref[part] = middle
            hat = middle * rms_scale(middle)
            full_ref[z, part * rows:(part + 1) * rows] = (hat * gain_ref[...].astype(F32)).astype(BF16)
            gath.send(0, part)
    scat.drain()
    gath.drain()


def back_kernel(n, parts, rows, partial_ref, mlp_ref, middle_ref, cot_ref, gain_ref, dmid_ref, full_ref, gaing_ref, out_ref,
                sbuf, rbuf, sbuf2, rbuf2, acc, ss, rs, gs, gr, ss2, rs2):
    z = lax.axis_index("narrow")
    line_barrier(n)
    scat = Scatter(n, parts, lambda d, p: partial_ref[d, p * rows:(p + 1) * rows], sbuf, rbuf, ss, rs)
    scat2 = Scatter(n, parts, lambda d, p: mlp_ref[d, p * rows:(p + 1) * rows], sbuf2, rbuf2, ss2, rs2)
    gath = Gather(n, parts, rows, full_ref, gs, gr)
    for part in range(parts + 1):
        for j in range(n - 1):
            if part < parts:
                scat.step(j, part)
            if part > 0:
                gath.send(j + 1, part - 1)
                scat2.step(j, part - 1)
        if part < parts:
            scat.final(part, acc)
            dn2 = acc[part]
            middle = middle_ref[part]
            scale = rms_scale(middle)
            hat = middle * scale
            part_sum = jnp.sum(dn2 * hat, axis=0, keepdims=True)
            if part == 0:
                gaing_ref[...] = part_sum
            else:
                gaing_ref[...] += part_sum
            dmid = cot_ref[part].astype(F32) + rms_back(dn2 * gain_ref[...].astype(F32), hat, scale)
            dmid_ref[part] = dmid
            full_ref[z, part * rows:(part + 1) * rows] = dmid.astype(BF16)
            gath.send(0, part)
    for part in range(parts):
        scat2.final(part, acc)
        out_ref[part] = middle_ref[part] + acc[part]
    scat.drain()
    scat2.drain()
    gath.drain()


def last_kernel(n, parts, rows, partial_ref, dmid_ref, x_ref, gain_ref, out_ref, gaing_ref, sbuf, rbuf, acc, ss, rs):
    line_barrier(n)
    scat = Scatter(n, parts, lambda d, p: partial_ref[d, p * rows:(p + 1) * rows], sbuf, rbuf, ss, rs)
    for part in range(parts):
        for j in range(n - 1):
            scat.step(j, part)
    for part in range(parts):
        scat.final(part, acc)
        dn = acc[part]
        x = x_ref[part].astype(F32)
        scale = rms_scale(x)
        hat = x * scale
        part_sum = jnp.sum(dn * hat, axis=0, keepdims=True)
        if part == 0:
            gaing_ref[...] = part_sum
        else:
            gaing_ref[...] += part_sum
        out_ref[part] = dmid_ref[part] + rms_back(dn * gain_ref[...].astype(F32), hat, scale)
    scat.drain()


def comm_call(body, name, cid, outs, scratch, args):
    vm = pl.BlockSpec(memory_space=pltpu.VMEM)
    return pl.pallas_call(
        body, name=name, out_shape=outs, in_specs=[vm] * len(args), out_specs=[vm] * len(outs), scratch_shapes=scratch,
        compiler_params=pltpu.CompilerParams(collective_id=cid, has_side_effects=True, vmem_limit_bytes=48 << 20),
    )(*args)


def doc_layout(lengths, seq_len):
    doc_ends = jnp.cumsum(lengths)
    starts = doc_ends - lengths
    places = lax.iota(jnp.int32, seq_len)
    segment = jnp.sum((places[:, None] >= doc_ends[None, :]).astype(jnp.int32), axis=1)
    member = segment[:, None] == lax.iota(jnp.int32, lengths.shape[0])[None, :]
    doc_first = jnp.sum(jnp.where(member, starts[None, :], 0), axis=1)
    allowed = (segment[:, None] == segment[None, :]) & (places[None, :] <= places[:, None])
    return (places - doc_first, allowed)


def rope_tables(inside, head_dim):
    half_dim = head_dim // 2
    frequency = jnp.power(1000000.0, -2.0 * lax.iota(jnp.float32, half_dim) / head_dim)
    angles = inside.astype(jnp.float32)[..., None] * frequency
    return (jnp.cos(angles), jnp.sin(angles))


def rotate(values, cos_table, sine_table):
    half = values.shape[-1] // 2
    first, second = values[..., :half], values[..., half:]
    cos, sin = cos_table[..., None, :], sine_table[..., None, :]
    return jnp.concatenate([first * cos - second * sin, second * cos + first * sin], axis=-1)


def dot(a, b, ca, cb):
    return lax.dot_general(a, b, (((ca,), (cb,)), ((), ())), preferred_element_type=F32)


def local(layer_input, document_lengths, attn_gain, w_query, w_key, w_value, query_gain, key_gain, w_out, mlp_gain,
          w_gate, w_up, w_down, output_cotangent):
    n = lax.axis_size("narrow")
    C, _, S, D = layer_input.shape
    T = n * C * S
    R = n * S
    HD = query_gain.shape[0]
    QC, KC = w_query.shape[1], w_key.shape[1]
    QH, KH = QC // HD, KC // HD
    G = QH // KH
    FC = w_gate.shape[1]
    sscale = HD ** (-0.5)
    w_qkv = jnp.concatenate([w_query, w_key, w_value], axis=1)
    w_both = jnp.concatenate([w_gate, w_up], axis=1)
    qg, kg = query_gain.astype(F32), key_gain.astype(F32)
    x_own = layer_input[:, 0]
    cot_own = output_cotangent[:, 0]
    sds = jax.ShapeDtypeStruct
    dma = pltpu.SemaphoreType.DMA
    gsem = lambda: dma((2, n - 1, C))
    rbufs = lambda: pltpu.VMEM((2, n - 1, C, S, D), BF16)

    normed_full, cot_full = comm_call(
        functools.partial(gather_kernel, n, C, S), "gather", 0,
        [sds((n, C * S, D), BF16)] * 2, [gsem(), gsem(), gsem(), gsem()],
        (x_own, attn_gain[None], cot_own))

    def to_rows(v):
        return v.reshape(n, C, S, -1).transpose(1, 0, 2, 3).reshape(C, R, -1)

    def from_rows(v):
        return v.reshape(C, n, S, -1).transpose(1, 0, 2, 3).reshape(T, -1)

    inside, allowed = jax.vmap(lambda l: doc_layout(l, R))(document_lengths[:, 0])
    cos, sin = rope_tables(inside, HD)
    proj = to_rows(dot(normed_full.reshape(T, D), w_qkv, 1, 0))
    q_raw = proj[..., :QC].reshape(C, R, QH, HD)
    k_raw = proj[..., QC:QC + KC].reshape(C, R, KH, HD)
    v_rows = proj[..., QC + KC:].astype(BF16).reshape(C, R, KH, HD)
    q_scale = rms_scale(q_raw)
    q_hat = q_raw * q_scale
    q_rot = rotate(q_hat * qg, cos, sin).astype(BF16)
    k_scale = rms_scale(k_raw)
    k_hat = k_raw * k_scale
    k_rot = rotate(k_hat * kg, cos, sin).astype(BF16)
    grouped = q_rot.reshape(C, R, KH, G, HD)
    es = functools.partial(jnp.einsum, preferred_element_type=F32)
    scores = jnp.where(allowed[:, None, None], es("btkgd,bukd->bkgtu", grouped, k_rot) * sscale, masked_score)
    top = jnp.max(scores, axis=-1, keepdims=True)
    ex = jnp.exp(scores - top)
    prob = ex / jnp.sum(ex, axis=-1, keepdims=True)
    prob_low = prob.astype(BF16)
    mix = from_rows(es("bkgtu,bukd->btkgd", prob_low, v_rows).reshape(C, R, QC).astype(BF16))
    attn_part = dot(mix, w_out, 1, 0).reshape(n, C * S, D)

    middle, n2_full = comm_call(
        functools.partial(mid_kernel, n, C, S), "middle", 1,
        [sds((C, S, D), F32), sds((n, C * S, D), BF16)],
        [rbufs(), rbufs(), pltpu.VMEM((C, S, D), F32), gsem(), gsem(), gsem(), gsem()],
        (attn_part, x_own, mlp_gain[None]))

    n2 = n2_full.reshape(T, D)
    cot = cot_full.reshape(T, D)
    gate_up = dot(n2, w_both, 1, 0)
    gate_pre, up_proj = gate_up[:, :FC], gate_up[:, FC:]
    sig = jax.nn.sigmoid(gate_pre)
    silu = gate_pre * sig
    activated = (silu * up_proj).astype(BF16)
    mlp_part = dot(activated, w_down, 1, 0).reshape(n, C * S, D)
    d_act = dot(cot, w_down, 1, 1)
    d_gate = d_act * up_proj * sig * (1.0 + gate_pre * (1.0 - sig))
    d_both = jnp.concatenate([d_gate, d_act * silu], axis=1).astype(BF16)
    dn2_part = dot(d_both, w_both, 1, 1).reshape(n, C * S, D)
    d_middle, db_full, mlp_gain_part, out_own = comm_call(
        functools.partial(back_kernel, n, C, S), "back", 2,
        [sds((C, S, D), F32), sds((n, C * S, D), BF16), sds((1, D), F32), sds((C, S, D), F32)],
        [rbufs(), rbufs(), rbufs(), rbufs(), pltpu.VMEM((C, S, D), F32)] + [gsem() for _ in range(6)],
        (dn2_part, mlp_part, middle, cot_own, mlp_gain[None]))
    scatter = lambda g, dim: lax.psum_scatter(g.astype(BF16), "wide", scatter_dimension=dim, tiled=True).astype(F32)
    down_share = scatter(dot(activated, cot, 0, 0), 1)
    both_share = scatter(dot(n2, d_both, 0, 0), 0)
    db = db_full.reshape(T, D)
    out_share = scatter(dot(mix, db, 0, 0), 1)
    d_mix = to_rows(dot(db, w_out, 1, 1).astype(BF16)).reshape(C, R, KH, G, HD)
    d_prob = es("btkgd,bukd->bkgtu", d_mix, v_rows)
    d_value = es("bkgtu,btkgd->bukd", prob_low, d_mix)
    d_score = (prob * (d_prob - jnp.sum(prob * d_prob, axis=-1, keepdims=True))).astype(BF16)
    d_query = es("bkgtu,bukd->btkgd", d_score, k_rot).reshape(C, R, QH, HD) * sscale
    d_key = es("bkgtu,btkgd->bukd", d_score, grouped) * sscale
    d_qn = rotate(d_query, cos, -sin)
    d_kn = rotate(d_key, cos, -sin)
    qg_part = jnp.sum(d_qn * q_hat, axis=(0, 1, 2))
    kg_part = jnp.sum(d_kn * k_hat, axis=(0, 1, 2))
    d_qr = rms_back(d_qn * qg, q_hat, q_scale)
    d_kr = rms_back(d_kn * kg, k_hat, k_scale)
    d_proj = from_rows(jnp.concatenate(
        [d_qr.reshape(C, R, QC), d_kr.reshape(C, R, KC), d_value.reshape(C, R, KC)], axis=-1).astype(BF16))
    dn_part = dot(d_proj, w_qkv, 1, 1).reshape(n, C * S, D)
    qkv_share = scatter(dot(normed_full.reshape(T, D), d_proj, 0, 0), 0)
    in_own, attn_gain_part = comm_call(
        functools.partial(last_kernel, n, C, S), "last", 3,
        [sds((C, S, D), F32), sds((1, D), F32)],
        [rbufs(), rbufs(), pltpu.VMEM((C, S, D), F32), gsem(), gsem()],
        (dn_part, d_middle, x_own, attn_gain[None]))
    small = lax.psum((attn_gain_part[0], qg_part, kg_part, mlp_gain_part[0]), ("wide", "narrow"))
    return (
        out_own[:, None], in_own[:, None], small[0],
        qkv_share[:, :QC], qkv_share[:, QC:QC + KC], qkv_share[:, QC + KC:],
        small[1], small[2], out_share, small[3], both_share[:, :FC], both_share[:, FC:], down_share,
    )


def solution(mesh):
    in_specs = (
        P(None, "wide", "narrow", None), P(None, "wide", None), P(), P(None, "narrow"), P(None, "narrow"), P(None, "narrow"),
        P(), P(), P("narrow", None), P(), P(None, "narrow"), P(None, "narrow"), P("narrow", None),
        P(None, "wide", "narrow", None),
    )
    out_specs = (
        P(None, "wide", "narrow", None), P(None, "wide", "narrow", None), P(), P("wide", "narrow"), P("wide", "narrow"),
        P("wide", "narrow"), P(), P(), P("narrow", "wide"), P(), P("wide", "narrow"), P("wide", "narrow"), P("narrow", "wide"),
    )
    return jax.shard_map(local, mesh=mesh, in_specs=in_specs, out_specs=out_specs, check_vma=False)
```

time: 1080 us -> 682 us (0.63)
  waiting for transfers between devices: 723 us -> 95.5 us
  Pallas kernels: 0 us -> 315 us
  matrix products: 156 us -> 98.7 us
  other arithmetic: 61.7 us -> 27.6 us
    reduce_scatter x12 -> x4, waiting for transfers between devices: 560 us -> 95.5 us  [local(): lax.psum_scatter(g.astype(BF16), 'wide', scatter_dimension=dim, tiled=True)]
    pallas_call x0 -> x4, Pallas kernels: none -> 315 us  [comm_call(): pl.pallas_call(body, name=name, out_shape=outs, in_specs=[vm] * len(args)...]
    all_gather x8 -> x0, waiting for transfers between devices: 161 us -> none  [the longest x2 42.9 us: local(): normed_full = lax.all_gather(normed, 'narrow', axis=0, tiled=True)]
    dot_general x36 -> x17, matrix products: 156 us -> 94.9 us  [the longest x12 83.2 us: dot(): lax.dot_general(a, b, (((ca,), (cb,)), ((), ())), preferred_element_type=...]
    reshape x10 -> x2, local copies, waits for them, and re-layouts: 14 us -> 2.08 us  [the longest x1 2.04 us: local(): k_raw = proj[..., QC:QC + KC].reshape(C, R, KH, HD)]
    reduce_sum x15 -> x5, other arithmetic: 16.9 us -> 5.14 us  [the longest x2 2.33 us: local(): qg_part = jnp.sum(d_qn * q_hat, axis=(0, 1, 2))]
    unnamed x217 -> x109, local copies, waits for them, and re-layouts: 27.1 us -> 18.9 us
  transfers between devices with their start and end apart: 20 -> 4, of which waited for: 18 -> 2; matrix products, arithmetic and copies ran while one was open for 16% -> 13% of each run, Pallas kernels for 0% -> 6%
where the time goes in v1:
time: 682 us; the launch traced here: 669 us
  Pallas kernels  315 us (46%)
  matrix products  98.7 us (14%)
  waiting for transfers between devices  95.5 us (14%)
  local copies, waits for them, and re-layouts  76.1 us (11%)
  blocking collectives  40.2 us (6%)
  other arithmetic  27.6 us (4%)
  between operations  14.6 us (2%)
    pallas_call x4, Pallas kernels, comm_call(): pl.pallas_call(body, name=name, out_shape=outs, in_specs=[vm] * len(args)...  315 us
    reduce_scatter x4, waiting for transfers between devices, local(): lax.psum_scatter(g.astype(BF16), 'wide', scatter_dimension=dim, tiled=True)  95.5 us
    dot_general x12, matrix products, dot(): lax.dot_general(a, b, (((ca,), (cb,)), ((), ())), preferred_element_type=...  83.2 us
    psum x1, blocking collectives, local(): lax.psum((attn_gain_part[0], qg_part, kg_part, mlp_gain_part[0]), ('wide'...  40.2 us
    unnamed x109, local copies, waits for them, and re-layouts  18.9 us
  transfers between devices with their start and end apart: 4, of which 2 were waited for; matrix products, arithmetic and copies ran while one was open for 13% of the time, Pallas kernels for 6%

profile of v1, /device:TPU:0, one launch (start us, length us, event | category | flops | bytes accessed | tf_op | source)
XLA Modules:
  0.0 668.5 jit_solution(5978995406925289551)
XLA Ops:
  8.1 2.1 constant_dynamic-update-slice_fusion.2
  10.5 1.9 copy-done.26
  12.5 74.2 %gather.1 = (bf16[4,128,2048]{2,1,0:T(8,128)(2,1)S(1)}, bf16[4,128,2048]{2,1,0:T(8,128)(2,1)S(1)}) custom-call(bf16[2,64,2048]{2,1,0:T(8,128)(2,1)S(1)} %bitcast.160, bf16[1,2048]{1,0:T(2,128)(2,1)S(1)} %broadcast_in_dim.30.gain_ref, bf16[2,64,2048]{2,1,0:T(8,128)(2,1)S(1)} %bitcast.163), custom_call_target="tpu_custom_call" | custom-call | tf_op jit(solution)/shard_map/gather/pallas_call | solution.py:255
  86.7 6.0 fusion.13
  95.6 5.9 constant_dynamic-update-slice_fusion.4
  102.6 2.0 copy.172
  104.7 1.1 multiply_reduce_fusion.5
  105.8 2.0 copy.173
  109.8 1.2 fusion.28
  112.0 2.5 copy.177
  115.2 1.3 multiply_reduce_fusion.2
  116.6 1.4 multiply_multiply_fusion
  118.9 2.0 copy.179
  120.8 2.0 copy.178
  122.8 1.3 multiply_multiply_fusion.1
  124.1 2.0 subtract_convert_fusion.1
  126.0 3.8 fusion.36
  129.9 2.8 fusion.16
  132.7 2.0 copy.181
  134.7 2.0 convert_element_type.76
  136.7 1.1 copy.182
  137.8 5.8 constant_dynamic-update-slice_fusion.3
  143.7 3.3 fusion.9.partial_ref
  147.0 84.4 %middle.1 = (f32[2,64,2048]{2,1,0:T(8,128)S(1)}, bf16[4,128,2048]{2,1,0:T(8,128)(2,1)S(1)}) custom-call(f32[4,128,2048]{2,1,0:T(8,128)} %fusion.9.partial_ref, bf16[2,64,2048]{2,1,0:T(8,128)(2,1)S(1)} %bitcast.161, bf16[1,2048]{1,0:T(2,128)(2,1)S(1)} %broadcast_in_dim.40.gain_ref), custom_call_target="tpu_custom_call" | custom-call | tf_op jit(solution)/shard_map/middle/pallas_call | solution.py:255
  231.4 12.1 %fusion.37 = f32[512,3072]{1,0:T(8,128)} fusion(bf16[512,2048]{1,0:T(8,128)(2,1)S(1)} %bitcast.173, bf16[2048,3072]{1,0:T(8,128)(2,1)} %constant_dynamic-update-slice_fusion.3), kind=kOutput, calls=%fused_computation.102 | convolution fusion | flops 6442450944 | bytes 20971520 | tf_op jit(solution)/shard_map/dot_general | solution.py:287
  243.6 6.7 %multiply_convert_fusion.2 = (bf16[512,1536]{1,0:T(8,128)(2,1)S(1)}, bf16[512,1536]{1,0:T(8,128)(2,1)S(1)}, bf16[512,1536]{1,0:T(8,128)(2,1)S(1)}) fusion(f32[512,3072]{1,0:T(8,128)} %fusion.37, bf16[512,2048]{1,0:T(8,128)(2,1)S(1)} %bitcast.170, bf16[1536,2048]{1,0:T(8,128)(2,1)S(1)} %bitcast.206), kind=kOutput, calls=%fused_computation.11 | convolution fusion | flops 3233021952 | bytes 19398656 | tf_op jit(solution)/shard_map/dot_general | solution.py:287
  250.3 5.0 fusion.38
  255.3 11.1 %fusion.11 = f32[512,2048]{1,0:T(8,128)} fusion(bf16[2048,3072]{1,0:T(8,128)(2,1)} %constant_dynamic-update-slice_fusion.3, bf16[512,1536]{1,0:T(8,128)(2,1)S(1)} %get-tuple-element.105, bf16[512,1536]{1,0:T(8,128)(2,1)S(1)} %get-tuple-element.104), kind=kOutput, calls=%fused_computation.24 | convolution fusion | flops 6448742400 | bytes 19922944 | tf_op jit(solution)/shard_map/dot_general | solution.py:287
  266.4 115.1 %back.1 = (f32[2,64,2048]{2,1,0:T(8,128)S(1)}, bf16[4,128,2048]{2,1,0:T(8,128)(2,1)}, f32[1,2048]{1,0:T(1,128)S(1)}, f32[2,64,2048]{2,1,0:T(8,128)S(1)}) custom-call(f32[4,128,2048]{2,1,0:T(8,128)} %bitcast.182, f32[4,128,2048]{2,1,0:T(8,128)} %bitcast.181, f32[2,64,2048]{2,1,0:T(8,128)S(1)} %get-tuple-element.26.middle_ref, ...), custom_call_target="tpu_custom_call" | custom-call | tf_op jit(solution)/shard_map/back/pallas_call | solution.py:255
  383.5 4.2 convolution_convert_fusion.3
  387.7 2.9 convolution_convert_fusion.4
  391.6 1.3 copy.202
  392.9 3.1 fusion.20
  396.0 2.4 fusion.6
  398.5 1.1 copy.204
  400.5 2.7 fusion.8
  404.2 1.3 fusion.18
  405.5 1.8 copy.196
  407.3 1.5 multiply_subtract_fusion
  408.8 1.1 multiply_reduce_fusion.4
  410.0 1.2 copy.197
  414.1 1.6 mul.395
  415.7 1.2 mul.396
  417.0 2.0 convolution_multiply_fusion
  419.1 1.2 pad_maximum_fusion.3
  420.3 2.6 copy.188
  423.9 2.5 copy.191
  426.6 1.6 mul.375
  428.2 2.6 mul.376
  430.8 1.7 multiply_reduce_fusion.3
  432.9 2.3 multiply_reduce_fusion
  437.2 4.4 convolution_convert_fusion.2
  441.9 8.2 %convolution_convert_fusion.1 = bf16[1536,2048]{1,0:T(8,128)(2,1)} fusion(bf16[512,1536]{1,0:T(8,128)(2,1)} %copy-done.47, bf16[512,2048]{1,0:T(8,128)(2,1)} %bitcast.169), kind=kOutput, calls=%fused_computation.2 | convolution fusion | flops 3224371200 | bytes 9961472 | tf_op jit(solution)/shard_map/dot_general | solution.py:287
  450.1 12.3 %convolution_convert_fusion = bf16[2048,3072]{1,0:T(8,128)(2,1)} fusion(bf16[512,2048]{1,0:T(8,128)(2,1)} %bitcast.174, bf16[512,1536]{1,0:T(8,128)(2,1)} %copy-done.49, bf16[512,1536]{1,0:T(8,128)(2,1)} %copy-done.48), kind=kOutput, calls=%fused_computation.1 | convolution fusion | flops 6455033856 | bytes 17825792 | tf_op jit(solution)/shard_map/dot_general | solution.py:287
  462.4 7.1 %fusion.3.partial_ref = f32[4,128,2048]{2,1,0:T(8,128)} fusion(bf16[4,128,1024]{2,1,0:T(8,128)(2,1)} %bitcast.198, bf16[2048,1024]{1,0:T(8,128)(2,1)} %copy-done.26), kind=kOutput, calls=%fused_computation.5 | convolution fusion | flops 2147483648 | bytes 9437184 | tf_op jit(solution)/shard_map/dot_general | solution.py:287
  469.5 41.9 %last.1 = (f32[2,64,2048]{2,1,0:T(8,128)S(1)}, f32[1,2048]{1,0:T(1,128)S(1)}) custom-call(f32[4,128,2048]{2,1,0:T(8,128)} %fusion.3.partial_ref, f32[2,64,2048]{2,1,0:T(8,128)S(1)} %copy-done.8, bf16[2,64,2048]{2,1,0:T(8,128)(2,1)S(1)} %bitcast.162, bf16[1,2048]{1,0:T(2,128)(2,1)S(1)} %broadcast_in_dim.30.gain_ref), custom_call_target="tpu_custom_call" | custom-call | tf_op jit(solution)/shard_map/last/pallas_call | solution.py:255
  512.4 40.2 %all-reduce = (f32[2048]{0:T(1024)}, f32[128]{0:T(128)}, f32[128]{0:T(128)}, f32[2048]{0:T(1024)}) all-reduce(f32[2048]{0:T(1024)S(1)} %bitcast.168, f32[128]{0:T(128)S(1)} %bitcast_reduce_fusion, f32[128]{0:T(128)S(1)} %bitcast_reduce_fusion.1, f32[2048]{0:T(1024)S(1)} %bitcast.167), channel_id=1, replica_groups=mesh['wide'=8,'narrow'=4] {'wide','narrow'}, use_global_device_ids=true, to_apply=%region_10.11 | all-reduce | flops 4352 | bytes 34816 | tf_op jit(solution)/shard_map/psum | solution.py:394
  552.6 1.8 convert_element_type.83
  554.4 1.8 slice.86
  556.2 1.8 fusion.35
  558.0 1.7 reduce-scatter.11.cloned.1.call-done
  559.6 2.4 convert_element_type.87
  562.0 93.8 %reduce-scatter.9.cloned.1.call-done = bf16[256,3072]{1,0:T(8,128)(2,1)} async-done(((bf16[2048,3072]{1,0:T(8,128)(2,1)}), bf16[256,3072]{1,0:T(8,128)(2,1)}) %reduce-scatter.9.cloned.1.call-update) | async-done | bytes 1572880 | tf_op jit(solution)/shard_map/reduce_scatter | solution.py:368
  655.8 3.4 fusion.34
  (158 shorter events, 25.3 us)
Async XLA Ops:
  7.2 136.5 %copy-start = (bf16[512,2048]{1,0:T(8,128)(2,1)S(1)}, bf16[512,2048]{1,0:T(8,128)(2,1)}, u32[]{:S(2)}) copy-start(bf16[512,2048]{1,0:T(8,128)(2,1)} %param.22) | copy-start | bytes 6291460
  7.2 545.4 %reduce-scatter.7.cloned.1.call-start = ((), (), s32[]{:S(2)}) async-start(), calls=%async_computation.5 | async-start | bytes 2359296 | tf_op jit(solution)/shard_map/reduce_scatter | solution.py:368
  8.1 2.1 copy-start.27
  8.1 2.2 copy-start.28
  10.2 2.3 copy-start.1
  10.2 2.3 copy-start.2
  10.5 2.0 copy-start.26
  86.6 6.1 copy-start.9
  86.6 6.1 copy-start.11
  93.0 1.6 copy-start.15
  95.6 6.8 %copy-start.42 = (s32[2,1,4]{2,1,0:T(1,128)S(1)}, s32[2,1,4]{2,1,0:T(1,128)}, u32[]{:S(2)}) copy-start(s32[2,1,4]{2,1,0:T(1,128)} %param.15) | copy-start | bytes 100
  101.5 6.3 copy-start.46
  102.4 7.5 %copy-start.45 = (f32[64]{0:T(128)S(1)}, f32[64]{0:T(128)}, u32[]{:S(2)}) copy-start(f32[64]{0:T(128)} %multiply_power_fusion) | copy-start | bytes 772
  111.0 0.8 copy-start.23
  114.5 3.4 copy-start.24
  115.2 3.7 copy-start.38
  116.5 4.3 copy-start.32
  129.9 2.8 copy-start.36
  134.7 3.1 copy-start.41
  147.0 96.6 %slice-start = ((s8[6291456]{0:T(1024)(128)(4,1)}), s8[4194304]{0:T(1024)(128)(4,1)S(1)}, s32[]{:S(2)}) async-start(s8[6291456]{0:T(1024)(128)(4,1)} %bitcast.205), calls=%async_computation.8 | async-start | bytes 8388608
  231.4 12.2 %copy-start.13 = (bf16[4,128,2048]{2,1,0:T(8,128)(2,1)}, bf16[4,128,2048]{2,1,0:T(8,128)(2,1)S(1)}, u32[]{:S(2)}) copy-start(bf16[4,128,2048]{2,1,0:T(8,128)(2,1)S(1)} %get-tuple-element.25) | copy-start | bytes 6291460
  231.4 12.2 %copy-start.10 = (bf16[4,128,2048]{2,1,0:T(8,128)(2,1)S(1)}, bf16[4,128,2048]{2,1,0:T(8,128)(2,1)}, u32[]{:S(2)}) copy-start(bf16[4,128,2048]{2,1,0:T(8,128)(2,1)} %copy-done.9) | copy-start | bytes 6291460
  231.4 12.2 %slice-start.1 = ((s8[6291456]{0:T(1024)(128)(4,1)}), s8[2097152]{0:T(1024)(128)(4,1)S(1)}, s32[]{:S(2)}) async-start(s8[6291456]{0:T(1024)(128)(4,1)} %bitcast.205), calls=%async_computation.9 | async-start | bytes 4194304
  250.3 5.0 copy-start.47
  250.3 5.0 copy-start.48
  250.3 5.0 copy-start.49
  381.5 1.0 copy-start.3
  382.5 1.0 copy-start.7
  387.7 166.7 %reduce-scatter.5.cloned.1.call-start = ((), (), s32[]{:S(2)}) async-start(), calls=%async_computation.4 | async-start | bytes 4718592 | tf_op jit(solution)/shard_map/reduce_scatter | solution.py:368
  392.9 3.1 copy-start.21
  392.9 3.1 copy-start.31
  392.9 3.1 copy-start.37
  400.5 3.7 copy-start.19
  400.5 3.7 copy-start.20
  403.2 1.0 copy-start.17
  405.5 3.3 copy-start.18
  407.3 1.5 copy-start.34
  407.3 1.5 copy-start.43
  408.8 3.4 copy-start.35
  414.1 4.8 copy-start.25
  417.0 2.2 copy-start.14
  417.0 2.2 copy-start.33
  417.0 2.2 copy-start.39
  426.4 4.4 copy-start.44
  426.4 4.4 copy-start.40
  426.4 4.4 copy-start.22
  430.8 2.1 copy-start.16
  432.9 2.3 copy-start.30
  435.2 2.0 copy-start.12
  435.4 1.0 copy-start.29
  441.6 118.0 %reduce-scatter.11.cloned.1.call-start = ((), (), s32[]{:S(2)}) async-start(), calls=%async_computation.7 | async-start | bytes 7077888 | tf_op jit(solution)/shard_map/reduce_scatter | solution.py:368
  450.1 205.8 %reduce-scatter.9.cloned.1.call-start = ((), (), s32[]{:S(2)}) async-start(), calls=%async_computation.6 | async-start | bytes 14155776 | tf_op jit(solution)/shard_map/reduce_scatter | solution.py:368
  462.4 7.1 %copy-start.8 = (f32[2,64,2048]{2,1,0:T(8,128)S(1)}, f32[2,64,2048]{2,1,0:T(8,128)}, u32[]{:S(2)}) copy-start(f32[2,64,2048]{2,1,0:T(8,128)} %copy-done.7) | copy-start | bytes 3145732
  511.3 1.0 copy-start.5
  562.0 97.2 %copy-start.4 = (f32[2,64,2048]{2,1,0:T(8,128)S(1)}, f32[2,64,2048]{2,1,0:T(8,128)}, u32[]{:S(2)}) copy-start(f32[2,64,2048]{2,1,0:T(8,128)} %copy-done.3) | copy-start | bytes 3145732
  659.3 1.6 copy-start.6
Sparse Core Ops, SparseCore 0:
  387.8 41.9 reduce-scatter.6
  441.8 52.0 reduce-scatter.4
  497.2 62.3 reduce-scatter.10
  563.4 92.3 reduce-scatter.8

commit v2 on v0

v2 whole, which is shorter than its diff:
```python
import functools

import jax
import jax.numpy as jnp
import numpy as np
from jax import lax
from jax.experimental import pallas as pl
from jax.experimental.pallas import tpu as pltpu
from jax.sharding import PartitionSpec as P

MESH = pl.DeviceIdType.MESH
F32 = jnp.float32
BF16 = jnp.bfloat16
norm_eps = 1e-06
masked_score = -1e30
HALVES = 2


def both(*conds):
    out = conds[0]
    for cond in conds[1:]:
        out = jnp.logical_and(out, cond)
    return out


def rows_at(index, rows):
    return pl.ds(pl.multiple_of(index * rows, rows), rows)


def lanes(index, width):
    return pl.ds(pl.multiple_of(index * width, width), width)


def dot(a, b, ca, cb):
    return lax.dot_general(a, b, (((ca,), (cb,)), ((), ())), preferred_element_type=F32)


def remote(src, dst, ssem, rsem, wide, narrow):
    return pltpu.make_async_remote_copy(
        src_ref=src, dst_ref=dst, send_sem=ssem, recv_sem=rsem, device_id=(wide, narrow), device_id_type=MESH
    )


def barrier(n, wide=0):
    w, z = lax.axis_index("wide"), lax.axis_index("narrow")
    bar = pltpu.get_barrier_semaphore()
    for step in range(1, n):
        pl.semaphore_signal(bar, inc=1, device_id=(w, lax.rem(z + step, n)), device_id_type=MESH)
    for step in range(1, wide):
        pl.semaphore_signal(bar, inc=1, device_id=(lax.rem(w + step, wide), z), device_id_type=MESH)
    pl.semaphore_wait(bar, n - 1 + max(wide - 1, 0))


class Line:
    def __init__(self, n, C, S):
        self.n, self.C, self.S = n, C, S
        self.pieces, self.rows = C * HALVES, S // HALVES
        self.w, self.z = lax.axis_index("wide"), lax.axis_index("narrow")

    def at(self, ref, chunk, p):
        start = chunk * self.S + (p % HALVES) * self.rows
        return ref.at[p // HALVES, pl.ds(pl.multiple_of(start, self.rows), self.rows)]


class Gather(Line):
    def __init__(self, n, C, S, full, ssem, rsem):
        super().__init__(n, C, S)
        self.full, self.ssem, self.rsem = full, ssem, rsem

    def copy(self, way, hop, p):
        chunk = self.z - hop if way == 0 else self.z + hop
        where = self.at(self.full, chunk, p)
        z_to = self.z + 1 if way == 0 else self.z - 1
        return remote(where, where, self.ssem.at[way, hop, p], self.rsem.at[way, hop, p], self.w, z_to)

    def arrival(self, way, hop, p):
        chunk = self.z - hop - 1 if way == 0 else self.z + hop + 1
        where = self.at(self.full, chunk, p)
        z_to = self.z + 1 if way == 0 else self.z - 1
        return remote(where, where, self.ssem.at[way, hop, p], self.rsem.at[way, hop, p], self.w, z_to)

    def has(self, way, hop):
        return self.z >= hop if way == 0 else self.z + hop <= self.n - 1

    def can_send(self, way, hop):
        edge = self.z < self.n - 1 if way == 0 else self.z > 0
        return both(self.has(way, hop), edge, hop < self.n - 1)

    def send(self, hop, p, ok=True):
        known = isinstance(hop, int)
        for way in (0, 1):
            if not (known and hop == 0):
                @pl.when(both(ok, hop > 0, self.has(way, hop)))
                def _():
                    self.arrival(way, hop - 1, p).wait_recv()

            if not (known and hop >= self.n - 1):
                @pl.when(both(ok, self.can_send(way, hop)))
                def _():
                    self.copy(way, hop, p).start()

    def drain(self):
        def step(t, carry):
            hop, p = t // self.pieces, t % self.pieces
            for way in (0, 1):
                @pl.when(self.can_send(way, hop))
                def _():
                    self.copy(way, hop, p).wait_send()
            return carry

        lax.fori_loop(0, (self.n - 1) * self.pieces, step, 0)


class Scatter(Line):
    def __init__(self, n, C, S, partial, sbuf, rbuf, ssem, rsem):
        super().__init__(n, C, S)
        self.partial, self.sbuf, self.rbuf, self.ssem, self.rsem = partial, sbuf, rbuf, ssem, rsem

    def copy(self, way, d, p):
        z_to = self.z + 1 - 2 * way
        slot = jnp.where(both(way == 1, d == z_to), self.n, d)
        return remote(
            self.at(self.sbuf, d, p), self.at(self.rbuf, slot, p), self.ssem.at[d, p], self.rsem.at[way, d, p], self.w, z_to
        )

    def slot(self, way, d):
        return jnp.where(both(way == 1, d == self.z), self.n, d)

    def arrived(self, way, d, p):
        where = self.at(self.rbuf, self.slot(way, d), p)
        remote(where, where, self.ssem.at[d, p], self.rsem.at[way, d, p], self.w, self.z).wait_recv()
        return where[...].astype(F32)

    def originate(self, p):
        def step(i, carry):
            way = jnp.where(self.z == 0, 0, 1)
            d = jnp.where(self.z == 0, self.n - 1 - i, i)

            @pl.when(jnp.logical_or(self.z == 0, self.z == self.n - 1))
            def _():
                if self.partial is not self.sbuf:
                    self.at(self.sbuf, d, p)[...] = self.at(self.partial, d, p)[...].astype(BF16)
                self.copy(way, d, p).start()

            return carry

        lax.fori_loop(0, self.n - 1, step, 0)

    def relay(self, i, p, ok=True):
        def step(order, carry):
            way = jnp.where(self.z < self.n // 2, order, 1 - order)
            d = jnp.where(way == 0, self.n - 1 - i, i)
            goes = jnp.where(way == 0, d > self.z, d < self.z)

            @pl.when(both(ok, goes, self.z > 0, self.z < self.n - 1))
            def _():
                value = self.arrived(way, d, p) + self.at(self.partial, d, p)[...].astype(F32)
                self.at(self.sbuf, d, p)[...] = value.astype(BF16)
                self.copy(way, d, p).start()

            return carry

        lax.fori_loop(0, 2, step, 0)

    def final(self, p, acc):
        acc[...] = self.at(self.partial, self.z, p)[...].astype(F32)
        for way, there in ((0, self.z > 0), (1, self.z < self.n - 1)):
            @pl.when(there)
            def _():
                acc[...] += self.arrived(way, self.z, p)

    def drain(self):
        def step(t, carry):
            d, p = t // self.pieces, t % self.pieces

            @pl.when(d != self.z)
            def _():
                self.copy(jnp.where(d > self.z, 0, 1), d, p).wait_send()

            return carry

        lax.fori_loop(0, self.n * self.pieces, step, 0)


def rms_scale(values):
    return lax.rsqrt(jnp.mean(values * values, axis=-1, keepdims=True) + norm_eps)


def rms_back(grad_in, hat, scale_rows):
    return scale_rows * (grad_in - hat * jnp.mean(grad_in * hat, axis=-1, keepdims=True))


def rope(v, cos2, sin2):
    return v * cos2 + pltpu.roll(v, v.shape[-1] // 2, axis=1) * sin2


def for_arrived(gath, hop, body):
    z, n = gath.z, gath.n
    if hop == 0:
        body(z)
        return
    left = (z >= hop).astype(jnp.int32)
    right = (z + hop <= n - 1).astype(jnp.int32)

    def step(i, carry):
        use_left = both(left == 1, i == 0)
        body(jnp.where(use_left, z - hop, z + hop))
        return carry

    lax.fori_loop(0, left + right, step, 0)


def front_kernel(n, C, S, HD, docs,
                 x_ref, gain_ref, lens_ref, freq_ref, qg_ref, kg_ref, wq_hbm, wk_hbm, wv_hbm,
                 normed_ref, q_ref, k_ref, qrot_ref, krot_ref, v_ref, prob_ref, mix_ref, cos_ref, sin_ref,
                 wq, wk, wv, bias, ssem, rsem, wsem):
    R = n * S
    QC, KC = wq.shape[1], wk.shape[1]
    G = QC // KC
    KH = KC // HD
    loads = [pltpu.make_async_copy(a, b, wsem.at[i]) for i, (a, b) in enumerate(((wq_hbm, wq), (wk_hbm, wk), (wv_hbm, wv)))]
    for load in loads:
        load.start()
    gath = Gather(n, C, S, normed_ref, ssem, rsem)
    z = gath.z
    for part in range(C):
        x = x_ref[part].astype(F32)
        normed_ref[part, rows_at(z, S)] = (x * rms_scale(x) * gain_ref[...].astype(F32)).astype(BF16)
    barrier(n)
    for p in range(gath.pieces):
        gath.send(0, p)
    for part in range(C):
        t = lax.broadcasted_iota(jnp.int32, (R, HD), 0)
        row = lax.broadcasted_iota(jnp.int32, (R, R), 0)
        col = lax.broadcasted_iota(jnp.int32, (R, R), 1)
        first = jnp.zeros((R, HD), jnp.int32)
        first_wide = jnp.zeros((R, R), jnp.int32)
        end = jnp.int32(0)
        for d in range(docs):
            end = end + lens_ref[part, d]
            first = jnp.where(t >= end, end, first)
            first_wide = jnp.where(row >= end, end, first_wide)
        angle = (t - first).astype(F32) * freq_ref[...]
        sign = jnp.where(lax.broadcasted_iota(jnp.int32, (R, HD), 1) < HD // 2, -1.0, 1.0)
        cos_ref[part] = jnp.cos(angle)
        sin_ref[part] = jnp.sin(angle) * sign
        bias[part] = jnp.where(both(col <= row, col >= first_wide), 0.0, masked_score)
    for load in loads:
        load.wait()

    def project(chunk, parts):
        rows = rows_at(chunk, S)
        lhs = jnp.concatenate([normed_ref[p, rows] for p in parts], axis=0)
        for w, out in ((wq, q_ref), (wk, k_ref), (wv, v_ref)):
            res = dot(lhs, w[...], 1, 0).astype(out.dtype)
            for i, p in enumerate(parts):
                out[p, rows] = res[i * S:(i + 1) * S]

    def attend(part):
        def heads(k, carry):
            cos2, sin2 = cos_ref[part], sin_ref[part]

            def turned(src, gain, col):
                raw = src[part, :, lanes(col, HD)]
                return rope(raw * rms_scale(raw) * gain[...].astype(F32), cos2, sin2).astype(BF16)

            kr = turned(k_ref, kg_ref, k)
            krot_ref[part, :, lanes(k, HD)] = kr
            for g in range(G):
                qr = turned(q_ref, qg_ref, k * G + g)
                qrot_ref[part, :, lanes(k * G + g, HD)] = qr
                s = dot(qr, kr, 1, 1) * HD ** (-0.5) + bias[part]
                ex = jnp.exp(s - jnp.max(s, axis=-1, keepdims=True))
                prob = ex / jnp.sum(ex, axis=-1, keepdims=True)
                prob_ref[part, k * G + g] = prob
                mix = dot(prob.astype(BF16), v_ref[part, :, lanes(k, HD)], 1, 0)
                mix_ref[part, :, lanes(k * G + g, HD)] = mix.astype(BF16)
            return carry

        lax.fori_loop(0, KH, heads, 0)

    for hop in range(n - 1):
        if hop > 0:
            for p in range(gath.pieces):
                gath.send(hop, p)
        for_arrived(gath, hop, lambda chunk: project(chunk, tuple(range(C))))
    for part in range(C):
        for h in range(HALVES):
            gath.send(n - 1, part * HALVES + h)
        for_arrived(gath, n - 1, lambda chunk: project(chunk, (part,)))
        attend(part)
    gath.drain()


def weight_block(A, B, sib_a, sib_b, q, cols):
    total = None
    for part in range(A.shape[0]):
        for term in (dot(A[part, :, cols], B[part], 0, 0), dot(sib_a[q, part], sib_b[part], 0, 0)):
            total = term if total is None else total + term
    return total


def middle_kernel(n, C, S, W, push, *refs):
    (x_ref, cot_ref, gain_ref, mix_hbm, wout_hbm, wgate_hbm, wup_hbm, wdown_hbm,
     middle_ref, dmid_ref, gaing_ref, dmix_ref, db_hbm, mlp_hbm) = refs[:14]
    rest = list(refs[14:])
    if push:
        sib_n2, sib_cot, sib_act, sib_dg, sib_du, recv_down, blk_gate, blk_up, own_down, own_gate, own_up = rest[:11]
        rest = rest[11:]
    else:
        n2_hbm, cot_hbm, act_hbm, dg_hbm, du_hbm = rest[:5]
        rest = rest[5:]
    (mixv, wout, wgate, wup, wdown, cotf, n2f, dbf, partial, sbuf, rbuf, sbufm, dact, act, dg, du, acc,
     wsem, cs, cr, s1s, s1r, g2s, g2r, s2s, s2r, g3s, g3r, osem) = rest[:29]
    rest = rest[29:]
    if push:
        stage, stage32, cols_sib, b_sib, sib_ss, sib_rs, down_ss, down_rs, lsem, ssem32 = rest
    R = n * S
    D = x_ref.shape[2]
    FC = wgate.shape[1]
    TN = 512
    nt, nd = FC // TN, D // TN
    P_ = C * HALVES
    rows = S // HALVES
    w, z = lax.axis_index("wide"), lax.axis_index("narrow")
    loads = [pltpu.make_async_copy(a, b, wsem.at[i]) for i, (a, b) in enumerate(
        ((mix_hbm, mixv), (wout_hbm, wout), (wdown_hbm, wdown), (wgate_hbm, wgate), (wup_hbm, wup)))]
    for load in loads:
        load.start()
    for part in range(C):
        cotf[part, rows_at(z, S)] = cot_ref[part]
    barrier(n, W if push else 0)
    gc = Gather(n, C, S, cotf, cs, cr)
    g2 = Gather(n, C, S, n2f, g2s, g2r)
    g3 = Gather(n, C, S, dbf, g3s, g3r)
    s1 = Scatter(n, C, S, partial, sbuf, rbuf, s1s, s1r)
    s2 = Scatter(n, C, S, partial, sbuf, rbuf, s2s, s2r)
    gain = gain_ref[...].astype(F32)
    loads[0].wait()
    loads[1].wait()

    def tiles(count, body):
        def step(j, carry):
            body(j)
            return carry

        lax.fori_loop(0, count, step, 0)

    for part in range(C):
        def out_tile(j):
            partial[part, :, lanes(j, TN)] = dot(mixv[part], wout[:, lanes(j, TN)], 1, 0)

        tiles(nd, out_tile)
        if part == 0:
            for p in range(2):
                s1.originate(p)
                gc.send(0, p)

    def mid_row(p):
        return p // HALVES, rows_at(p % HALVES, rows)

    def phase_one(p):
        @pl.when(p + 2 < P_)
        def _():
            s1.originate(p + 2)
            gc.send(0, p + 2)

        def service(i, carry):
            s1.relay(i, p, p < P_)
            gc.send(i + 1, p, p < P_)
            g2.send(i + 1, p - 1, p > 0)
            return carry

        lax.fori_loop(0, n - 1, service, 0)
        s1.final(p, acc)
        part, rr = mid_row(p)
        middle = x_ref[part, rr].astype(F32) + acc[...]
        middle_ref[part, rr] = middle
        g2.at(n2f, z, p)[...] = (middle * rms_scale(middle) * gain).astype(BF16)
        g2.send(0, p)

    tiles(P_, phase_one)
    loads[2].wait()

    def dact_tile(part, j):
        dact[:, lanes(j, TN)] = dot(cotf[part], wdown[rows_at(j, TN), :], 1, 1)

    for i in range(max(n - 1, nt)):
        if i < nt:
            dact_tile(0, i)
        if i < n - 1:
            g2.send(i + 1, P_ - 1)
    s1.drain()
    if push:
        core = w % 2
        mate = w + 1 - 2 * core
        Q = W // 2
        q_me = w // 2

        def swap(index, src, dst, part):
            return remote(src.at[part], dst.at[part], sib_ss.at[index, part], sib_rs.at[index, part], mate, z)

        for part in range(C):
            swap(0, n2f, sib_n2, part).start()
            swap(1, cotf, sib_cot, part).start()
    loads[3].wait()
    loads[4].wait()

    def service(t, ok=True):
        p, i = t // (n - 1), t % (n - 1)
        s2.relay(i, p, both(ok, p < P_))

        @pl.when(both(ok, i == n - 2, p < P_))
        def _():
            s2.final(p, acc)
            part, rr = mid_row(p)
            dn2 = acc[...]
            middle = middle_ref[part, rr]
            scale = rms_scale(middle)
            hat = middle * scale
            gaing_ref[...] += jnp.sum(dn2 * hat, axis=0, keepdims=True)
            dmid = cot_ref[part, rr].astype(F32) + rms_back(dn2 * gain, hat, scale)
            dmid_ref[part, rr] = dmid
            g3.at(dbf, z, p)[...] = dmid.astype(BF16)

        g3.send(i + 1, p - 1, both(ok, p > 0, p <= P_))

        @pl.when(both(ok, i == n - 2, p < P_))
        def _():
            g3.send(0, p)

    gaing_ref[...] = jnp.zeros_like(gaing_ref)
    per_part = HALVES * (n - 1)

    def feed(part):
        def gate_tile(j):
            @pl.when(part > 0)
            def _():
                dact_tile(part, j)

            at = lanes(j, TN)
            gate = dot(n2f[part], wgate[:, at], 1, 0)
            up = dot(n2f[part], wup[:, at], 1, 0)
            sig = jax.nn.sigmoid(gate)
            silu = gate * sig
            d_act = dact[:, at]
            act[part, :, at] = (silu * up).astype(BF16)
            dg[part, :, at] = (d_act * up * sig * (1.0 + gate * (1.0 - sig))).astype(BF16)
            du[part, :, at] = (d_act * silu).astype(BF16)
            service((part - 1) * per_part + j, both(part > 0, j < per_part))

        tiles(nt, gate_tile)
        if push:
            swap(2, act, sib_act, part).start()
            swap(3, dg, sib_dg, part).start()
            swap(4, du, sib_du, part).start()

        def back_tile(j):
            at = rows_at(j, TN)
            partial[part, :, lanes(j, TN)] = dot(dg[part], wgate[at, :], 1, 1) + dot(du[part], wup[at, :], 1, 1)
            service((part - 1) * per_part + nt + j, both(part > 0, nt + j < per_part))

        tiles(nd, back_tile)
        for h in range(HALVES):
            s2.originate(part * HALVES + h)

    tiles(C, feed)

    def mlp_tile(j):
        for part in range(C):
            sbufm[part, :, lanes(j, TN)] = dot(act[part], wdown[:, lanes(j, TN)], 1, 0).astype(BF16)

    first = (C - 1) * per_part
    last = (P_ + 1) * (n - 1)
    if push:
        width = D // W

        def load_cols(src):
            for q in range(Q):
                for part in range(C):
                    yield pltpu.make_async_copy(
                        src.at[part, :, lanes(2 * q + core, width)], cols_sib.at[q, part], lsem.at[0, q, part])

        def load_b(src):
            for part in range(C):
                yield pltpu.make_async_copy(src.at[part], b_sib.at[part], lsem.at[1, 0, part])

        def fetch(copies):
            copies = list(copies)
            for copy in copies:
                copy.start()
            for copy in copies:
                copy.wait()

        def down_push(o):
            q = lax.rem(q_me + o, Q)
            return remote(stage.at[o - 1], recv_down.at[o - 1], down_ss.at[o - 1], down_rs.at[o - 1], 2 * q + core, z)

        def block(A, B, o):
            q = lax.rem(q_me + o, Q)
            return weight_block(A, B, cols_sib, b_sib, q, lanes(2 * q + core, width))

        def own_copy(dst, index):
            return pltpu.make_async_copy(stage32, dst, ssem32.at[index])

        def put_copy(dst, o, index):
            slot = Q - 1 + (o - 1) % 2
            return pltpu.make_async_copy(stage.at[slot], dst.at[o - 1], osem.at[4 + index * (Q - 1) + o - 1])

        work = []

        def start_down():
            for part in range(C):
                swap(1, sib_cot, sib_cot, part).wait_recv()
                swap(2, sib_act, sib_act, part).wait_recv()
            fetch(load_cols(sib_cot))
            fetch(load_b(sib_act))

        def down(o):
            if o == 1:
                start_down()
            if o < Q:
                stage[o - 1] = block(cotf, act, o).astype(BF16)
                down_push(o).start()
            else:
                stage32[...] = block(cotf, act, 0)
                own_copy(own_down, 0).start()

        def other(index, B, sib_b, own, blocks, o):
            if o == 1:
                for part in range(C):
                    if index == 0:
                        swap(0, sib_n2, sib_n2, part).wait_recv()
                    swap(3 + index, sib_b, sib_b, part).wait_recv()
                if index == 0:
                    fetch(load_cols(sib_n2))
                fetch(load_b(sib_b))
            if o < Q:
                if o > 2:
                    put_copy(blocks, o - 2, index).wait()
                elif index > 0:
                    prev = Q - 1 - (Q - 1 - o) % 2
                    put_copy(blk_gate, prev, 0).wait()
                stage[Q - 1 + (o - 1) % 2] = block(n2f, B, o).astype(BF16)
                put_copy(blocks, o, index).start()
            else:
                own_copy(own_gate, index).wait()
                stage32[...] = block(n2f, B, 0)
                own_copy(own, index + 1).start()

        for o in range(1, Q + 1):
            work.append(functools.partial(down, o))
        for j in range(nd):
            work.append(functools.partial(mlp_tile, j))
        for o in range(1, Q + 1):
            work.append(functools.partial(other, 0, dg, sib_dg, own_gate, blk_gate, o))
        for o in range(1, Q + 1):
            work.append(functools.partial(other, 1, du, sib_du, own_up, blk_up, o))
        steps = last - first
        done = 0
        for k in range(steps):
            service(first + k)
            upto = -(-len(work) * (k + 1) // steps)
            for piece in work[done:upto]:
                piece()
            done = upto
    else:
        tiles(last - first, lambda k: service(first + k))
        tiles(nd, mlp_tile)
        outs = [pltpu.make_async_copy(a, b, osem.at[4 + i]) for i, (a, b) in enumerate(
            ((n2f, n2_hbm), (cotf, cot_hbm), (act, act_hbm), (dg, dg_hbm), (du, du_hbm)))]
        for out in outs:
            out.start()
    mlp_out = pltpu.make_async_copy(sbufm, mlp_hbm, osem.at[0])
    mlp_out.start()
    db_out = pltpu.make_async_copy(dbf, db_hbm, osem.at[1])
    db_out.start()
    for part in range(C):
        dmix_ref[part] = dot(dbf[part], wout[...], 1, 1).astype(BF16)
    mlp_out.wait()
    db_out.wait()
    gc.drain()
    g2.drain()
    g3.drain()
    s2.drain()
    if push:
        for part in range(C):
            for index, (a, b) in enumerate(((n2f, sib_n2), (cotf, sib_cot), (act, sib_act), (dg, sib_dg), (du, sib_du))):
                swap(index, a, b, part).wait_send()
        for index, blocks in enumerate((blk_gate, blk_up)):
            for o in range(1, Q):
                if index == 1 and o > Q - 3:
                    put_copy(blocks, o, index).wait()
        own_copy(own_up, 2).wait()
        for o in range(1, Q):
            down_push(o).wait_send()
            down_push(o).wait_recv()
    else:
        for out in outs:
            out.wait()


def last_kernel(n, C, S, W, HD, push, *refs):
    (x_ref, middle_ref, dmid_ref, gain_ref, qg_ref, kg_ref, gmlp_ref, q_ref, k_ref, qrot_ref, krot_ref, v_ref, prob_ref,
     cos_ref, sin_ref, dmix_ref, mlp_hbm, wq_hbm, wk_hbm, wv_hbm) = refs[:20]
    rest = list(refs[20:])
    if push:
        mix_hbm, db_hbm, normed_hbm, blk_gate, blk_up = rest[:5]
        rest = rest[5:]
    out_ref, in_ref, ga_ref, gm_ref, gq_ref, gk_ref = rest[:6]
    rest = rest[6:]
    if push:
        recv_gate, recv_up, recv_out, recv_qkv, own_out, own_qkv = rest[:6]
        rest = rest[6:]
    else:
        dproj_hbm = rest[0]
        rest = rest[1:]
    (wq, wk, wv, dproj, partial, sbuf, rbuf, sbufm, rbufm, acc, gains, small, small_two,
     lsem, s3s, s3r, sms, smr, gs1, gr1, gs2, gr2) = rest[:22]
    rest = rest[22:]
    if push:
        (mixv, dbv, normv, sib_mix, sib_db, sib_norm, sib_dproj, stage_out, stage_qkv,
         sib_ss, sib_rs, push_ss, push_rs) = rest
    R, D = n * S, x_ref.shape[2]
    QC, KC = wq.shape[1], wk.shape[1]
    G, KH = QC // KC, KC // HD
    TN = 512
    nd = D // TN
    P_ = C * HALVES
    rows = S // HALVES
    w, z = lax.axis_index("wide"), lax.axis_index("narrow")
    pairs = [(mlp_hbm, sbufm), (wq_hbm, wq), (wk_hbm, wk), (wv_hbm, wv)]
    if push:
        pairs += [(mix_hbm, mixv), (db_hbm, dbv), (normed_hbm, normv)]
    loads = [pltpu.make_async_copy(a, b, lsem.at[i]) for i, (a, b) in enumerate(pairs)]
    for load in loads:
        load.start()
    barrier(n, W)
    sm = Scatter(n, C, S, sbufm, sbufm, rbufm, sms, smr)
    s3 = Scatter(n, C, S, partial, sbuf, rbuf, s3s, s3r)
    if push:
        core = w % 2
        mate = w + 1 - 2 * core
        Q = W // 2
        q_me = w // 2
        width = D // W

        def direct(index, src, dst, o):
            q = lax.rem(q_me + o, Q)
            return remote(src.at[o - 1], dst.at[o - 1], push_ss.at[index, o - 1], push_rs.at[index, o - 1], 2 * q + core, z)

        def swap(index, src, dst, part):
            return remote(src.at[part], dst.at[part], sib_ss.at[index, part], sib_rs.at[index, part], mate, z)

        for index, (src, dst) in enumerate(((blk_gate, recv_gate), (blk_up, recv_up))):
            for o in range(1, Q):
                direct(index, src, dst, o).start()
    loads[0].wait()
    for p in range(2):
        sm.originate(p)
    if push:
        for load in loads[4:]:
            load.wait()
        for part in range(C):
            for index, (a, b) in enumerate(((mixv, sib_mix), (dbv, sib_db), (normv, sib_norm))):
                swap(index, a, b, part).start()

    def piece_row(p):
        return p // HALVES, rows_at(p % HALVES, rows)

    def mlp_service(p):
        for i in range(n - 1):
            sm.relay(i, p)
        sm.final(p, acc)
        part, rr = piece_row(p)
        out_ref[part, rr] = middle_ref[part, rr] + acc[...]

        @pl.when(p + 2 < P_)
        def _():
            sm.originate(p + 2)

    gain = gain_ref[...].astype(F32)

    def service(t):
        p, i = t // (n - 1), t % (n - 1)
        s3.relay(i, p)

        @pl.when(i == n - 2)
        def _():
            s3.final(p, acc)
            part, rr = piece_row(p)
            dn = acc[...]
            x = x_ref[part, rr].astype(F32)
            scale = rms_scale(x)
            hat = x * scale
            gains[0:1, :] += jnp.sum(dn * hat, axis=0, keepdims=True)
            in_ref[part, rr] = dmid_ref[part, rr] + rms_back(dn * gain, hat, scale)

    gains[...] = jnp.zeros_like(gains)
    scale = HD ** (-0.5)
    qgain, kgain = qg_ref[...].astype(F32), kg_ref[...].astype(F32)

    def unit(part, k):
        cos2, sin2 = cos_ref[part], sin_ref[part]
        kr, vr = krot_ref[part, :, lanes(k, HD)], v_ref[part, :, lanes(k, HD)]

        def unturned(grad, raw, head_gain, at):
            d_n = grad * cos2 - pltpu.roll(grad, HD // 2, axis=1) * sin2
            r = rms_scale(raw)
            hat = raw * r
            gains[at:at + 1, :HD] += jnp.sum(d_n * hat, axis=0, keepdims=True)
            return rms_back(d_n * head_gain, hat, r).astype(BF16)

        dk, dv = None, None
        for g in range(G):
            h = k * G + g
            pr = prob_ref[part, h]
            dm = dmix_ref[part, :, lanes(h, HD)]
            dp = dot(dm, vr, 1, 1)
            one = dot(pr.astype(BF16), dm, 0, 0)
            dv = one if dv is None else dv + one
            ds = (pr * (dp - jnp.sum(pr * dp, axis=-1, keepdims=True))).astype(BF16)
            one = dot(ds, qrot_ref[part, :, lanes(h, HD)], 0, 0)
            dk = one if dk is None else dk + one
            dq = dot(ds, kr, 1, 0) * scale
            dproj[part, :, lanes(h, HD)] = unturned(dq, q_ref[part, :, lanes(h, HD)], qgain, 1)
        dproj[part, :, lanes(QC // HD + k, HD)] = unturned(dk * scale, k_ref[part, :, lanes(k, HD)], kgain, 2)
        dproj[part, :, lanes(QC // HD + KH + k, HD)] = dv.astype(BF16)

    pieces_per_unit = -(-P_ // (C * KH))

    def backward(part):
        def heads(k, carry):
            unit(part, k)
            for e in range(pieces_per_unit):
                p = (part * KH + k) * pieces_per_unit + e

                @pl.when(p < P_)
                def _():
                    mlp_service(p)

            return carry

        lax.fori_loop(0, KH, heads, 0)

        @pl.when(part == 0)
        def _():
            for load in loads[1:4]:
                load.wait()

        if push:
            swap(3, dproj, sib_dproj, part).start()

        def back_tile(j, carry):
            at = rows_at(j, TN)
            partial[part, :, lanes(j, TN)] = (
                dot(dproj[part, :, 0:QC], wq[at, :], 1, 1) + dot(dproj[part, :, QC:QC + KC], wk[at, :], 1, 1)
                + dot(dproj[part, :, QC + KC:QC + 2 * KC], wv[at, :], 1, 1))
            return carry

        lax.fori_loop(0, nd, back_tile, 0)
        for h in range(HALVES):
            s3.originate(part * HALVES + h)

    def both_parts(part, carry):
        backward(part)
        return carry

    lax.fori_loop(0, C, both_parts, 0)
    steps = P_ * (n - 1)
    if push:
        def block(A, B, sib_a, sib_b, q):
            cols = lanes(2 * q + core, width)
            total = None
            for part in range(C):
                for term in (dot(A[part, :, cols], B[part], 0, 0), dot(sib_a[part, :, cols], sib_b[part], 0, 0)):
                    total = term if total is None else total + term
            return total

        def out_block(o):
            if o == 1:
                for part in range(C):
                    for index, (a, b) in enumerate(((mixv, sib_mix), (dbv, sib_db), (normv, sib_norm), (dproj, sib_dproj))):
                        swap(index, a, b, part).wait_recv()
            if o < Q:
                stage_out[o - 1] = block(dbv, mixv, sib_db, sib_mix, lax.rem(q_me + o, Q)).astype(BF16)
                direct(2, stage_out, recv_out, o).start()
            else:
                own_out[...] = block(dbv, mixv, sib_db, sib_mix, q_me)

        def qkv_block(o):
            if o < Q:
                stage_qkv[o - 1] = block(normv, dproj, sib_norm, sib_dproj, lax.rem(q_me + o, Q)).astype(BF16)
                direct(3, stage_qkv, recv_qkv, o).start()
            else:
                own_qkv[...] = block(normv, dproj, sib_norm, sib_dproj, q_me)

        work = [functools.partial(f, o) for f in (qkv_block, out_block) for o in range(1, Q + 1)]
        work = [functools.partial(f, o) for f in (out_block, qkv_block) for o in range(1, Q)] + [
            functools.partial(f, Q) for f in (out_block, qkv_block)]
        done = 0
        for k in range(steps):
            service(k)
            upto = min(len(work), k + 1)
            for piece in work[done:upto]:
                piece()
            done = upto
        for piece in work[done:]:
            piece()
    else:
        def only_service(k, carry):
            service(k)
            return carry

        lax.fori_loop(0, steps, only_service, 0)
        out = pltpu.make_async_copy(dproj, dproj_hbm, lsem.at[4])
        out.start()
    L = 2 * D + 2 * HD
    small[w, :, 0:D] = gains[0:1, :]
    small[w, :, D:2 * D] = gmlp_ref[...]
    small[w, :, 2 * D:2 * D + HD] = gains[1:2, :HD]
    small[w, :, 2 * D + HD:L] = gains[2:3, :HD]

    def to_wide(s):
        return remote(small.at[w], small.at[w], gs1.at[s], gr1.at[s], lax.rem(w + s, W), z)

    def to_narrow(s):
        return remote(small_two.at[z], small_two.at[z], gs2.at[s], gr2.at[s], w, lax.rem(z + s, n))

    for s in range(1, W):
        to_wide(s).start()
    for s in range(1, W):
        to_wide(s).wait_recv()
    total = small[0]
    for s in range(1, W):
        total = total + small[s]
    small_two[z] = total
    for s in range(1, n):
        to_narrow(s).start()
    for s in range(1, n):
        to_narrow(s).wait_recv()
    total = small_two[0]
    for s in range(1, n):
        total = total + small_two[s]
    ga_ref[...] = total[:, 0:D]
    gm_ref[...] = total[:, D:2 * D]
    gq_ref[...] = total[:, 2 * D:2 * D + HD]
    gk_ref[...] = total[:, 2 * D + HD:L]
    for s in range(1, W):
        to_wide(s).wait_send()
    for s in range(1, n):
        to_narrow(s).wait_send()
    sm.drain()
    s3.drain()
    if push:
        for part in range(C):
            for index, (a, b) in enumerate(((mixv, sib_mix), (dbv, sib_db), (normv, sib_norm), (dproj, sib_dproj))):
                swap(index, a, b, part).wait_send()
        for index, (src, dst) in enumerate(((blk_gate, recv_gate), (blk_up, recv_up), (stage_out, recv_out), (stage_qkv, recv_qkv))):
            for o in range(1, Q):
                direct(index, src, dst, o).wait_send()
                direct(index, src, dst, o).wait_recv()
    else:
        out.wait()


def local(W, layer_input, document_lengths, attn_gain, w_query, w_key, w_value, query_gain, key_gain, w_out, mlp_gain,
          w_gate, w_up, w_down, output_cotangent):
    n = lax.axis_size("narrow")
    C, _, S, D = layer_input.shape
    R = n * S
    T = C * R
    HD = query_gain.shape[0]
    QC, KC = w_query.shape[1], w_key.shape[1]
    QH = QC // HD
    FC = w_gate.shape[1]
    docs = document_lengths.shape[2]
    P_ = C * HALVES
    push = W % 2 == 0 and W >= 4 and W <= 8 and (D // W) % 128 == 0
    Q = W // 2
    width = D // W
    x_own, cot_own = layer_input[:, 0], output_cotangent[:, 0]
    sds = jax.ShapeDtypeStruct
    dma = pltpu.SemaphoreType.DMA
    gsem = lambda: dma((2, n - 1, P_))
    half = np.arange(HD) % (HD // 2)
    freq = jnp.asarray(np.power(np.float32(1000000.0), np.float32(-2.0) * half.astype(np.float32) / np.float32(HD))[None], F32)
    vm = pl.BlockSpec(memory_space=pltpu.VMEM)
    hbm = pl.BlockSpec(memory_space=pl.ANY)
    smem = pl.BlockSpec(memory_space=pltpu.SMEM)
    VM = pltpu.VMEM

    normed_full, q_raw, k_raw, q_rot, k_rot, v_rows, prob, mix, cos2, sin2 = pl.pallas_call(
        functools.partial(front_kernel, n, C, S, HD, docs), name="front",
        out_shape=[sds((C, R, D), BF16), sds((C, R, QC), F32), sds((C, R, KC), F32), sds((C, R, QC), BF16), sds((C, R, KC), BF16),
                   sds((C, R, KC), BF16), sds((C, QH, R, R), F32), sds((C, R, QC), BF16), sds((C, R, HD), F32), sds((C, R, HD), F32)],
        in_specs=[vm, vm, smem, vm, vm, vm, hbm, hbm, hbm], out_specs=[vm] * 10,
        scratch_shapes=[VM(w_query.shape, BF16), VM(w_key.shape, BF16), VM(w_value.shape, BF16),
                        VM((C, R, R), F32), gsem(), gsem(), dma((3,))],
        compiler_params=pltpu.CompilerParams(collective_id=0, has_side_effects=True, vmem_limit_bytes=48 << 20),
    )(x_own, attn_gain[None], document_lengths[:, 0], freq, query_gain[None], key_gain[None], w_query, w_key, w_value)

    full, wide_rows = sds((C, R, D), BF16), sds((C, R, FC), BF16)
    outs = [sds((C, S, D), F32), sds((C, S, D), F32), sds((1, D), F32), sds((C, R, QC), BF16), full, full]
    specs = [vm, vm, vm, vm, hbm, hbm]
    line = lambda: [VM((C, R, D), BF16), VM((C, R + S, D), BF16)]
    scratch = (
        [VM((C, R, QC), BF16), VM(w_out.shape, BF16), VM(w_gate.shape, BF16), VM(w_up.shape, BF16), VM(w_down.shape, BF16)]
        + [VM((C, R, D), BF16)] * 3 + [VM((C, R, D), F32)] + line()
        + [VM((C, R, D), BF16), VM((R, FC), F32)] + [VM((C, R, FC), BF16)] * 3 + [VM((S // HALVES, D), F32)]
        + [dma((5,)), gsem(), gsem(), dma((n, P_)), dma((2, n, P_)), gsem(), gsem(), dma((n, P_)), dma((2, n, P_)),
           gsem(), gsem(), dma((4 + max(2 * (Q - 1), 5),))]
    )
    if push:
        some, own = sds((Q - 1, width, FC), BF16), sds((width, FC), F32)
        outs += [full, full, wide_rows, wide_rows, wide_rows, some, some, some, own, own, own]
        scratch += [VM((Q + 1, width, FC), BF16), VM((width, FC), F32), VM((Q, C, R, width), BF16), VM((C, R, FC), BF16),
                    dma((5, C)), dma((5, C)), dma((Q - 1,)), dma((Q - 1,)), dma((2, Q, C)), dma((3,))]
    else:
        outs += [full, full, wide_rows, wide_rows, wide_rows]
    res = pl.pallas_call(
        functools.partial(middle_kernel, n, C, S, W, push), name="middle", out_shape=outs,
        in_specs=[vm] * 3 + [hbm] * 5, out_specs=specs + [hbm] * (len(outs) - len(specs)), scratch_shapes=scratch,
        compiler_params=pltpu.CompilerParams(collective_id=1, has_side_effects=True, vmem_limit_bytes=63 << 20),
    )(x_own, cot_own, mlp_gain[None], mix, w_out, w_gate, w_up, w_down)
    middle, d_middle, gmlp, d_mix, db_full, mlp_sums = res[:6]

    args = [x_own, middle, d_middle, attn_gain[None], query_gain[None], key_gain[None], gmlp, q_raw, k_raw, q_rot, k_rot, v_rows,
            prob, cos2, sin2, d_mix, mlp_sums, w_query, w_key, w_value]
    in_specs = [vm] * 16 + [hbm] * 4
    own_rows = sds((C, S, D), F32)
    outs = [own_rows, own_rows, sds((1, D), F32), sds((1, D), F32), sds((1, HD), F32), sds((1, HD), F32)]
    specs = [vm] * 6
    PC = QC + 2 * KC
    L = 2 * D + 2 * HD
    scratch = (
        [VM(w_query.shape, BF16), VM(w_key.shape, BF16), VM(w_value.shape, BF16), VM((C, R, PC), BF16), VM((C, R, D), F32)]
        + line() + line() + [VM((S // HALVES, D), F32), VM((8, D), F32), VM((W, 1, L), F32), VM((n, 1, L), F32)]
        + [dma((7,)), dma((n, P_)), dma((2, n, P_)), dma((n, P_)), dma((2, n, P_)), dma((W,)), dma((W,)), dma((n,)), dma((n,))]
    )
    if push:
        sib_n2, sib_cot, sib_act, sib_dg, sib_du, recv_down, blk_gate, blk_up, own_down, own_gate, own_up = res[6:]
        args += [mix, db_full, normed_full, blk_gate, blk_up]
        in_specs += [hbm] * 5
        outs += [sds((Q - 1, width, FC), BF16)] * 2 + [sds((Q - 1, width, QC), BF16), sds((Q - 1, width, PC), BF16),
                                                       sds((width, QC), F32), sds((width, PC), F32)]
        specs += [hbm] * 4 + [vm] * 2
        scratch += [VM((C, R, QC), BF16), VM((C, R, D), BF16), VM((C, R, D), BF16)]
        scratch += [VM((C, R, QC), BF16), VM((C, R, D), BF16), VM((C, R, D), BF16), VM((C, R, PC), BF16)]
        scratch += [VM((Q - 1, width, QC), BF16), VM((Q - 1, width, PC), BF16)]
        scratch += [dma((4, C)), dma((4, C)), dma((4, Q - 1)), dma((4, Q - 1))]
    else:
        outs += [sds((C, R, PC), BF16)]
        specs += [hbm]
    last = pl.pallas_call(
        functools.partial(last_kernel, n, C, S, W, HD, push), name="last", out_shape=outs, in_specs=in_specs, out_specs=specs,
        scratch_shapes=scratch,
        compiler_params=pltpu.CompilerParams(collective_id=2, has_side_effects=True, vmem_limit_bytes=60 << 20),
    )(*args)
    out_own, in_own, g_attn, g_mlp, g_query, g_key = last[:6]
    if push:
        recv_gate, recv_up, recv_out, recv_qkv, own_out, own_qkv = last[6:]

        def gathered(own, parts):
            return own + jnp.sum(parts.astype(F32), axis=0)

        down = gathered(own_down, recv_down).T
        gate, up = gathered(own_gate, recv_gate), gathered(own_up, recv_up)
        out_g = gathered(own_out, recv_out).T
        qkv = gathered(own_qkv, recv_qkv)
    else:
        n2, cot, act, dg, du = [v.reshape(T, -1) for v in res[6:]]
        d_proj = last[6].reshape(T, PC)
        db, mixed, normed = db_full.reshape(T, D), mix.reshape(T, QC), normed_full.reshape(T, D)

        def scatter(a, b, dim):
            return lax.psum_scatter(dot(a, b, 0, 0).astype(BF16), "wide", scatter_dimension=dim, tiled=True).astype(F32)

        down, gate, up = scatter(act, cot, 1), scatter(n2, dg, 0), scatter(n2, du, 0)
        out_g, qkv = scatter(mixed, db, 1), scatter(normed, d_proj, 0)
    return (
        out_own[:, None], in_own[:, None], g_attn[0], qkv[:, :QC], qkv[:, QC:QC + KC], qkv[:, QC + KC:],
        g_query[0], g_key[0], out_g, g_mlp[0], gate, up, down,
    )


def solution(mesh):
    rows = P(None, "wide", "narrow", None)
    cols, tall = P(None, "narrow"), P("narrow", None)
    in_specs = (rows, P(None, "wide", None), P(), cols, cols, cols, P(), P(), tall, P(), cols, cols, tall, rows)
    both_ways, turned = P("wide", "narrow"), P("narrow", "wide")
    out_specs = (rows, rows, P(), both_ways, both_ways, both_ways, P(), P(), turned, P(), both_ways, both_ways, turned)
    body = functools.partial(local, mesh.shape["wide"])
    return jax.shard_map(body, mesh=mesh, in_specs=in_specs, out_specs=out_specs, check_vma=False)
```

time: 1080 us -> 401 us (0.37)
  waiting for transfers between devices: 723 us -> 0 us
  Pallas kernels: 0 us -> 366 us
  matrix products: 156 us -> 0 us
  other arithmetic: 61.7 us -> 9.86 us
  local copies, waits for them, and re-layouts: 73.9 us -> 24.1 us
  blocking collectives: 41.1 us -> 0 us
  between operations: 16.1 us -> 0.78 us
    reduce_scatter x12 -> x0, waiting for transfers between devices: 560 us -> none  [the longest x1 157 us: local(): lax.psum_scatter(totals[1], 'wide', scatter_dimension=0, tiled=True)]
    pallas_call x0 -> x3, Pallas kernels: none -> 366 us  [the longest x1 200 us: local(): pl.pallas_call(functools.partial(middle_kernel, n, C, S, W, push), name='...]
    all_gather x8 -> x0, waiting for transfers between devices: 161 us -> none  [the longest x2 42.9 us: local(): normed_full = lax.all_gather(normed, 'narrow', axis=0, tiled=True)]
    dot_general x36 -> x0, matrix products: 156 us -> none  [the longest x8 48.3 us: contract_rows(): lax.dot_general(left_side, right_side, (((0,), (0,)), ((), ())), preferre...]
    psum x1 -> x0, blocking collectives: 41.1 us -> none  [local(): small_sums = lax.psum(small_totals, ('wide', 'narrow'))]
    reduce_sum x24 -> x4, other arithmetic: 24.3 us -> 5.7 us  [gathered(): return own + jnp.sum(parts.astype(F32), axis=0)]
    reshape x10 -> x0, local copies, waits for them, and re-layouts: 14 us -> none  [the longest x2 3.31 us: local(): d_value.reshape(seq_len, key_cols)]
    slice x12 -> x2, local copies, waits for them, and re-layouts: 15.5 us -> 1.68 us  [the longest x1 0.84 us: local(): qkv[:, :QC]]
  transfers between devices with their start and end apart: 20 -> 0, of which waited for: 18 -> 0; matrix products, arithmetic and copies ran while one was open for 16% -> 0% of each run, Pallas kernels for 0% -> 0%
where the time goes in v2:
time: 401 us
  Pallas kernels  366 us (91%)
  local copies, waits for them, and re-layouts  24.1 us (6%)
  other arithmetic  9.86 us (2%)
    pallas_call x1, Pallas kernels, local(): pl.pallas_call(functools.partial(middle_kernel, n, C, S, W, push), name='...  200 us
    pallas_call x1, Pallas kernels, local(): pl.pallas_call(functools.partial(last_kernel, n, C, S, W, HD, push), name...  119 us
    pallas_call x1, Pallas kernels, local(): pl.pallas_call(functools.partial(front_kernel, n, C, S, HD, docs), name='...  47.1 us
    unnamed x62, local copies, waits for them, and re-layouts  20.4 us

profile of v2, /device:TPU:0, one launch (start us, length us, event | category | flops | bytes accessed | tf_op | source)
XLA Modules:
  0.0 400.5 jit_solution(9958888083122098985)
XLA Ops:
  0.6 0.7 broadcast_in_dim.22.gain_ref.refs_3_
  1.3 0.0 copy-start.10
  1.3 1.3 broadcast_in_dim.21.refs_2_
  2.6 0.0 copy-start
  2.6 1.0 copy-done
  3.7 0.0 copy-start.1
  3.7 1.2 copy-done.1
  4.9 0.0 copy-start.11
  4.9 0.7 copy-done.11
  5.6 0.0 copy-start.12
  5.6 0.7 copy-done.12
  6.2 0.0 copy-start.13
  6.2 0.7 copy-done.13
  6.9 0.0 copy-start.14
  6.9 0.7 copy-done.14
  7.5 47.1 %front.1 = (bf16[2,256,2048]{2,1,0:T(8,128)(2,1)}, f32[2,256,512]{2,1,0:T(8,128)S(1)}, f32[2,256,256]{2,1,0:T(8,128)S(1)}, bf16[2,256,512]{2,1,0:T(8,128)(2,1)S(...) custom-call(bf16[2,64,2048]{2,1,0:T(8,128)(2,1)S(1)} %bitcast.21, ...), custom_call_target="tpu_custom_call" | custom-call | tf_op jit(solution)/shard_map/front/pallas_call | solution.py:893
  54.7 0.0 copy-done.10
  54.7 0.0 copy-start.2
  54.7 0.8 copy-done.2
  55.5 0.0 copy-start.3
  55.5 1.0 copy-done.3
  56.5 0.8 copy-done.4
  57.2 0.8 copy-done.5
  58.0 0.7 copy-done.6
  58.7 0.7 copy-done.7
  59.4 0.7 copy-done.8
  60.1 0.7 copy-done.9
  60.8 199.7 %middle.1 = (f32[2,64,2048]{2,1,0:T(8,128)}, f32[2,64,2048]{2,1,0:T(8,128)}, f32[1,2048]{1,0:T(1,128)}, bf16[2,256,512]{2,1,0:T(8,128)(2,1)}, bf16[2,256,2048]{2...) custom-call(bf16[2,64,2048]{2,1,0:T(8,128)(2,1)} %bitcast.19, ...), custom_call_target="tpu_custom_call" | custom-call | tf_op jit(solution)/shard_map/middle/pallas_call | solution.py:921
  260.6 119.0 %last.1 = (f32[2,64,2048]{2,1,0:T(8,128)}, f32[2,64,2048]{2,1,0:T(8,128)}, f32[1,2048]{1,0:T(1,128)}, f32[1,2048]{1,0:T(1,128)}, f32[1,128]{1,0:T(1,128)}, /*ind...) custom-call(bf16[2,64,2048]{2,1,0:T(8,128)(2,1)} %bitcast.20, ...), custom_call_target="tpu_custom_call" | custom-call | tf_op jit(solution)/shard_map/last/pallas_call | solution.py:955
  379.5 0.0 copy-start.16
  379.6 1.4 convert_reduce_fusion.4
  381.0 1.1 add_bitcast_fusion.1
  382.1 0.0 copy-start.20
  382.1 1.0 copy.30
  383.1 0.0 copy-done.16
  383.1 0.3 convert_reduce_fusion.3
  383.4 0.1 copy-done.20
  383.5 0.2 add.15
  383.7 0.8 slice.12
  384.5 0.8 fusion
  385.4 0.0 copy-done.15
  385.4 0.4 convert_reduce_fusion
  385.7 1.0 copy-done.19
  386.8 0.2 add_bitcast_fusion
  387.0 1.6 copy.31
  388.6 3.6 convert_reduce_fusion.1
  392.2 0.0 copy-done.18
  392.2 0.0 copy-start.17
  392.2 1.3 add.18
  393.6 0.6 copy-done.17
  394.2 1.3 add.17
  395.6 0.1 copy-done.22
  395.7 0.0 copy-start.23
  395.7 1.0 copy.38
  396.7 0.6 copy-done.21
  397.3 1.0 copy.39
  398.3 0.0 copy-done.24
  398.3 0.6 copy.40
  398.9 0.0 copy-done.26
  398.9 0.5 copy.41
  399.4 0.0 copy-done.25
  399.4 0.5 copy.42
  399.9 0.0 copy-done.23
  399.9 0.6 copy.43
  (14 shorter events, 0.0 us)
Async XLA Ops:
  1.3 53.3 %copy-start.10 = (bf16[1,2048]{1,0:T(2,128)(2,1)}, bf16[1,2048]{1,0:T(2,128)(2,1)S(1)}, u32[]{:S(2)}) copy-start(bf16[1,2048]{1,0:T(2,128)(2,1)S(1)} %broadcast_in_dim.22.gain_ref.refs_3_) | copy-start | bytes 12292
  2.6 1.0 copy-start
  3.7 1.2 copy-start.1
  4.9 0.7 copy-start.11
  5.6 0.7 copy-start.12
  6.2 0.7 copy-start.13
  6.9 0.7 copy-start.14
  54.7 0.8 copy-start.2
  55.5 1.0 copy-start.3
  56.5 0.8 copy-start.4
  57.2 0.8 copy-start.5
  58.0 0.7 copy-start.6
  58.7 0.7 copy-start.7
  59.4 0.7 copy-start.8
  60.1 0.7 copy-start.9
  379.5 3.6 copy-start.16
  382.1 1.4 copy-start.20
  383.5 1.9 copy-start.15
  385.4 1.4 copy-start.19
  388.6 3.6 copy-start.18
  392.2 2.0 copy-start.17
  394.2 1.5 copy-start.22
  395.7 1.6 copy-start.21
  395.7 2.6 copy-start.24
  395.7 3.2 copy-start.26
  395.7 3.7 copy-start.25
  395.7 4.2 %copy-start.23 = (f32[1,2048]{1,0:T(1,128)S(1)}, f32[1,2048]{1,0:T(1,128)}, u32[]{:S(2)}) copy-start(f32[1,2048]{1,0:T(1,128)} %get-tuple-element.74) | copy-start | bytes 24580

commit v3 on v2

v3 whole, which is shorter than its diff:
```python
import functools

import jax
import jax.numpy as jnp
import numpy as np
from jax import lax
from jax.experimental import pallas as pl
from jax.experimental.pallas import tpu as pltpu
from jax.sharding import PartitionSpec as P

MESH = pl.DeviceIdType.MESH
F32 = jnp.float32
BF16 = jnp.bfloat16
norm_eps = 1e-06
masked_score = -1e30
HALVES = 2


def both(*conds):
    out = True
    for cond in conds:
        if isinstance(cond, bool):
            if not cond:
                return False
        else:
            out = cond if out is True else jnp.logical_and(out, cond)
    return out


def when(cond):
    if isinstance(cond, bool):
        return (lambda body: body()) if cond else (lambda body: None)
    return pl.when(cond)


def rows_at(index, rows):
    return pl.ds(pl.multiple_of(index * rows, rows), rows)


def lanes(index, width):
    return pl.ds(pl.multiple_of(index * width, width), width)


def dot(a, b, ca, cb):
    return lax.dot_general(a, b, (((ca,), (cb,)), ((), ())), preferred_element_type=F32)


def remote(src, dst, ssem, rsem, wide, narrow):
    return pltpu.make_async_remote_copy(
        src_ref=src, dst_ref=dst, send_sem=ssem, recv_sem=rsem, device_id=(wide, narrow), device_id_type=MESH
    )


def barrier(n, wide=0):
    w, z = lax.axis_index("wide"), lax.axis_index("narrow")
    bar = pltpu.get_barrier_semaphore()
    for step in range(1, n):
        pl.semaphore_signal(bar, inc=1, device_id=(w, lax.rem(z + step, n)), device_id_type=MESH)
    for step in range(1, wide):
        pl.semaphore_signal(bar, inc=1, device_id=(lax.rem(w + step, wide), z), device_id_type=MESH)
    pl.semaphore_wait(bar, n - 1 + max(wide - 1, 0))


class Line:
    def __init__(self, n, C, S):
        self.n, self.C, self.S = n, C, S
        self.pieces, self.rows = C * HALVES, S // HALVES
        self.w, self.z = lax.axis_index("wide"), lax.axis_index("narrow")

    def at(self, ref, chunk, p):
        start = chunk * self.S + (p % HALVES) * self.rows
        return ref.at[p // HALVES, pl.ds(pl.multiple_of(start, self.rows), self.rows)]


class Gather(Line):
    def __init__(self, n, C, S, full, ssem, rsem):
        super().__init__(n, C, S)
        self.full, self.ssem, self.rsem = full, ssem, rsem

    def copy(self, way, hop, p):
        chunk = self.z - hop if way == 0 else self.z + hop
        where = self.at(self.full, chunk, p)
        z_to = self.z + 1 if way == 0 else self.z - 1
        return remote(where, where, self.ssem.at[way, hop, p], self.rsem.at[way, hop, p], self.w, z_to)

    def arrival(self, way, hop, p):
        chunk = self.z - hop - 1 if way == 0 else self.z + hop + 1
        where = self.at(self.full, chunk, p)
        z_to = self.z + 1 if way == 0 else self.z - 1
        return remote(where, where, self.ssem.at[way, hop, p], self.rsem.at[way, hop, p], self.w, z_to)

    def has(self, way, hop):
        return self.z >= hop if way == 0 else self.z + hop <= self.n - 1

    def can_send(self, way, hop):
        edge = self.z < self.n - 1 if way == 0 else self.z > 0
        return both(self.has(way, hop), edge, hop < self.n - 1)

    def send(self, hop, p, ok=True):
        known = isinstance(hop, int)
        for way in (0, 1):
            if not (known and hop == 0):
                @when(both(ok, hop > 0, self.has(way, hop)))
                def _():
                    self.arrival(way, hop - 1, p).wait_recv()

            if not (known and hop >= self.n - 1):
                @when(both(ok, self.can_send(way, hop)))
                def _():
                    self.copy(way, hop, p).start()

    def drain(self):
        def step(t, carry):
            hop, p = t // self.pieces, t % self.pieces
            for way in (0, 1):
                @when(self.can_send(way, hop))
                def _():
                    self.copy(way, hop, p).wait_send()
            return carry

        lax.fori_loop(0, (self.n - 1) * self.pieces, step, 0)


class Scatter(Line):
    def __init__(self, n, C, S, partial, sbuf, rbuf, ssem, rsem):
        super().__init__(n, C, S)
        self.partial, self.sbuf, self.rbuf, self.ssem, self.rsem = partial, sbuf, rbuf, ssem, rsem

    def copy(self, way, d, p):
        z_to = self.z + 1 - 2 * way
        slot = jnp.where(both(way == 1, d == z_to), self.n, d)
        return remote(
            self.at(self.sbuf, d, p), self.at(self.rbuf, slot, p), self.ssem.at[d, p], self.rsem.at[way, d, p], self.w, z_to
        )

    def slot(self, way, d):
        return jnp.where(both(way == 1, d == self.z), self.n, d)

    def arrived(self, way, d, p):
        where = self.at(self.rbuf, self.slot(way, d), p)
        remote(where, where, self.ssem.at[d, p], self.rsem.at[way, d, p], self.w, self.z).wait_recv()
        return where[...].astype(F32)

    def originate(self, p):
        def step(i, carry):
            way = jnp.where(self.z == 0, 0, 1)
            d = jnp.where(self.z == 0, self.n - 1 - i, i)

            @when(jnp.logical_or(self.z == 0, self.z == self.n - 1))
            def _():
                if self.partial is not self.sbuf:
                    self.at(self.sbuf, d, p)[...] = self.at(self.partial, d, p)[...].astype(BF16)
                self.copy(way, d, p).start()

            return carry

        lax.fori_loop(0, self.n - 1, step, 0)

    def pass_on(self, order, p, ok=True):
        inner = both(ok, self.z > 0, self.z < self.n - 1)

        @when(inner)
        def _():
            def step(i, carry):
                way = jnp.where(self.z < self.n // 2, order, 1 - order)
                d = jnp.where(way == 0, self.n - 1 - i, i)

                @when(jnp.where(way == 0, d > self.z, d < self.z))
                def _():
                    value = self.arrived(way, d, p) + self.at(self.partial, d, p)[...].astype(F32)
                    self.at(self.sbuf, d, p)[...] = value.astype(BF16)
                    self.copy(way, d, p).start()

                return carry

            lax.fori_loop(0, self.n - 1, step, 0)

    def final(self, p, acc):
        acc[...] = self.at(self.partial, self.z, p)[...].astype(F32)
        for way, there in ((0, self.z > 0), (1, self.z < self.n - 1)):
            @when(there)
            def _():
                acc[...] += self.arrived(way, self.z, p)

    def drain(self, lo=0, hi=None):
        hi = self.pieces if hi is None else hi

        def step(t, carry):
            d, p = t // (hi - lo), lo + t % (hi - lo)

            @when(d != self.z)
            def _():
                self.copy(jnp.where(d > self.z, 0, 1), d, p).wait_send()

            return carry

        lax.fori_loop(0, self.n * (hi - lo), step, 0)


def rms_scale(values):
    return lax.rsqrt(jnp.mean(values * values, axis=-1, keepdims=True) + norm_eps)


def rms_back(grad_in, hat, scale_rows):
    return scale_rows * (grad_in - hat * jnp.mean(grad_in * hat, axis=-1, keepdims=True))


def rope(v, cos2, sin2):
    return v * cos2 + pltpu.roll(v, v.shape[-1] // 2, axis=1) * sin2


def chain(k, lo, hi, scat, gath, finish, n):
    def within(p):
        return both(p >= lo, p < hi)

    f = lo + k - 2

    @when(within(f))
    def _():
        finish(f)
        if gath is not None:
            gath.send(0, f)

    scat.pass_on(1, lo + k - 1, within(lo + k - 1))
    scat.pass_on(0, lo + k, within(lo + k))
    if gath is not None:
        for hop in range(1, n):
            gath.send(hop, f - hop, within(f - hop))


class Square:
    def __init__(self, stage, transit, recv, ssem, rsem):
        self.stage, self.transit, self.recv, self.ssem, self.rsem = stage, transit, recv, ssem, rsem
        w = lax.axis_index("wide")
        self.z = lax.axis_index("narrow")
        core, chip = w % 2, w // 2
        self.beside = 2 * (chip + 1 - 2 * (chip % 2)) + core
        self.below = 2 * (chip + 2 - 4 * (chip // 2)) + core
        self.far = 2 * (3 - chip) + core
        self.owners = (self.far, self.beside, self.below)

    def copy(self, m):
        N = self.transit.shape[1]
        h0, h1 = pl.ds(0, N // 2), pl.ds(N // 2, N // 2)
        block, half, there = ((0, h0, 0), (0, h1, 0), (1, h0, 1), (2, h1, 1), (2, h0, 2), (1, h1, 2))[m]
        to = (self.beside, self.below, self.beside, self.below, self.below, self.beside)[m]
        dst = self.transit.at[:, half] if there == 0 else self.recv.at[there - 1, :, half]
        return remote(self.stage.at[block, :, half], dst, self.ssem.at[m], self.rsem.at[m], to, self.z)

    def put(self, block):
        for m in ((0, 1), (2,), (3,))[block]:
            self.copy(m).start()

    def pass_on(self):
        N = self.transit.shape[1]
        for m, block, half in ((0, 2, pl.ds(0, N // 2)), (1, 1, pl.ds(N // 2, N // 2))):
            self.copy(m).wait_recv()
            value = self.stage[block, :, half].astype(F32) + self.transit[:, half].astype(F32)
            self.stage[block, :, half] = value.astype(BF16)
            self.copy(4 + m).start()

    def drain(self):
        for m in range(6):
            self.copy(m).wait_send()
        for m in range(2, 6):
            self.copy(m).wait_recv()


def for_arrived(gath, hop, body):
    z, n = gath.z, gath.n
    if hop == 0:
        body(z)
        return
    left = (z >= hop).astype(jnp.int32)
    right = (z + hop <= n - 1).astype(jnp.int32)

    def step(i, carry):
        use_left = both(left == 1, i == 0)
        body(jnp.where(use_left, z - hop, z + hop))
        return carry

    lax.fori_loop(0, left + right, step, 0)


def row_of(ref):
    return ref[...].astype(F32).reshape(1, ref.shape[0])


def front_kernel(n, C, S, HD, docs,
                 lens_ref, gain_ref, qg_ref, kg_ref, freq_ref, x_hbm, wq_hbm, wk_hbm, wv_hbm,
                 normed_out, q_out, k_out, qrot_out, krot_out, v_out, prob_out, mix_out, cos_out, sin_out,
                 x_ref, normed_ref, q_ref, k_ref, qrot_ref, krot_ref, v_ref, prob_ref, mix_ref, cos_ref, sin_ref,
                 wq, wk, wv, bias, ssem, rsem, wsem, osem):
    R, D = n * S, x_ref.shape[2]
    QC, KC = wq.shape[1], wk.shape[1]
    G = QC // KC
    KH = KC // HD
    loads = [pltpu.make_async_copy(a, b, wsem.at[i]) for i, (a, b) in enumerate(
        ((x_hbm, x_ref), (wq_hbm, wq), (wk_hbm, wk), (wv_hbm, wv)))]
    for load in loads:
        load.start()
    gain, qgain, kgain, freq = [row_of(v) for v in (gain_ref, qg_ref, kg_ref, freq_ref)]
    saved = ((q_ref, q_out), (k_ref, k_out), (qrot_ref, qrot_out), (krot_ref, krot_out), (v_ref, v_out),
             (prob_ref, prob_out), (mix_ref, mix_out), (cos_ref, cos_out), (sin_ref, sin_out), (normed_ref, normed_out))

    def saves(part):
        return [pltpu.make_async_copy(a.at[part], b.at[part], osem.at[i, part]) for i, (a, b) in enumerate(saved)]

    gath = Gather(n, C, S, normed_ref, ssem, rsem)
    z = gath.z
    loads[0].wait()
    for part in range(C):
        x = x_ref[part].astype(F32)
        normed_ref[part, rows_at(z, S)] = (x * rms_scale(x) * gain).astype(BF16)
    barrier(n)
    for p in range(gath.pieces):
        gath.send(0, p)
    for part in range(C):
        t = lax.broadcasted_iota(jnp.int32, (R, HD), 0)
        row = lax.broadcasted_iota(jnp.int32, (R, R), 0)
        col = lax.broadcasted_iota(jnp.int32, (R, R), 1)
        first = jnp.zeros((R, HD), jnp.int32)
        first_wide = jnp.zeros((R, R), jnp.int32)
        end = jnp.int32(0)
        for d in range(docs):
            end = end + lens_ref[part, d]
            first = jnp.where(t >= end, end, first)
            first_wide = jnp.where(row >= end, end, first_wide)
        angle = (t - first).astype(F32) * freq
        sign = jnp.where(lax.broadcasted_iota(jnp.int32, (R, HD), 1) < HD // 2, -1.0, 1.0)
        cos_ref[part] = jnp.cos(angle)
        sin_ref[part] = jnp.sin(angle) * sign
        bias[part] = jnp.where(both(col <= row, col >= first_wide), 0.0, masked_score)
    for load in loads[1:]:
        load.wait()

    def project(chunk, parts):
        rows = rows_at(chunk, S)
        lhs = jnp.concatenate([normed_ref[p, rows] for p in parts], axis=0)
        for w, out in ((wq, q_ref), (wk, k_ref), (wv, v_ref)):
            res = dot(lhs, w[...], 1, 0).astype(out.dtype)
            for i, p in enumerate(parts):
                out[p, rows] = res[i * S:(i + 1) * S]

    def attend(part):
        def heads(k, carry):
            cos2, sin2 = cos_ref[part], sin_ref[part]

            def turned(src, head_gain, col):
                raw = src[part, :, lanes(col, HD)]
                return rope(raw * rms_scale(raw) * head_gain, cos2, sin2).astype(BF16)

            kr = turned(k_ref, kgain, k)
            krot_ref[part, :, lanes(k, HD)] = kr
            for g in range(G):
                qr = turned(q_ref, qgain, k * G + g)
                qrot_ref[part, :, lanes(k * G + g, HD)] = qr
                s = dot(qr, kr, 1, 1) * HD ** (-0.5) + bias[part]
                ex = jnp.exp(s - jnp.max(s, axis=-1, keepdims=True))
                prob = ex / jnp.sum(ex, axis=-1, keepdims=True)
                prob_ref[part, k * G + g] = prob
                mix = dot(prob.astype(BF16), v_ref[part, :, lanes(k, HD)], 1, 0)
                mix_ref[part, :, lanes(k * G + g, HD)] = mix.astype(BF16)
            return carry

        lax.fori_loop(0, KH, heads, 0)

    for hop in range(n - 1):
        if hop > 0:
            for p in range(gath.pieces):
                gath.send(hop, p)
        for_arrived(gath, hop, lambda chunk: project(chunk, tuple(range(C))))
    for part in range(C):
        for h in range(HALVES):
            gath.send(n - 1, part * HALVES + h)
        for_arrived(gath, n - 1, lambda chunk: project(chunk, (part,)))
        attend(part)
        for save in saves(part):
            save.start()
    gath.drain()
    for part in range(C):
        for save in saves(part):
            save.wait()


def weight_block(A, B, sib_a, sib_b, cols):
    total = None
    for part in range(A.shape[0]):
        for term in (dot(A[part, :, cols], B[part], 0, 0), dot(sib_a(part), sib_b[part], 0, 0)):
            total = term if total is None else total + term
    return total


def middle_kernel(n, C, S, W, push, *refs):
    (gain_ref, x_hbm, cot_hbm_in, mix_hbm, wout_hbm, wgate_hbm, wup_hbm, wdown_hbm,
     middle_hbm, dmid_hbm, gaing_ref, dmix_hbm, db_hbm, mlp_hbm, out_hbm) = refs[:15]
    rest = list(refs[15:])
    if push:
        sib_n2, sib_cot, sib_act, sib_dg, sib_du, recv_down, recv_gate, blk_up, own_down, own_gate, own_up = rest[:11]
        rest = rest[11:]
    else:
        n2_hbm, cot_hbm, act_hbm, dg_hbm, du_hbm = rest[:5]
        rest = rest[5:]
    (x_ref, cot_ref, middle_ref, dmid_ref, out_ref, dmix_ref, mixv, wout, wgate, wup, wdown, cotf, n2f, dbf, partial, sbuf, rbuf, sbufm,
     dact, act, dg, du, acc, wsem, cs, cr, s1s, s1r, g2s, g2r, s2s, s2r, g3s, g3r, sms, smr, osem) = rest[:37]
    rest = rest[37:]
    if push:
        (stage_d, stage_g, stage_u, transit_d, transit_g, stage32, cols_sib, b_sib, sib_ss, sib_rs,
         down_ss, down_rs, gate_ss, gate_rs, lsem, ssem32) = rest
    R = n * S
    D = x_ref.shape[2]
    FC = wgate.shape[1]
    TN = 512
    nt, nd = FC // TN, D // TN
    P_ = C * HALVES
    rows = S // HALVES
    w, z = lax.axis_index("wide"), lax.axis_index("narrow")
    loads = [pltpu.make_async_copy(a, b, wsem.at[i]) for i, (a, b) in enumerate(
        ((mix_hbm, mixv), (wout_hbm, wout), (wdown_hbm, wdown), (wgate_hbm, wgate), (wup_hbm, wup), (cot_hbm_in, cot_ref),
         (x_hbm, x_ref)))]
    for index in (5, 0, 1, 6, 2, 3, 4):
        loads[index].start()
    gain = row_of(gain_ref)
    loads[5].wait()
    for part in range(C):
        cotf[part, rows_at(z, S)] = cot_ref[part]
    barrier(n, W if push else 0)
    gc = Gather(n, C, S, cotf, cs, cr)
    g2 = Gather(n, C, S, n2f, g2s, g2r)
    g3 = Gather(n, C, S, dbf, g3s, g3r)
    s1 = Scatter(n, C, S, partial, sbuf, rbuf, s1s, s1r)
    s2 = Scatter(n, C, S, partial, sbuf, rbuf, s2s, s2r)
    sm = Scatter(n, C, S, sbufm, sbufm, rbuf, sms, smr)
    loads[0].wait()
    loads[1].wait()
    loads[6].wait()

    def tiles(count, body):
        def step(j, carry):
            body(j)
            return carry

        lax.fori_loop(0, count, step, 0)

    for part in range(C):
        def out_tile(j):
            partial[part, :, lanes(j, TN)] = dot(mixv[part], wout[:, lanes(j, TN)], 1, 0)

        tiles(nd, out_tile)
        if part == 0:
            for p in range(2):
                s1.originate(p)
                gc.send(0, p)

    def mid_row(p):
        return p // HALVES, rows_at(p % HALVES, rows)

    def after_attention(p):
        s1.final(p, acc)
        part, rr = mid_row(p)
        middle = x_ref[part, rr].astype(F32) + acc[...]
        middle_ref[part, rr] = middle
        g2.at(n2f, z, p)[...] = (middle * rms_scale(middle) * gain).astype(BF16)

    def phase_one(k):
        @when(k + 2 < P_)
        def _():
            s1.originate(k + 2)
            gc.send(0, k + 2)

        chain(k, 0, P_, s1, g2, after_attention, n)
        for hop in range(1, n):
            gc.send(hop, k + 1 - hop, both(k + 1 - hop >= 0, k + 1 - hop < P_))

    def dact_tile(part, j):
        dact[:, lanes(j, TN)] = dot(cotf[part], wdown[rows_at(j, TN), :], 1, 1)

    first_in = HALVES + n + 1
    ready = HALVES + n - 3

    def early(k):
        phase_one(k)

        @when(k == ready - 1)
        def _():
            loads[2].wait()

        @when(both(k >= ready, k < ready + nt))
        def _():
            dact_tile(0, k - ready)

    tiles(first_in, early)
    for j in range(max(first_in - ready, 0), nt):
        dact_tile(0, j)
    loads[3].wait()
    loads[4].wait()
    late = P_ + n + 1 - first_in
    if push:
        core = w % 2
        mate = w + 1 - 2 * core

        def swap(index, src, dst, part):
            return remote(src.at[part], dst.at[part], sib_ss.at[index, part], sib_rs.at[index, part], mate, z)

    def after_feed(p):
        s2.final(p, acc)
        part, rr = mid_row(p)
        dn2 = acc[...]
        middle = middle_ref[part, rr]
        scale = rms_scale(middle)
        hat = middle * scale
        gaing_ref[...] += jnp.sum(dn2 * hat, axis=0, keepdims=True)
        dmid = cot_ref[part, rr].astype(F32) + rms_back(dn2 * gain, hat, scale)
        dmid_ref[part, rr] = dmid
        g3.at(dbf, z, p)[...] = dmid.astype(BF16)

    gaing_ref[...] = jnp.zeros_like(gaing_ref)
    steps = HALVES + n + 1

    def feed(part):
        def service(e):
            @when(both(part == 0, e % 2 == 1, e // 2 < late))
            def _():
                phase_one(first_in + e // 2)

            @when(both(part > 0, e < steps))
            def _():
                chain(e, 0, HALVES, s2, g3, after_feed, n)

        def gate_tile(j):
            @when(part > 0)
            def _():
                dact_tile(part, j)

            at = lanes(j, TN)
            gate = dot(n2f[part], wgate[:, at], 1, 0)
            up = dot(n2f[part], wup[:, at], 1, 0)
            sig = jax.nn.sigmoid(gate)
            silu = gate * sig
            d_act = dact[:, at]
            act[part, :, at] = (silu * up).astype(BF16)
            dg[part, :, at] = (d_act * up * sig * (1.0 + gate * (1.0 - sig))).astype(BF16)
            du[part, :, at] = (d_act * silu).astype(BF16)
            service(j)

        tiles(nt, gate_tile)
        if push:
            for index, (a, b) in enumerate(((n2f, sib_n2), (cotf, sib_cot), (act, sib_act), (dg, sib_dg), (du, sib_du))):
                swap(index, a, b, part).start()

        def back_tile(j):
            at = rows_at(j, TN)
            partial[part, :, lanes(j, TN)] = dot(dg[part], wgate[at, :], 1, 1) + dot(du[part], wup[at, :], 1, 1)
            service(nt + j)

        tiles(nd, back_tile)
        tiles(max(steps, 2 * late) - nt - nd, lambda e: service(nt + nd + e))

        @when(part == 0)
        def _():
            s1.drain()

        for h in range(HALVES):
            s2.originate(part * HALVES + h)

    tiles(C, feed)

    def tail(k):
        chain(k, HALVES, P_, s2, g3, after_feed, n)

    def mlp_sums(part):
        for j in range(nd):
            sbufm[part, :, lanes(j, TN)] = dot(act[part], wdown[:, lanes(j, TN)], 1, 0).astype(BF16)

    def mlp_step(k):
        chain(k, 0, HALVES, sm, None, mlp_done, n)

    def mlp_done(p):
        sm.final(p, acc)
        part, rr = mid_row(p)
        out_ref[part, rr] = middle_ref[part, rr] + acc[...]

    mlp_begun = 2

    def mlp_start():
        mlp_sums(0)
        for h in range(HALVES):
            sm.originate(h)

    def mix_back(part):
        dmix_ref[part] = dot(dbf[part], wout[...], 1, 1).astype(BF16)

    if push:
        width = D // W
        down = Square(stage_d, transit_d, recv_down, down_ss, down_rs)
        gate = Square(stage_g, transit_g, recv_gate, gate_ss, gate_rs)
        owners = down.owners

        def fetch(cols, b):
            copies = []
            if cols is not None:
                for q, owner in enumerate(owners + (w,)):
                    for part in range(C):
                        copies.append(pltpu.make_async_copy(
                            cols.at[part, :, lanes(owner, width)], cols_sib.at[q, part], lsem.at[0, q, part]))
            for part in range(C):
                copies.append(pltpu.make_async_copy(b.at[part], b_sib.at[part], lsem.at[1, 0, part]))
            for copy in copies:
                copy.start()
            for copy in copies:
                copy.wait()

        def block(A, B, q):
            return weight_block(A, B, lambda part: cols_sib[q, part], b_sib, lanes((owners + (w,))[q], width))

        def own_copy(dst, index):
            return pltpu.make_async_copy(stage32, dst, ssem32.at[index])

        def up_copy(q):
            return pltpu.make_async_copy(stage_u.at[q % 2], blk_up.at[q], osem.at[6 + q])

        def arrive(*pairs):
            for part in range(C):
                for index, dst in pairs:
                    swap(index, dst, dst, part).wait_recv()

        def down_block(q):
            if q == 0:
                arrive((1, sib_cot), (2, sib_act))
                fetch(sib_cot, sib_act)
            if q < 3:
                stage_d[q] = block(cotf, act, q).astype(BF16)
                down.put(q)
            else:
                stage32[...] = block(cotf, act, q)
                own_copy(own_down, 0).start()

        def gate_block(q):
            if q == 0:
                arrive((0, sib_n2), (3, sib_dg))
                fetch(sib_n2, sib_dg)
            if q < 3:
                stage_g[q] = block(n2f, dg, q).astype(BF16)
                gate.put(q)
            else:
                own_copy(own_down, 0).wait()
                stage32[...] = block(n2f, dg, q)
                own_copy(own_gate, 1).start()

        def up_block(q):
            if q == 0:
                arrive((4, sib_du))
                fetch(None, sib_du)
            if q < 3:
                if q == 2:
                    up_copy(0).wait()
                stage_u[q % 2] = block(n2f, du, q).astype(BF16)
                up_copy(q).start()
            else:
                own_copy(own_gate, 1).wait()
                stage32[...] = block(n2f, du, q)
                own_copy(own_up, 2).start()

        work = [[(down_block, 0), (down_block, 1)], [(down_block, 2), (down_block, 3)],
                [(gate_block, 0), (gate_block, 1)], [(gate_block, 2), (down.pass_on,)],
                [(gate_block, 3), (up_block, 0), (up_block, 1)], [(up_block, 2), (up_block, 3)],
                [(gate.pass_on,), (mlp_sums, 1), (mix_back, 0)]]
    else:
        outs = [pltpu.make_async_copy(a, b, osem.at[6 + i]) for i, (a, b) in enumerate(
            ((n2f, n2_hbm), (cotf, cot_hbm), (act, act_hbm), (dg, dg_hbm), (du, du_hbm)))]
        for out in outs:
            out.start()
        work = [[] for _ in range(steps - 1)] + [[(mlp_sums, 1), (mix_back, 0)]]
    work += [[]] * (steps - len(work))
    for k in range(steps):
        if k == mlp_begun - 1:
            mlp_start()
        tail(k)
        if k >= mlp_begun:
            mlp_step(k - mlp_begun)
        for piece in work[k]:
            piece[0](*piece[1:])
    for k in range(steps - mlp_begun, HALVES + 2):
        mlp_step(k)
    ends = [pltpu.make_async_copy(a, b, osem.at[i]) for i, (a, b) in enumerate(
        ((sbufm, mlp_hbm), (dbf, db_hbm), (middle_ref, middle_hbm), (dmid_ref, dmid_hbm), (out_ref, out_hbm), (dmix_ref, dmix_hbm)))]
    for end in ends[:5]:
        end.start()
    for part in range(1, C):
        mix_back(part)
    ends[5].start()
    gc.drain()
    g2.drain()
    g3.drain()
    s2.drain()
    sm.drain(0, HALVES)
    for end in ends:
        end.wait()
    if push:
        for part in range(C):
            for index, (a, b) in enumerate(((n2f, sib_n2), (cotf, sib_cot), (act, sib_act), (dg, sib_dg), (du, sib_du))):
                swap(index, a, b, part).wait_send()
        for q in (1, 2):
            up_copy(q).wait()
        own_copy(own_up, 2).wait()
        down.drain()
        gate.drain()
    else:
        for out in outs:
            out.wait()


def last_kernel(n, C, S, W, HD, push, *refs):
    gain_ref, qg_ref, kg_ref, gmlp_ref = refs[:4]
    sources = refs[4:20]
    rest = list(refs[20:])
    if push:
        mix_hbm, db_hbm, normed_hbm, blk_up = rest[:4]
        rest = rest[4:]
    out_hbm, in_hbm, ga_ref, gm_ref, gq_ref, gk_ref = rest[:6]
    rest = rest[6:]
    if push:
        recv_up, recv_out, recv_qkv, own_out, own_qkv = rest[:5]
        rest = rest[5:]
    else:
        dproj_hbm = rest[0]
        rest = rest[1:]
    held = rest[:18]
    (sbufm, q_ref, k_ref, qrot_ref, krot_ref, v_ref, prob_ref, cos_ref, sin_ref, dmix_ref, wq, wk, wv,
     middle_ref, dmid_ref, x_ref) = held[:16]
    out_ref, in_ref = held[16:18]
    rest = rest[18:]
    (dproj, partial, sbuf, rbuf, rbufm, acc, gains, small, small_two,
     lsem, s3s, s3r, sms, smr, gs1, gr1, gs2, gr2, osem) = rest[:19]
    rest = rest[19:]
    if push:
        (mixv, dbv, normv, sib_mix, sib_db, sib_norm, sib_dproj, sib_ss, sib_rs) = rest[:9]
        squares = rest[9:]
    R, D = n * S, x_ref.shape[2]
    QC, KC = wq.shape[1], wk.shape[1]
    G, KH = QC // KC, KC // HD
    TN = 512
    nd = D // TN
    P_ = C * HALVES
    rows = S // HALVES
    w, z = lax.axis_index("wide"), lax.axis_index("narrow")
    loads = [pltpu.make_async_copy(a, b, lsem.at[i]) for i, (a, b) in enumerate(zip(sources, held[:16]))]
    for load in loads:
        load.start()
    if push:
        extra = [pltpu.make_async_copy(a, b, lsem.at[16 + i]) for i, (a, b) in enumerate(
            ((mix_hbm, mixv), (db_hbm, dbv), (normed_hbm, normv)))]
        for load in extra:
            load.start()
    barrier(n, W)
    sm = Scatter(n, C, S, sbufm, sbufm, rbufm, sms, smr)
    s3 = Scatter(n, C, S, partial, sbuf, rbuf, s3s, s3r)
    if push:
        core = w % 2
        mate = w + 1 - 2 * core
        width = D // W
        up_sums, out_sums, qkv_sums = [
            Square(squares[i], squares[i + 1], recv, squares[i + 2], squares[i + 3])
            for i, recv in ((0, recv_up), (4, recv_out), (8, recv_qkv))]
        stage_up, stage_out, stage_qkv = squares[0], squares[4], squares[8]
        blocks = [pltpu.make_async_copy(blk_up.at[q], stage_up.at[q], lsem.at[19 + q]) for q in range(3)]
        for q in range(3):
            blocks[q].start()

        def swap(index, src, dst, part):
            return remote(src.at[part], dst.at[part], sib_ss.at[index, part], sib_rs.at[index, part], mate, z)

    loads[0].wait()
    for p in range(HALVES, P_):
        sm.originate(p)
    if push:
        for q in range(3):
            blocks[q].wait()
            up_sums.put(q)
        for load in extra:
            load.wait()
        for part in range(C):
            for index, (a, b) in enumerate(((mixv, sib_mix), (dbv, sib_db), (normv, sib_norm))):
                swap(index, a, b, part).start()

    def piece_row(p):
        return p // HALVES, rows_at(p % HALVES, rows)

    def mlp_done(p):
        sm.final(p, acc)
        part, rr = piece_row(p)
        out_ref[0, rr] = middle_ref[part, rr] + acc[...]

    gain, qgain, kgain = [row_of(v) for v in (gain_ref, qg_ref, kg_ref)]

    def grad_done(p):
        s3.final(p, acc)
        part, rr = piece_row(p)
        dn = acc[...]
        x = x_ref[part, rr].astype(F32)
        scale = rms_scale(x)
        hat = x * scale
        gains[0:1, :] += jnp.sum(dn * hat, axis=0, keepdims=True)
        in_ref[part, rr] = dmid_ref[part, rr] + rms_back(dn * gain, hat, scale)

    gains[...] = jnp.zeros_like(gains)
    scale = HD ** (-0.5)
    for load in loads[1:]:
        load.wait()

    def unit(part, k):
        cos2, sin2 = cos_ref[part], sin_ref[part]
        kr, vr = krot_ref[part, :, lanes(k, HD)], v_ref[part, :, lanes(k, HD)]

        def unturned(grad, raw, head_gain, at):
            d_n = grad * cos2 - pltpu.roll(grad, HD // 2, axis=1) * sin2
            r = rms_scale(raw)
            hat = raw * r
            gains[at:at + 1, :HD] += jnp.sum(d_n * hat, axis=0, keepdims=True)
            return rms_back(d_n * head_gain, hat, r).astype(BF16)

        dk, dv = None, None
        for g in range(G):
            h = k * G + g
            pr = prob_ref[part, h]
            dm = dmix_ref[part, :, lanes(h, HD)]
            dp = dot(dm, vr, 1, 1)
            one = dot(pr.astype(BF16), dm, 0, 0)
            dv = one if dv is None else dv + one
            ds = (pr * (dp - jnp.sum(pr * dp, axis=-1, keepdims=True))).astype(BF16)
            one = dot(ds, qrot_ref[part, :, lanes(h, HD)], 0, 0)
            dk = one if dk is None else dk + one
            dq = dot(ds, kr, 1, 0) * scale
            dproj[part, :, lanes(h, HD)] = unturned(dq, q_ref[part, :, lanes(h, HD)], qgain, 1)
        dproj[part, :, lanes(QC // HD + k, HD)] = unturned(dk * scale, k_ref[part, :, lanes(k, HD)], kgain, 2)
        dproj[part, :, lanes(QC // HD + KH + k, HD)] = dv.astype(BF16)

    per_part = KH + 1

    def between(e):
        chain(e, HALVES, P_, sm, None, mlp_done, n)
        chain(e - per_part, 0, HALVES, s3, None, grad_done, n)
        if push:
            @when(e == per_part)
            def _():
                up_sums.pass_on()

    def backward(part):
        def heads(k, carry):
            unit(part, k)
            between(part * per_part + k)
            return carry

        lax.fori_loop(0, KH, heads, 0)
        if push:
            swap(3, dproj, sib_dproj, part).start()

        def back_tile(j, carry):
            at = rows_at(j, TN)
            partial[part, :, lanes(j, TN)] = (
                dot(dproj[part, :, 0:QC], wq[at, :], 1, 1) + dot(dproj[part, :, QC:QC + KC], wk[at, :], 1, 1)
                + dot(dproj[part, :, QC + KC:QC + 2 * KC], wv[at, :], 1, 1))
            return carry

        lax.fori_loop(0, nd, back_tile, 0)
        for h in range(HALVES):
            s3.originate(part * HALVES + h)
        between(part * per_part + KH)

    def both_parts(part, carry):
        backward(part)
        return carry

    lax.fori_loop(0, C, both_parts, 0)
    done = C * per_part
    for e in range(done, max(HALVES + 2, per_part + HALVES + 2)):
        between(e)
    steps = HALVES + 2
    if push:
        def block(A, B, sib_a, sib_b, owner):
            cols = lanes(owner, width)
            return weight_block(A, B, lambda part: sib_a[part, :, cols], sib_b, cols)

        def out_block(q):
            if q == 0:
                for part in range(C):
                    for index, (a, b) in enumerate(((mixv, sib_mix), (dbv, sib_db), (normv, sib_norm), (dproj, sib_dproj))):
                        swap(index, a, b, part).wait_recv()
            if q < 3:
                stage_out[q] = block(dbv, mixv, sib_db, sib_mix, out_sums.owners[q]).astype(BF16)
                out_sums.put(q)
            else:
                own_out[...] = block(dbv, mixv, sib_db, sib_mix, w)

        def qkv_block(q):
            if q < 3:
                stage_qkv[q] = block(normv, dproj, sib_norm, sib_dproj, qkv_sums.owners[q]).astype(BF16)
                qkv_sums.put(q)
            else:
                own_qkv[...] = block(normv, dproj, sib_norm, sib_dproj, w)

        work = [[(out_block, 0), (qkv_block, 0)], [(qkv_block, 1), (qkv_block, 2)], [(out_block, 1), (out_block, 2)],
                [(qkv_block, 3), (out_block, 3), (qkv_sums.pass_on,), (out_sums.pass_on,)]]
        assert len(work) == steps
    else:
        work = [[]] * steps
    for k in range(steps):
        chain(k, HALVES, P_, s3, None, grad_done, n)
        for piece in work[k]:
            piece[0](*piece[1:])
    if not push:
        out = pltpu.make_async_copy(dproj, dproj_hbm, lsem.at[16])
        out.start()
    ends = [pltpu.make_async_copy(a, b, osem.at[i]) for i, (a, b) in enumerate(((out_ref, out_hbm), (in_ref, in_hbm)))]
    for end in ends:
        end.start()
    L = 2 * D + 2 * HD
    small[w, :, 0:D] = gains[0:1, :]
    small[w, :, D:2 * D] = gmlp_ref[...]
    small[w, :, 2 * D:2 * D + HD] = gains[1:2, :HD]
    small[w, :, 2 * D + HD:L] = gains[2:3, :HD]

    def to_wide(s):
        return remote(small.at[w], small.at[w], gs1.at[s], gr1.at[s], lax.rem(w + s, W), z)

    def to_narrow(s):
        return remote(small_two.at[z], small_two.at[z], gs2.at[s], gr2.at[s], w, lax.rem(z + s, n))

    for s in range(1, W):
        to_wide(s).start()
    for s in range(1, W):
        to_wide(s).wait_recv()
    total = small[0]
    for s in range(1, W):
        total = total + small[s]
    small_two[z] = total
    for s in range(1, n):
        to_narrow(s).start()
    for s in range(1, n):
        to_narrow(s).wait_recv()
    total = small_two[0]
    for s in range(1, n):
        total = total + small_two[s]
    for ref, lo, hi in ((ga_ref, 0, D), (gm_ref, D, 2 * D), (gq_ref, 2 * D, 2 * D + HD), (gk_ref, 2 * D + HD, L)):
        ref[...] = total[:, lo:hi].reshape(hi - lo)
    for s in range(1, W):
        to_wide(s).wait_send()
    for s in range(1, n):
        to_narrow(s).wait_send()
    sm.drain(HALVES, P_)
    s3.drain()
    for end in ends:
        end.wait()
    if push:
        for part in range(C):
            for index, (a, b) in enumerate(((mixv, sib_mix), (dbv, sib_db), (normv, sib_norm), (dproj, sib_dproj))):
                swap(index, a, b, part).wait_send()
        for sums in (up_sums, out_sums, qkv_sums):
            sums.drain()
    else:
        out.wait()


def finish_kernel(*refs):
    own_down, recv_down, own_out, recv_out, own_gate, recv_gate, own_up, recv_up, own_qkv, recv_qkv = refs[:10]
    low, high = refs[10:12]
    passed = refs[12:17]
    down, out_g, gate, up, g_q, g_k, g_v, out_ref = refs[17:25]
    out_ref[0], out_ref[1] = low[0], high[0]

    def total(own, parts):
        value = own[...]
        for i in range(parts.shape[0]):
            value = value + parts[i].astype(F32)
        return value

    down[...] = total(own_down, recv_down).T
    out_g[...] = total(own_out, recv_out).T
    gate[...] = total(own_gate, recv_gate)
    up[...] = total(own_up, recv_up)
    qkv = total(own_qkv, recv_qkv)
    first, second = g_q.shape[1], g_q.shape[1] + g_k.shape[1]
    g_q[...], g_k[...], g_v[...] = qkv[:, :first], qkv[:, first:second], qkv[:, second:]
    for a, b in zip(passed, refs[25:]):
        b[...] = a[...]


def local(W, layer_input, document_lengths, attn_gain, w_query, w_key, w_value, query_gain, key_gain, w_out, mlp_gain,
          w_gate, w_up, w_down, output_cotangent):
    n = lax.axis_size("narrow")
    C, _, S, D = layer_input.shape
    R = n * S
    T = C * R
    HD = query_gain.shape[0]
    QC, KC = w_query.shape[1], w_key.shape[1]
    QH = QC // HD
    FC = w_gate.shape[1]
    docs = document_lengths.shape[2]
    P_ = C * HALVES
    grid = 4
    push = (W == 8 and (D // W) % 128 == 0 and FC % (128 * grid) == 0 and QC % (128 * grid) == 0
            and S % (8 * grid) == 0)
    assert C == 2
    width = D // W
    x_own, cot_own = layer_input[:, 0], output_cotangent[:, 0]
    sds = jax.ShapeDtypeStruct
    dma = pltpu.SemaphoreType.DMA
    gsem = lambda: dma((2, n - 1, P_))
    half = np.arange(HD) % (HD // 2)
    freq = jnp.asarray(np.power(np.float32(1000000.0), np.float32(-2.0) * half.astype(np.float32) / np.float32(HD)), F32)
    vm = pl.BlockSpec(memory_space=pltpu.VMEM)
    hbm = pl.BlockSpec(memory_space=pl.ANY)
    smem = pl.BlockSpec(memory_space=pltpu.SMEM)
    VM = pltpu.VMEM

    shapes = [((C, R, D), BF16), ((C, R, QC), F32), ((C, R, KC), F32), ((C, R, QC), BF16), ((C, R, KC), BF16),
              ((C, R, KC), BF16), ((C, QH, R, R), F32), ((C, R, QC), BF16), ((C, R, HD), F32), ((C, R, HD), F32)]
    normed_full, q_raw, k_raw, q_rot, k_rot, v_rows, prob, mix, cos2, sin2 = pl.pallas_call(
        functools.partial(front_kernel, n, C, S, HD, docs), name="front",
        out_shape=[sds(*one) for one in shapes], in_specs=[smem, vm, vm, vm, vm, hbm, hbm, hbm, hbm], out_specs=[hbm] * 10,
        scratch_shapes=[VM((C, S, D), BF16)] + [VM(*one) for one in shapes]
        + [VM(w_query.shape, BF16), VM(w_key.shape, BF16), VM(w_value.shape, BF16),
           VM((C, R, R), F32), gsem(), gsem(), dma((4,)), dma((10, C))],
        compiler_params=pltpu.CompilerParams(collective_id=0, has_side_effects=True, vmem_limit_bytes=56 << 20),
    )(document_lengths[:, 0], attn_gain, query_gain, key_gain, freq, x_own, w_query, w_key, w_value)

    full, wide_rows = sds((C, R, D), BF16), sds((C, R, FC), BF16)
    outs = [sds((C, S, D), F32), sds((C, S, D), F32), sds((1, D), F32), sds((C, R, QC), BF16), full, full, sds((1, S, D), F32)]
    specs = [hbm, hbm, vm, hbm, hbm, hbm, hbm]
    line = lambda: [VM((C, R, D), BF16), VM((C, R + S, D), BF16)]
    scratch = (
        [VM((C, S, D), BF16), VM((C, S, D), BF16), VM((C, S, D), F32), VM((C, S, D), F32), VM((1, S, D), F32), VM((C, R, QC), BF16)]
        + [VM((C, R, QC), BF16), VM(w_out.shape, BF16), VM(w_gate.shape, BF16), VM(w_up.shape, BF16), VM(w_down.shape, BF16)]
        + [VM((C, R, D), BF16)] * 3 + [VM((C, R, D), F32)] + line()
        + [VM((C, R, D), BF16), VM((R, FC), F32)] + [VM((C, R, FC), BF16)] * 3 + [VM((S // HALVES, D), F32)]
        + [dma((7,)), gsem(), gsem(), dma((n, P_)), dma((2, n, P_)), gsem(), gsem(), dma((n, P_)), dma((2, n, P_)),
           gsem(), gsem(), dma((n, P_)), dma((2, n, P_)), dma((11,))]
    )
    if push:
        sums, own = sds((2, width, FC), BF16), sds((width, FC), F32)
        outs += [full, full, wide_rows, wide_rows, wide_rows, sums, sums, sds((3, width, FC), BF16), own, own, own]
        scratch += [VM((3, width, FC), BF16), VM((3, width, FC), BF16), VM((2, width, FC), BF16), VM((width, FC), BF16),
                    VM((width, FC), BF16), VM((width, FC), F32), VM((4, C, R, width), BF16), VM((C, R, FC), BF16),
                    dma((5, C)), dma((5, C)), dma((6,)), dma((6,)), dma((6,)), dma((6,)), dma((2, 4, C)), dma((3,))]
    else:
        outs += [full, full, wide_rows, wide_rows, wide_rows]
    res = pl.pallas_call(
        functools.partial(middle_kernel, n, C, S, W, push), name="middle", out_shape=outs,
        in_specs=[vm] + [hbm] * 7, out_specs=specs + [hbm] * (len(outs) - len(specs)), scratch_shapes=scratch,
        compiler_params=pltpu.CompilerParams(collective_id=1, has_side_effects=True, vmem_limit_bytes=63 << 20),
    )(mlp_gain, x_own, cot_own, mix, w_out, w_gate, w_up, w_down)
    middle, d_middle, gmlp, d_mix, db_full, mlp_sums, out_low = res[:7]

    args = [attn_gain, query_gain, key_gain, gmlp, mlp_sums, q_raw, k_raw, q_rot, k_rot, v_rows, prob, cos2, sin2, d_mix, w_query, w_key, w_value,
            middle, d_middle, x_own]
    in_specs = [vm] * 4 + [hbm] * 16
    held = [VM(v.shape, v.dtype) for v in args[4:]] + [VM((1, S, D), F32), VM((C, S, D), F32)]
    own_rows = sds((C, S, D), F32)
    outs = [sds((1, S, D), F32), own_rows, sds((D,), F32), sds((D,), F32), sds((HD,), F32), sds((HD,), F32)]
    specs = [hbm] * 2 + [vm] * 4
    PC = QC + 2 * KC
    L = 2 * D + 2 * HD
    scratch = (
        held + [VM((C, R, PC), BF16), VM((C, R, D), F32)]
        + line() + line()[1:] + [VM((S // HALVES, D), F32), VM((8, D), F32), VM((W, 1, L), F32), VM((n, 1, L), F32)]
        + [dma((22,)), dma((n, P_)), dma((2, n, P_)), dma((n, P_)), dma((2, n, P_)), dma((W,)), dma((W,)), dma((n,)), dma((n,)),
           dma((2,))]
    )
    if push:
        sib_n2, sib_cot, sib_act, sib_dg, sib_du, recv_down, recv_gate, blk_up, own_down, own_gate, own_up = res[7:]
        args += [mix, db_full, normed_full, blk_up]
        in_specs += [hbm] * 4
        outs += [sds((2, width, FC), BF16)] + [sds((2, width, QC), BF16), sds((2, width, PC), BF16),
                                                       sds((width, QC), F32), sds((width, PC), F32)]
        specs += [hbm] * 3 + [vm] * 2
        scratch += [VM((C, R, QC), BF16), VM((C, R, D), BF16), VM((C, R, D), BF16)]
        scratch += [VM((C, R, QC), BF16), VM((C, R, D), BF16), VM((C, R, D), BF16), VM((C, R, PC), BF16)]
        scratch += [dma((4, C)), dma((4, C))]
        for cols in (FC, QC, PC):
            scratch += [VM((3, width, cols), BF16), VM((width, cols), BF16), dma((6,)), dma((6,))]
    else:
        outs += [sds((C, R, PC), BF16)]
        specs += [hbm]
    last = pl.pallas_call(
        functools.partial(last_kernel, n, C, S, W, HD, push), name="last", out_shape=outs, in_specs=in_specs, out_specs=specs,
        scratch_shapes=scratch,
        compiler_params=pltpu.CompilerParams(collective_id=2, has_side_effects=True, vmem_limit_bytes=60 << 20),
    )(*args)
    out_high, in_own, g_attn, g_mlp, g_query, g_key = last[:6]
    if push:
        recv_up, recv_out, recv_qkv, own_out, own_qkv = last[6:]

        def by_rows(rows, cols, lead=None):
            if lead is None:
                return pl.BlockSpec((rows // grid, cols), lambda i: (i, 0))
            return pl.BlockSpec((lead, rows // grid, cols), lambda i: (0, i, 0))

        def by_cols(rows, cols, lead=None):
            if lead is None:
                return pl.BlockSpec((rows, cols // grid), lambda i: (0, i))
            return pl.BlockSpec((lead, rows, cols // grid), lambda i: (0, 0, i))

        def shard(parts):
            return pl.BlockSpec((parts, S // grid, D), lambda i: (0, i, 0))

        same = [shard(C)] + [pl.BlockSpec(v.shape, lambda i: (0,)) for v in last[2:6]]
        down, out_g, gate, up, g_q, g_k, g_v, out_own, in_own, g_attn, g_mlp, g_query, g_key = pl.pallas_call(
            finish_kernel, name="finish", grid=(grid,),
            out_shape=[sds((FC, width), F32), sds((QC, width), F32), sds((width, FC), F32), sds((width, FC), F32),
                       sds((width, QC), F32), sds((width, KC), F32), sds((width, KC), F32)]
            + [own_rows] + [sds(v.shape, v.dtype) for v in last[1:6]],
            in_specs=[by_cols(width, FC), by_cols(width, FC, 2), by_cols(width, QC), by_cols(width, QC, 2),
                      by_rows(width, FC), by_rows(width, FC, 2), by_rows(width, FC), by_rows(width, FC, 2),
                      by_rows(width, PC), by_rows(width, PC, 2), shard(1), shard(1)] + same,
            out_specs=[by_rows(FC, width), by_rows(QC, width), by_rows(width, FC), by_rows(width, FC), by_rows(width, QC),
                       by_rows(width, KC), by_rows(width, KC), shard(C)] + same,
            compiler_params=pltpu.CompilerParams(vmem_limit_bytes=62 << 20),
        )(own_down, recv_down, own_out, recv_out, own_gate, recv_gate, own_up, recv_up, own_qkv, recv_qkv, out_low, *last[:6])
        projections = (g_q, g_k, g_v)
    else:
        n2, cot, act, dg, du = [v.reshape(T, -1) for v in res[7:]]
        d_proj = last[6].reshape(T, PC)
        db, mixed, normed = db_full.reshape(T, D), mix.reshape(T, QC), normed_full.reshape(T, D)

        def scatter(a, b, dim):
            return lax.psum_scatter(dot(a, b, 0, 0).astype(BF16), "wide", scatter_dimension=dim, tiled=True).astype(F32)

        down, gate, up = scatter(act, cot, 1), scatter(n2, dg, 0), scatter(n2, du, 0)
        out_g, qkv = scatter(mixed, db, 1), scatter(normed, d_proj, 0)
        out_own = jnp.concatenate([out_low, out_high], axis=0)
        projections = (qkv[:, :QC], qkv[:, QC:QC + KC], qkv[:, QC + KC:])
    return (
        out_own[:, None], in_own[:, None], g_attn, *projections,
        g_query, g_key, out_g, g_mlp, gate, up, down,
    )


def solution(mesh):
    rows = P(None, "wide", "narrow", None)
    cols, tall = P(None, "narrow"), P("narrow", None)
    in_specs = (rows, P(None, "wide", None), P(), cols, cols, cols, P(), P(), tall, P(), cols, cols, tall, rows)
    both_ways, turned = P("wide", "narrow"), P("narrow", "wide")
    out_specs = (rows, rows, P(), both_ways, both_ways, both_ways, P(), P(), turned, P(), both_ways, both_ways, turned)
    body = functools.partial(local, mesh.shape["wide"])
    return jax.shard_map(body, mesh=mesh, in_specs=in_specs, out_specs=out_specs, check_vma=False)
```

time: 401 us -> 334 us (0.83)
  Pallas kernels: 366 us -> 333 us
  local copies, waits for them, and re-layouts: 24.1 us -> 0 us
  other arithmetic: 9.86 us -> 0 us
    pallas_call x1, Pallas kernels: 119 us -> 80.8 us  [local(): pl.pallas_call(functools.partial(last_kernel, n, C, S, W, HD, push), name...]
    unnamed x62 -> x0, local copies, waits for them, and re-layouts: 20.4 us -> none
    pallas_call x0 -> x1, Pallas kernels: none -> 8.54 us  [local(): pl.pallas_call(finish_kernel, name='finish', grid=(grid,), out_shape=[sds...]
    reduce_sum x4 -> x0, other arithmetic: 5.7 us -> none  [gathered(): return own + jnp.sum(parts.astype(F32), axis=0)]
    pallas_call x1, Pallas kernels: 200 us -> 196 us  [local(): pl.pallas_call(functools.partial(middle_kernel, n, C, S, W, push), name='...]
where the time goes in v3:
time: 334 us
  Pallas kernels  333 us (100%)
    pallas_call x1, Pallas kernels, local(): pl.pallas_call(functools.partial(middle_kernel, n, C, S, W, push), name='...  196 us
    pallas_call x1, Pallas kernels, local(): pl.pallas_call(functools.partial(last_kernel, n, C, S, W, HD, push), name...  80.8 us
    pallas_call x1, Pallas kernels, local(): pl.pallas_call(functools.partial(front_kernel, n, C, S, HD, docs), name='...  47.9 us
    pallas_call x1, Pallas kernels, local(): pl.pallas_call(finish_kernel, name='finish', grid=(grid,), out_shape=[sds...  8.54 us

profile of v3, /device:TPU:0, one launch (start us, length us, event | category | flops | bytes accessed | tf_op | source)
XLA Modules:
  0.0 333.7 jit_solution(16298672388918864487)
XLA Ops:
  0.6 47.9 %front.1 = (bf16[2,256,2048]{2,1,0:T(8,128)(2,1)}, f32[2,256,512]{2,1,0:T(8,128)}, f32[2,256,256]{2,1,0:T(8,128)}, bf16[2,256,512]{2,1,0:T(8,128)(2,1)}, bf16[2,...) custom-call(s32[2,4]{1,0:T(2,128)} %bitcast.13, ...), custom_call_target="tpu_custom_call" | custom-call | tf_op jit(solution)/shard_map/front/pallas_call | solution.py:1018
  48.6 195.6 %middle.1 = (f32[2,64,2048]{2,1,0:T(8,128)}, f32[2,64,2048]{2,1,0:T(8,128)}, f32[1,2048]{1,0:T(1,128)}, bf16[2,256,512]{2,1,0:T(8,128)(2,1)}, bf16[2,256,2048]{2...) custom-call(bf16[2048]{0:T(1024)(128)(2,1)} %refs_0_.2, ...), custom_call_target="tpu_custom_call" | custom-call | tf_op jit(solution)/shard_map/middle/pallas_call | solution.py:1047
  244.2 80.8 %last.1 = (f32[1,64,2048]{2,1,0:T(8,128)}, f32[2,64,2048]{2,1,0:T(8,128)}, f32[2048]{0:T(1024)}, f32[2048]{0:T(1024)}, f32[128]{0:T(128)}, /*index=5*/f32[128]{0...) custom-call(bf16[2048]{0:T(1024)(128)(2,1)} %refs_0_.3, ...), custom_call_target="tpu_custom_call" | custom-call | tf_op jit(solution)/shard_map/last/pallas_call | solution.py:1084
  325.0 8.5 %finish.1 = (f32[1536,256]{1,0:T(8,128)}, f32[512,256]{1,0:T(8,128)}, f32[256,1536]{1,0:T(8,128)}, f32[256,1536]{1,0:T(8,128)}, f32[256,512]{1,0:T(8,128)}, /*in...) custom-call(f32[256,1536]{1,0:T(8,128)} %get-tuple-element.61.refs_0, ...), custom_call_target="tpu_custom_call" | custom-call | tf_op jit(solution)/shard_map/finish/pallas_call | solution.py:1107

commit v4 on v3

--- a/solution.py
+++ b/solution.py
@@ -224,7 +224,7 @@
     scat.pass_on(1, lo + k - 1, within(lo + k - 1))
     scat.pass_on(0, lo + k, within(lo + k))
     if gath is not None:
-        for hop in range(1, n):
+        for hop in range(n - 1, 0, -1):
             gath.send(hop, f - hop, within(f - hop))
 
 
@@ -266,55 +266,83 @@
             self.copy(m).wait_recv()
 
 
-def for_arrived(gath, hop, body):
-    z, n = gath.z, gath.n
-    if hop == 0:
-        body(z)
-        return
-    left = (z >= hop).astype(jnp.int32)
-    right = (z + hop <= n - 1).astype(jnp.int32)
-
-    def step(i, carry):
-        use_left = both(left == 1, i == 0)
-        body(jnp.where(use_left, z - hop, z + hop))
-        return carry
-
-    lax.fori_loop(0, left + right, step, 0)
-
-
 def row_of(ref):
     return ref[...].astype(F32).reshape(1, ref.shape[0])
 
 
-def front_kernel(n, C, S, HD, docs,
-                 lens_ref, gain_ref, qg_ref, kg_ref, freq_ref, x_hbm, wq_hbm, wk_hbm, wv_hbm,
-                 normed_out, q_out, k_out, qrot_out, krot_out, v_out, prob_out, mix_out, cos_out, sin_out,
-                 x_ref, normed_ref, q_ref, k_ref, qrot_ref, krot_ref, v_ref, prob_ref, mix_ref, cos_ref, sin_ref,
-                 wq, wk, wv, bias, ssem, rsem, wsem, osem):
-    R, D = n * S, x_ref.shape[2]
-    QC, KC = wq.shape[1], wk.shape[1]
-    G = QC // KC
-    KH = KC // HD
+def weight_block(A, B, sib_a, sib_b, cols):
+    total = None
+    for part in range(A.shape[0]):
+        for term in (dot(A[part, :, cols], B[part], 0, 0), dot(sib_a(part), sib_b[part], 0, 0)):
+            total = term if total is None else total + term
+    return total
+
+
+def middle_kernel(n, C, S, W, HD, docs, push, *refs):
+    (lens_ref, attn_gain_ref, qg_ref, kg_ref, freq_ref, gain_ref, x_hbm, cot_hbm_in, wq_hbm, wk_hbm, wv_hbm,
+     wout_hbm, wgate_hbm, wup_hbm, wdown_hbm) = refs[:15]
+    (raws_hbm, prob_hbm, rots_hbm, tabs_hbm, mix_hbm, normed_hbm,
+     middle_hbm, dmid_hbm, gaing_ref, dmix_hbm, db_hbm, mlp_hbm, out_hbm) = refs[15:28]
+    rest = list(refs[28:])
+    if push:
+        sib_n2, sib_cot, sib_act, sib_dg, sib_du, recv_down, recv_gate, blk_up, own_down, own_gate, own_up = rest[:11]
+        rest = rest[11:]
+    else:
+        n2_hbm, cot_hbm, act_hbm, dg_hbm, du_hbm = rest[:5]
+        rest = rest[5:]
+    (x_ref, cot_ref, middle_ref, dmid_ref, out_ref, dmix_ref, mixv, wout, wgate, wup, wdown, cotf, n2f, dbf, partial, sbuf, rbuf, sbufm,
+     dact, act, dg, du, acc, wsem, g1s, g1r, cs, cr, s1s, s1r, g2s, g2r, s2s, s2r, g3s, g3r, sms, smr, osem, vsem) = rest[:40]
+    rest = rest[40:]
+    if push:
+        (stage_d, stage_g, stage_u, transit_d, transit_g, stage32, cols_sib, b_sib, sib_ss, sib_rs,
+         down_ss, down_rs, gate_ss, gate_rs, lsem, ssem32) = rest
+    R = n * S
+    D = x_ref.shape[2]
+    FC = wgate.shape[1]
+    TN = 512
+    nt, nd = FC // TN, D // TN
+    P_ = C * HALVES
+    rows = S // HALVES
+    w, z = lax.axis_index("wide"), lax.axis_index("narrow")
+    QC, KC = mixv.shape[2], wk_hbm.shape[1]
+    QH, KH = QC // HD, KC // HD
+    G = QH // KH
+    PC = QC + 2 * KC
+    table_lanes = C * 2 * HD
+    assert table_lanes % R == 0 and table_lanes + C * R <= FC and PC <= FC
+    assert D % R == 0 and QC + KC <= D - QH * R
+    prob_at = D // R - QH
+
+    def tiles(count, body):
+        def step(j, carry):
+            body(j)
+            return carry
+
+        lax.fori_loop(0, count, step, 0)
+
     loads = [pltpu.make_async_copy(a, b, wsem.at[i]) for i, (a, b) in enumerate(
-        ((x_hbm, x_ref), (wq_hbm, wq), (wk_hbm, wk), (wv_hbm, wv)))]
-    for load in loads:
+        ((x_hbm, x_ref), (cot_hbm_in, cot_ref), (wq_hbm, wgate.at[:, 0:QC]), (wk_hbm, wgate.at[:, QC:QC + KC]),
+         (wv_hbm, wgate.at[:, QC + KC:PC]), (wout_hbm, wout), (wdown_hbm, wdown), (wup_hbm, wup), (wgate_hbm, wgate)))]
+    for load in loads[:8]:
         load.start()
-    gain, qgain, kgain, freq = [row_of(v) for v in (gain_ref, qg_ref, kg_ref, freq_ref)]
-    saved = ((q_ref, q_out), (k_ref, k_out), (qrot_ref, qrot_out), (krot_ref, krot_out), (v_ref, v_out),
-             (prob_ref, prob_out), (mix_ref, mix_out), (cos_ref, cos_out), (sin_ref, sin_out), (normed_ref, normed_out))
-
-    def saves(part):
-        return [pltpu.make_async_copy(a.at[part], b.at[part], osem.at[i, part]) for i, (a, b) in enumerate(saved)]
-
-    gath = Gather(n, C, S, normed_ref, ssem, rsem)
-    z = gath.z
+    gain, again, qgain, kgain, freq = [row_of(v) for v in (gain_ref, attn_gain_ref, qg_ref, kg_ref, freq_ref)]
     loads[0].wait()
     for part in range(C):
         x = x_ref[part].astype(F32)
-        normed_ref[part, rows_at(z, S)] = (x * rms_scale(x) * gain).astype(BF16)
-    barrier(n)
-    for p in range(gath.pieces):
-        gath.send(0, p)
+        dbf[part, rows_at(z, S)] = (x * rms_scale(x) * again).astype(BF16)
+    barrier(n, W if push else 0)
+    g1 = Gather(n, C, S, dbf, g1s, g1r)
+    gc = Gather(n, C, S, cotf, cs, cr)
+    g2 = Gather(n, C, S, n2f, g2s, g2r)
+    g3 = Gather(n, C, S, dbf, g3s, g3r)
+    s1 = Scatter(n, C, S, partial, sbuf, rbuf, s1s, s1r)
+    s2 = Scatter(n, C, S, partial, sbuf, rbuf, s2s, s2r)
+    sm = Scatter(n, C, S, sbufm, sbufm, rbuf, sms, smr)
+    for p in range(2):
+        g1.send(0, p)
+    loads[1].wait()
+    for part in range(C):
+        cotf[part, rows_at(z, S)] = cot_ref[part]
     for part in range(C):
         t = lax.broadcasted_iota(jnp.int32, (R, HD), 0)
         row = lax.broadcasted_iota(jnp.int32, (R, R), 0)
@@ -328,129 +356,80 @@
             first_wide = jnp.where(row >= end, end, first_wide)
         angle = (t - first).astype(F32) * freq
         sign = jnp.where(lax.broadcasted_iota(jnp.int32, (R, HD), 1) < HD // 2, -1.0, 1.0)
-        cos_ref[part] = jnp.cos(angle)
-        sin_ref[part] = jnp.sin(angle) * sign
-        bias[part] = jnp.where(both(col <= row, col >= first_wide), 0.0, masked_score)
-    for load in loads[1:]:
+        dact[:, lanes(2 * part, HD)] = jnp.cos(angle)
+        dact[:, lanes(2 * part + 1, HD)] = jnp.sin(angle) * sign
+        dact[:, lanes(table_lanes // R + part, R)] = jnp.where(both(col <= row, col >= first_wide), 0.0, masked_score)
+
+    cot_from = HALVES + n - 1
+
+    def cot_low(t):
+        @when(t == cot_from)
+        def _():
+            for p in range(HALVES):
+                gc.send(0, p)
+
+        for hop in range(n - 1, 0, -1):
+            p = t - cot_from - 1 - hop
+            gc.send(hop, p, both(p >= 0, p < HALVES))
+
+    def first_step(t):
+        for hop in range(n - 1, 0, -1):
+            p = t - hop
+            g1.send(hop, p, both(p >= 0, p < P_))
+
+        @when(t + 1 < P_)
+        def _():
+            g1.send(0, t + 1)
+
+        cot_low(t)
+
+    half_in = HALVES + n - 2
+    all_in = P_ + n - 2
+    tiles(half_in, lambda i: first_step(i + 1))
+    for load in loads[2:5]:
         load.wait()
 
-    def project(chunk, parts):
-        rows = rows_at(chunk, S)
-        lhs = jnp.concatenate([normed_ref[p, rows] for p in parts], axis=0)
-        for w, out in ((wq, q_ref), (wk, k_ref), (wv, v_ref)):
-            res = dot(lhs, w[...], 1, 0).astype(out.dtype)
-            for i, p in enumerate(parts):
-                out[p, rows] = res[i * S:(i + 1) * S]
-
-    def attend(part):
-        def heads(k, carry):
-            cos2, sin2 = cos_ref[part], sin_ref[part]
-
-            def turned(src, head_gain, col):
-                raw = src[part, :, lanes(col, HD)]
-                return rope(raw * rms_scale(raw) * head_gain, cos2, sin2).astype(BF16)
-
-            kr = turned(k_ref, kgain, k)
-            krot_ref[part, :, lanes(k, HD)] = kr
-            for g in range(G):
-                qr = turned(q_ref, qgain, k * G + g)
-                qrot_ref[part, :, lanes(k * G + g, HD)] = qr
-                s = dot(qr, kr, 1, 1) * HD ** (-0.5) + bias[part]
-                ex = jnp.exp(s - jnp.max(s, axis=-1, keepdims=True))
-                prob = ex / jnp.sum(ex, axis=-1, keepdims=True)
-                prob_ref[part, k * G + g] = prob
-                mix = dot(prob.astype(BF16), v_ref[part, :, lanes(k, HD)], 1, 0)
-                mix_ref[part, :, lanes(k * G + g, HD)] = mix.astype(BF16)
-            return carry
-
-        lax.fori_loop(0, KH, heads, 0)
-
-    for hop in range(n - 1):
-        if hop > 0:
-            for p in range(gath.pieces):
-                gath.send(hop, p)
-        for_arrived(gath, hop, lambda chunk: project(chunk, tuple(range(C))))
-    for part in range(C):
-        for h in range(HALVES):
-            gath.send(n - 1, part * HALVES + h)
-        for_arrived(gath, n - 1, lambda chunk: project(chunk, (part,)))
-        attend(part)
-        for save in saves(part):
-            save.start()
-    gath.drain()
-    for part in range(C):
-        for save in saves(part):
+    def project(part):
+        lhs = dbf[part]
+        partial[part, :, 0:QC + KC] = dot(lhs, wgate[:, 0:QC + KC], 1, 0)
+        act[part, :, QC + KC:PC] = dot(lhs, wgate[:, QC + KC:PC], 1, 0).astype(BF16)
+
+    def attend(part, k):
+        cos2, sin2 = dact[:, lanes(2 * part, HD)], dact[:, lanes(2 * part + 1, HD)]
+
+        def turned(index, head_gain):
+            raw = partial[part, :, lanes(index, HD)]
+            value = rope(raw * rms_scale(raw) * head_gain, cos2, sin2).astype(BF16)
+            act[part, :, lanes(index, HD)] = value
+            return value
+
+        kr = turned(QH + k, kgain)
+        for g in range(G):
+            h = k * G + g
+            qr = turned(h, qgain)
+            s = dot(qr, kr, 1, 1) * HD ** (-0.5) + dact[:, lanes(table_lanes // R + part, R)]
+            ex = jnp.exp(s - jnp.max(s, axis=-1, keepdims=True))
+            prob = ex / jnp.sum(ex, axis=-1, keepdims=True)
+            partial[part, :, lanes(prob_at + h, R)] = prob
+            mix = dot(prob.astype(BF16), act[part, :, lanes(QH + KH + k, HD)], 1, 0)
+            mixv[part, :, lanes(h, HD)] = mix.astype(BF16)
+
+    def saves(part, lo=0, hi=6):
+        return [pltpu.make_async_copy(a, b, vsem.at[i, part]) for i, (a, b) in list(enumerate((
+            (partial.at[part, :, 0:QC + KC], raws_hbm.at[part]), (partial.at[part, :, prob_at * R:D], prob_hbm.at[part]),
+            (act.at[part, :, 0:PC], rots_hbm.at[part]), (dact.at[:, lanes(part, 2 * HD)], tabs_hbm.at[part]),
+            (mixv.at[part], mix_hbm.at[part]), (dbf.at[part], normed_hbm.at[part]))))[lo:hi]]
+
+    def out_project(part):
+        for save in saves(part, 0, 2):
             save.wait()
 
-
-def weight_block(A, B, sib_a, sib_b, cols):
-    total = None
-    for part in range(A.shape[0]):
-        for term in (dot(A[part, :, cols], B[part], 0, 0), dot(sib_a(part), sib_b[part], 0, 0)):
-            total = term if total is None else total + term
-    return total
-
-
-def middle_kernel(n, C, S, W, push, *refs):
-    (gain_ref, x_hbm, cot_hbm_in, mix_hbm, wout_hbm, wgate_hbm, wup_hbm, wdown_hbm,
-     middle_hbm, dmid_hbm, gaing_ref, dmix_hbm, db_hbm, mlp_hbm, out_hbm) = refs[:15]
-    rest = list(refs[15:])
-    if push:
-        sib_n2, sib_cot, sib_act, sib_dg, sib_du, recv_down, recv_gate, blk_up, own_down, own_gate, own_up = rest[:11]
-        rest = rest[11:]
-    else:
-        n2_hbm, cot_hbm, act_hbm, dg_hbm, du_hbm = rest[:5]
-        rest = rest[5:]
-    (x_ref, cot_ref, middle_ref, dmid_ref, out_ref, dmix_ref, mixv, wout, wgate, wup, wdown, cotf, n2f, dbf, partial, sbuf, rbuf, sbufm,
-     dact, act, dg, du, acc, wsem, cs, cr, s1s, s1r, g2s, g2r, s2s, s2r, g3s, g3r, sms, smr, osem) = rest[:37]
-    rest = rest[37:]
-    if push:
-        (stage_d, stage_g, stage_u, transit_d, transit_g, stage32, cols_sib, b_sib, sib_ss, sib_rs,
-         down_ss, down_rs, gate_ss, gate_rs, lsem, ssem32) = rest
-    R = n * S
-    D = x_ref.shape[2]
-    FC = wgate.shape[1]
-    TN = 512
-    nt, nd = FC // TN, D // TN
-    P_ = C * HALVES
-    rows = S // HALVES
-    w, z = lax.axis_index("wide"), lax.axis_index("narrow")
-    loads = [pltpu.make_async_copy(a, b, wsem.at[i]) for i, (a, b) in enumerate(
-        ((mix_hbm, mixv), (wout_hbm, wout), (wdown_hbm, wdown), (wgate_hbm, wgate), (wup_hbm, wup), (cot_hbm_in, cot_ref),
-         (x_hbm, x_ref)))]
-    for index in (5, 0, 1, 6, 2, 3, 4):
-        loads[index].start()
-    gain = row_of(gain_ref)
-    loads[5].wait()
-    for part in range(C):
-        cotf[part, rows_at(z, S)] = cot_ref[part]
-    barrier(n, W if push else 0)
-    gc = Gather(n, C, S, cotf, cs, cr)
-    g2 = Gather(n, C, S, n2f, g2s, g2r)
-    g3 = Gather(n, C, S, dbf, g3s, g3r)
-    s1 = Scatter(n, C, S, partial, sbuf, rbuf, s1s, s1r)
-    s2 = Scatter(n, C, S, partial, sbuf, rbuf, s2s, s2r)
-    sm = Scatter(n, C, S, sbufm, sbufm, rbuf, sms, smr)
-    loads[0].wait()
-    loads[1].wait()
-    loads[6].wait()
-
-    def tiles(count, body):
-        def step(j, carry):
-            body(j)
-            return carry
-
-        lax.fori_loop(0, count, step, 0)
-
-    for part in range(C):
         def out_tile(j):
             partial[part, :, lanes(j, TN)] = dot(mixv[part], wout[:, lanes(j, TN)], 1, 0)
 
         tiles(nd, out_tile)
-        if part == 0:
-            for p in range(2):
-                s1.originate(p)
-                gc.send(0, p)
+        for h in range(HALVES):
+            s1.originate(part * HALVES + h)
 
     def mid_row(p):
         return p // HALVES, rows_at(p % HALVES, rows)
@@ -463,37 +442,65 @@
         g2.at(n2f, z, p)[...] = (middle * rms_scale(middle) * gain).astype(BF16)
 
     def phase_one(k):
-        @when(k + 2 < P_)
+        chain(k, 0, P_, s1, g2, after_attention, n)
+        cot_low(all_in + 1 + k)
+
+    def cot_high(e):
+        @when(e == 0)
         def _():
-            s1.originate(k + 2)
-            gc.send(0, k + 2)
-
-        chain(k, 0, P_, s1, g2, after_attention, n)
-        for hop in range(1, n):
-            gc.send(hop, k + 1 - hop, both(k + 1 - hop >= 0, k + 1 - hop < P_))
+            for h in range(HALVES):
+                gc.send(0, HALVES + h)
+
+        step = jnp.where(e < 4, e - 1, e - 2)
+        for hop in range(n - 1, 0, -1):
+            p = HALVES + step - hop
+            gc.send(hop, p, both(e != 4, step > 0, p >= HALVES, p < P_))
 
     def dact_tile(part, j):
         dact[:, lanes(j, TN)] = dot(cotf[part], wdown[rows_at(j, TN), :], 1, 1)
 
+    project(0)
+    for k in range(max(KH, all_in - half_in)):
+        if half_in + 1 + k <= all_in:
+            first_step(half_in + 1 + k)
+        if k < KH:
+            attend(0, k)
+    for save in saves(0):
+        save.start()
+    project(1)
+    loads[8].start()
+    loads[5].wait()
+    out_project(0)
+    for k in range(KH):
+        attend(1, k)
+        if k == KH - 1:
+            for save in saves(1):
+                save.start()
+        if k < 2:
+            phase_one(k)
+    for k in range(KH, 2):
+        phase_one(k)
+    out_project(1)
     first_in = HALVES + n + 1
-    ready = HALVES + n - 3
+    ready = max(2, cot_from + HALVES + n - 2 - all_in)
+    loads[6].wait()
+    for part in range(C):
+        for save in saves(part, 2, 6):
+            save.wait()
 
     def early(k):
-        phase_one(k)
-
-        @when(k == ready - 1)
+        phase_one(2 + k)
+
+        @when(both(2 + k >= ready, 2 + k < ready + nt))
         def _():
-            loads[2].wait()
-
-        @when(both(k >= ready, k < ready + nt))
-        def _():
-            dact_tile(0, k - ready)
-
-    tiles(first_in, early)
+            dact_tile(0, 2 + k - ready)
+
+    tiles(first_in - 2, early)
     for j in range(max(first_in - ready, 0), nt):
         dact_tile(0, j)
-    loads[3].wait()
-    loads[4].wait()
+    loads[7].wait()
+    loads[8].wait()
+    g1.drain()
     late = P_ + n + 1 - first_in
     if push:
         core = w % 2
@@ -515,7 +522,8 @@
         g3.at(dbf, z, p)[...] = dmid.astype(BF16)
 
     gaing_ref[...] = jnp.zeros_like(gaing_ref)
-    steps = HALVES + n + 1
+    early_steps = (2, 5)
+    assert nt + nd == 7 and HALVES + n - 1 == 5 and late == 2
 
     def feed(part):
         def service(e):
@@ -523,9 +531,14 @@
             def _():
                 phase_one(first_in + e // 2)
 
-            @when(both(part > 0, e < steps))
+            @when(part == 0)
             def _():
-                chain(e, 0, HALVES, s2, g3, after_feed, n)
+                cot_high(e)
+
+            for step, at in enumerate(early_steps):
+                @when(both(part > 0, e == at))
+                def _():
+                    chain(step, 0, P_, s2, g3, after_feed, n)
 
         def gate_tile(j):
             @when(part > 0)
@@ -554,8 +567,6 @@
             service(nt + j)
 
         tiles(nd, back_tile)
-        tiles(max(steps, 2 * late) - nt - nd, lambda e: service(nt + nd + e))
-
         @when(part == 0)
         def _():
             s1.drain()
@@ -566,7 +577,7 @@
     tiles(C, feed)
 
     def tail(k):
-        chain(k, HALVES, P_, s2, g3, after_feed, n)
+        chain(k, 0, P_, s2, g3, after_feed, n)
 
     def mlp_sums(part):
         for j in range(nd):
@@ -580,7 +591,8 @@
         part, rr = mid_row(p)
         out_ref[part, rr] = middle_ref[part, rr] + acc[...]
 
-    mlp_begun = 2
+    begin, steps = len(early_steps), P_ + n + 1
+    mlp_begun = 5
 
     def mlp_start():
         mlp_sums(0)
@@ -663,22 +675,22 @@
 
         work = [[(down_block, 0), (down_block, 1)], [(down_block, 2), (down_block, 3)],
                 [(gate_block, 0), (gate_block, 1)], [(gate_block, 2), (down.pass_on,)],
-                [(gate_block, 3), (up_block, 0), (up_block, 1)], [(up_block, 2), (up_block, 3)],
-                [(gate.pass_on,), (mlp_sums, 1), (mix_back, 0)]]
+                [(gate_block, 3), (up_block, 0), (up_block, 1)], [(up_block, 2), (gate.pass_on,), (mix_back, 0)],
+                [(up_block, 3), (mlp_sums, 1)]]
     else:
         outs = [pltpu.make_async_copy(a, b, osem.at[6 + i]) for i, (a, b) in enumerate(
             ((n2f, n2_hbm), (cotf, cot_hbm), (act, act_hbm), (dg, dg_hbm), (du, du_hbm)))]
         for out in outs:
             out.start()
-        work = [[] for _ in range(steps - 1)] + [[(mlp_sums, 1), (mix_back, 0)]]
-    work += [[]] * (steps - len(work))
-    for k in range(steps):
+        work = [[] for _ in range(steps - begin - 1)] + [[(mlp_sums, 1), (mix_back, 0)]]
+    assert len(work) == steps - begin
+    for k in range(begin, steps):
+        tail(k)
         if k == mlp_begun - 1:
             mlp_start()
-        tail(k)
         if k >= mlp_begun:
             mlp_step(k - mlp_begun)
-        for piece in work[k]:
+        for piece in work[k - begin]:
             piece[0](*piece[1:])
     for k in range(steps - mlp_begun, HALVES + 2):
         mlp_step(k)
@@ -712,8 +724,8 @@
 
 def last_kernel(n, C, S, W, HD, push, *refs):
     gain_ref, qg_ref, kg_ref, gmlp_ref = refs[:4]
-    sources = refs[4:20]
-    rest = list(refs[20:])
+    sources = refs[4:16]
+    rest = list(refs[16:])
     if push:
         mix_hbm, db_hbm, normed_hbm, blk_up = rest[:4]
         rest = rest[4:]
@@ -725,11 +737,10 @@
     else:
         dproj_hbm = rest[0]
         rest = rest[1:]
-    held = rest[:18]
-    (sbufm, q_ref, k_ref, qrot_ref, krot_ref, v_ref, prob_ref, cos_ref, sin_ref, dmix_ref, wq, wk, wv,
-     middle_ref, dmid_ref, x_ref) = held[:16]
-    out_ref, in_ref = held[16:18]
-    rest = rest[18:]
+    held = rest[:14]
+    (sbufm, raws, rots, prob_ref, tabs, dmix_ref, wq, wk, wv, middle_ref, dmid_ref, x_ref) = held[:12]
+    out_ref, in_ref = held[12:14]
+    rest = rest[14:]
     (dproj, partial, sbuf, rbuf, rbufm, acc, gains, small, small_two,
      lsem, s3s, s3r, sms, smr, gs1, gr1, gs2, gr2, osem) = rest[:19]
     rest = rest[19:]
@@ -744,11 +755,11 @@
     P_ = C * HALVES
     rows = S // HALVES
     w, z = lax.axis_index("wide"), lax.axis_index("narrow")
-    loads = [pltpu.make_async_copy(a, b, lsem.at[i]) for i, (a, b) in enumerate(zip(sources, held[:16]))]
+    loads = [pltpu.make_async_copy(a, b, lsem.at[i]) for i, (a, b) in enumerate(zip(sources, held[:12]))]
     for load in loads:
         load.start()
     if push:
-        extra = [pltpu.make_async_copy(a, b, lsem.at[16 + i]) for i, (a, b) in enumerate(
+        extra = [pltpu.make_async_copy(a, b, lsem.at[12 + i]) for i, (a, b) in enumerate(
             ((mix_hbm, mixv), (db_hbm, dbv), (normed_hbm, normv)))]
         for load in extra:
             load.start()
@@ -763,7 +774,7 @@
             Square(squares[i], squares[i + 1], recv, squares[i + 2], squares[i + 3])
             for i, recv in ((0, recv_up), (4, recv_out), (8, recv_qkv))]
         stage_up, stage_out, stage_qkv = squares[0], squares[4], squares[8]
-        blocks = [pltpu.make_async_copy(blk_up.at[q], stage_up.at[q], lsem.at[19 + q]) for q in range(3)]
+        blocks = [pltpu.make_async_copy(blk_up.at[q], stage_up.at[q], lsem.at[15 + q]) for q in range(3)]
         for q in range(3):
             blocks[q].start()
 
@@ -809,8 +820,8 @@
         load.wait()
 
     def unit(part, k):
-        cos2, sin2 = cos_ref[part], sin_ref[part]
-        kr, vr = krot_ref[part, :, lanes(k, HD)], v_ref[part, :, lanes(k, HD)]
+        cos2, sin2 = tabs[part, :, 0:HD], tabs[part, :, HD:2 * HD]
+        kr, vr = rots[part, :, lanes(QC // HD + k, HD)], rots[part, :, lanes(QC // HD + KH + k, HD)]
 
         def unturned(grad, raw, head_gain, at):
             d_n = grad * cos2 - pltpu.roll(grad, HD // 2, axis=1) * sin2
@@ -822,17 +833,17 @@
         dk, dv = None, None
         for g in range(G):
             h = k * G + g
-            pr = prob_ref[part, h]
+            pr = prob_ref[part, :, lanes(h, R)]
             dm = dmix_ref[part, :, lanes(h, HD)]
             dp = dot(dm, vr, 1, 1)
             one = dot(pr.astype(BF16), dm, 0, 0)
             dv = one if dv is None else dv + one
             ds = (pr * (dp - jnp.sum(pr * dp, axis=-1, keepdims=True))).astype(BF16)
-            one = dot(ds, qrot_ref[part, :, lanes(h, HD)], 0, 0)
+            one = dot(ds, rots[part, :, lanes(h, HD)], 0, 0)
             dk = one if dk is None else dk + one
             dq = dot(ds, kr, 1, 0) * scale
-            dproj[part, :, lanes(h, HD)] = unturned(dq, q_ref[part, :, lanes(h, HD)], qgain, 1)
-        dproj[part, :, lanes(QC // HD + k, HD)] = unturned(dk * scale, k_ref[part, :, lanes(k, HD)], kgain, 2)
+            dproj[part, :, lanes(h, HD)] = unturned(dq, raws[part, :, lanes(h, HD)], qgain, 1)
+        dproj[part, :, lanes(QC // HD + k, HD)] = unturned(dk * scale, raws[part, :, lanes(QC // HD + k, HD)], kgain, 2)
         dproj[part, :, lanes(QC // HD + KH + k, HD)] = dv.astype(BF16)
 
     per_part = KH + 1
@@ -845,6 +856,34 @@
             def _():
                 up_sums.pass_on()
 
+    if push:
+        def block(A, B, sib_a, sib_b, owner):
+            cols = lanes(owner, width)
+            return weight_block(A, B, lambda part: sib_a[part, :, cols], sib_b, cols)
+
+        def arrive(*pairs):
+            for part in range(C):
+                for index, dst in pairs:
+                    swap(index, dst, dst, part).wait_recv()
+
+        def out_block(q):
+            if q == 0:
+                arrive((0, sib_mix), (1, sib_db))
+            if q < 3:
+                stage_out[q] = block(dbv, mixv, sib_db, sib_mix, out_sums.owners[q]).astype(BF16)
+                out_sums.put(q)
+            else:
+                own_out[...] = block(dbv, mixv, sib_db, sib_mix, w)
+
+        def qkv_block(q):
+            if q == 0:
+                arrive((2, sib_norm), (3, sib_dproj))
+            if q < 3:
+                stage_qkv[q] = block(normv, dproj, sib_norm, sib_dproj, qkv_sums.owners[q]).astype(BF16)
+                qkv_sums.put(q)
+            else:
+                own_qkv[...] = block(normv, dproj, sib_norm, sib_dproj, w)
+
     def backward(part):
         def heads(k, carry):
             unit(part, k)
@@ -866,6 +905,11 @@
         for h in range(HALVES):
             s3.originate(part * HALVES + h)
         between(part * per_part + KH)
+        if push:
+            @when(part == 0)
+            def _():
+                for q in range(3):
+                    out_block(q)
 
     def both_parts(part, carry):
         backward(part)
@@ -877,30 +921,8 @@
         between(e)
     steps = HALVES + 2
     if push:
-        def block(A, B, sib_a, sib_b, owner):
-            cols = lanes(owner, width)
-            return weight_block(A, B, lambda part: sib_a[part, :, cols], sib_b, cols)
-
-        def out_block(q):
-            if q == 0:
-                for part in range(C):
-                    for index, (a, b) in enumerate(((mixv, sib_mix), (dbv, sib_db), (normv, sib_norm), (dproj, sib_dproj))):
-                        swap(index, a, b, part).wait_recv()
-            if q < 3:
-                stage_out[q] = block(dbv, mixv, sib_db, sib_mix, out_sums.owners[q]).astype(BF16)
-                out_sums.put(q)
-            else:
-                own_out[...] = block(dbv, mixv, sib_db, sib_mix, w)
-
-        def qkv_block(q):
-            if q < 3:
-                stage_qkv[q] = block(normv, dproj, sib_norm, sib_dproj, qkv_sums.owners[q]).astype(BF16)
-                qkv_sums.put(q)
-            else:
-                own_qkv[...] = block(normv, dproj, sib_norm, sib_dproj, w)
-
-        work = [[(out_block, 0), (qkv_block, 0)], [(qkv_block, 1), (qkv_block, 2)], [(out_block, 1), (out_block, 2)],
-                [(qkv_block, 3), (out_block, 3), (qkv_sums.pass_on,), (out_sums.pass_on,)]]
+        work = [[(qkv_block, 0), (out_sums.pass_on,)], [(qkv_block, 1), (qkv_block, 2)], [(qkv_block, 3)],
+                [(out_block, 3), (qkv_sums.pass_on,)]]
         assert len(work) == steps
     else:
         work = [[]] * steps
@@ -1013,28 +1035,20 @@
     smem = pl.BlockSpec(memory_space=pltpu.SMEM)
     VM = pltpu.VMEM
 
-    shapes = [((C, R, D), BF16), ((C, R, QC), F32), ((C, R, KC), F32), ((C, R, QC), BF16), ((C, R, KC), BF16),
-              ((C, R, KC), BF16), ((C, QH, R, R), F32), ((C, R, QC), BF16), ((C, R, HD), F32), ((C, R, HD), F32)]
-    normed_full, q_raw, k_raw, q_rot, k_rot, v_rows, prob, mix, cos2, sin2 = pl.pallas_call(
-        functools.partial(front_kernel, n, C, S, HD, docs), name="front",
-        out_shape=[sds(*one) for one in shapes], in_specs=[smem, vm, vm, vm, vm, hbm, hbm, hbm, hbm], out_specs=[hbm] * 10,
-        scratch_shapes=[VM((C, S, D), BF16)] + [VM(*one) for one in shapes]
-        + [VM(w_query.shape, BF16), VM(w_key.shape, BF16), VM(w_value.shape, BF16),
-           VM((C, R, R), F32), gsem(), gsem(), dma((4,)), dma((10, C))],
-        compiler_params=pltpu.CompilerParams(collective_id=0, has_side_effects=True, vmem_limit_bytes=56 << 20),
-    )(document_lengths[:, 0], attn_gain, query_gain, key_gain, freq, x_own, w_query, w_key, w_value)
-
+    PC = QC + 2 * KC
     full, wide_rows = sds((C, R, D), BF16), sds((C, R, FC), BF16)
-    outs = [sds((C, S, D), F32), sds((C, S, D), F32), sds((1, D), F32), sds((C, R, QC), BF16), full, full, sds((1, S, D), F32)]
-    specs = [hbm, hbm, vm, hbm, hbm, hbm, hbm]
+    kept = [sds((C, R, QC + KC), F32), sds((C, R, QH * R), F32), sds((C, R, PC), BF16), sds((C, R, 2 * HD), F32),
+            sds((C, R, QC), BF16), full]
+    outs = kept + [sds((C, S, D), F32), sds((C, S, D), F32), sds((1, D), F32), sds((C, R, QC), BF16), full, full, sds((1, S, D), F32)]
+    specs = [hbm] * 8 + [vm] + [hbm] * 4
     line = lambda: [VM((C, R, D), BF16), VM((C, R + S, D), BF16)]
     scratch = (
         [VM((C, S, D), BF16), VM((C, S, D), BF16), VM((C, S, D), F32), VM((C, S, D), F32), VM((1, S, D), F32), VM((C, R, QC), BF16)]
         + [VM((C, R, QC), BF16), VM(w_out.shape, BF16), VM(w_gate.shape, BF16), VM(w_up.shape, BF16), VM(w_down.shape, BF16)]
         + [VM((C, R, D), BF16)] * 3 + [VM((C, R, D), F32)] + line()
         + [VM((C, R, D), BF16), VM((R, FC), F32)] + [VM((C, R, FC), BF16)] * 3 + [VM((S // HALVES, D), F32)]
-        + [dma((7,)), gsem(), gsem(), dma((n, P_)), dma((2, n, P_)), gsem(), gsem(), dma((n, P_)), dma((2, n, P_)),
-           gsem(), gsem(), dma((n, P_)), dma((2, n, P_)), dma((11,))]
+        + [dma((9,)), gsem(), gsem(), gsem(), gsem(), dma((n, P_)), dma((2, n, P_)), gsem(), gsem(), dma((n, P_)), dma((2, n, P_)),
+           gsem(), gsem(), dma((n, P_)), dma((2, n, P_)), dma((11,)), dma((6, C))]
     )
     if push:
         sums, own = sds((2, width, FC), BF16), sds((width, FC), F32)
@@ -1045,25 +1059,26 @@
     else:
         outs += [full, full, wide_rows, wide_rows, wide_rows]
     res = pl.pallas_call(
-        functools.partial(middle_kernel, n, C, S, W, push), name="middle", out_shape=outs,
-        in_specs=[vm] + [hbm] * 7, out_specs=specs + [hbm] * (len(outs) - len(specs)), scratch_shapes=scratch,
-        compiler_params=pltpu.CompilerParams(collective_id=1, has_side_effects=True, vmem_limit_bytes=63 << 20),
-    )(mlp_gain, x_own, cot_own, mix, w_out, w_gate, w_up, w_down)
+        functools.partial(middle_kernel, n, C, S, W, HD, docs, push), name="middle", out_shape=outs,
+        in_specs=[smem] + [vm] * 5 + [hbm] * 9, out_specs=specs + [hbm] * (len(outs) - len(specs)), scratch_shapes=scratch,
+        compiler_params=pltpu.CompilerParams(collective_id=0, has_side_effects=True, vmem_limit_bytes=63 << 20),
+    )(document_lengths[:, 0], attn_gain, query_gain, key_gain, freq, mlp_gain, x_own, cot_own, w_query, w_key, w_value, w_out, w_gate, w_up, w_down)
+    raws, prob, rots, tabs, mix, normed_full = res[:6]
+    res = res[6:]
     middle, d_middle, gmlp, d_mix, db_full, mlp_sums, out_low = res[:7]
 
-    args = [attn_gain, query_gain, key_gain, gmlp, mlp_sums, q_raw, k_raw, q_rot, k_rot, v_rows, prob, cos2, sin2, d_mix, w_query, w_key, w_value,
+    args = [attn_gain, query_gain, key_gain, gmlp, mlp_sums, raws, rots, prob, tabs, d_mix, w_query, w_key, w_value,
             middle, d_middle, x_own]
-    in_specs = [vm] * 4 + [hbm] * 16
+    in_specs = [vm] * 4 + [hbm] * 12
     held = [VM(v.shape, v.dtype) for v in args[4:]] + [VM((1, S, D), F32), VM((C, S, D), F32)]
     own_rows = sds((C, S, D), F32)
     outs = [sds((1, S, D), F32), own_rows, sds((D,), F32), sds((D,), F32), sds((HD,), F32), sds((HD,), F32)]
     specs = [hbm] * 2 + [vm] * 4
-    PC = QC + 2 * KC
     L = 2 * D + 2 * HD
     scratch = (
         held + [VM((C, R, PC), BF16), VM((C, R, D), F32)]
         + line() + line()[1:] + [VM((S // HALVES, D), F32), VM((8, D), F32), VM((W, 1, L), F32), VM((n, 1, L), F32)]
-        + [dma((22,)), dma((n, P_)), dma((2, n, P_)), dma((n, P_)), dma((2, n, P_)), dma((W,)), dma((W,)), dma((n,)), dma((n,)),
+        + [dma((18,)), dma((n, P_)), dma((2, n, P_)), dma((n, P_)), dma((2, n, P_)), dma((W,)), dma((W,)), dma((n,)), dma((n,)),
            dma((2,))]
     )
     if push:
@@ -1084,7 +1099,7 @@
     last = pl.pallas_call(
         functools.partial(last_kernel, n, C, S, W, HD, push), name="last", out_shape=outs, in_specs=in_specs, out_specs=specs,
         scratch_shapes=scratch,
-        compiler_params=pltpu.CompilerParams(collective_id=2, has_side_effects=True, vmem_limit_bytes=60 << 20),
+        compiler_params=pltpu.CompilerParams(collective_id=1, has_side_effects=True, vmem_limit_bytes=60 << 20),
     )(*args)
     out_high, in_own, g_attn, g_mlp, g_query, g_key = last[:6]
     if push:

time: 334 us -> 297 us (0.89)
  Pallas kernels: 333 us -> 296 us
    pallas_call x2 -> x1, Pallas kernels: 244 us -> 214 us  [local(): pl.pallas_call(functools.partial(middle_kernel, n, C, S, W, HD, docs, pus...]
    pallas_call x1, Pallas kernels: 80.8 us -> 73.9 us  [local(): pl.pallas_call(functools.partial(last_kernel, n, C, S, W, HD, push), name...]
where the time goes in v4:
time: 297 us
  Pallas kernels  296 us (100%)
    pallas_call x1, Pallas kernels, local(): pl.pallas_call(functools.partial(middle_kernel, n, C, S, W, HD, docs, pus...  214 us
    pallas_call x1, Pallas kernels, local(): pl.pallas_call(functools.partial(last_kernel, n, C, S, W, HD, push), name...  73.9 us
    pallas_call x1, Pallas kernels, local(): pl.pallas_call(finish_kernel, name='finish', grid=(grid,), out_shape=[sds...  8.54 us

profile of v4, /device:TPU:0, one launch (start us, length us, event | category | flops | bytes accessed | tf_op | source)
XLA Modules:
  0.0 297.1 jit_solution(6310430497086608507)
XLA Ops:
  0.6 213.8 %middle.1 = (f32[2,256,768]{2,1,0:T(8,128)}, f32[2,256,1024]{2,1,0:T(8,128)}, bf16[2,256,1024]{2,1,0:T(8,128)(2,1)}, f32[2,256,256]{2,1,0:T(8,128)}, bf16[2,256,...) custom-call(s32[2,4]{1,0:T(2,128)} %bitcast.12, ...), custom_call_target="tpu_custom_call" | custom-call | tf_op jit(solution)/shard_map/middle/pallas_call | solution.py:1061
  214.4 73.9 %last.1 = (f32[1,64,2048]{2,1,0:T(8,128)}, f32[2,64,2048]{2,1,0:T(8,128)}, f32[2048]{0:T(1024)}, f32[2048]{0:T(1024)}, f32[128]{0:T(128)}, /*index=5*/f32[128]{0...) custom-call(bf16[2048]{0:T(1024)(128)(2,1)} %refs_0_.1, ...), custom_call_target="tpu_custom_call" | custom-call | tf_op jit(solution)/shard_map/last/pallas_call | solution.py:1099
  288.4 8.5 %finish.1 = (f32[1536,256]{1,0:T(8,128)}, f32[512,256]{1,0:T(8,128)}, f32[256,1536]{1,0:T(8,128)}, f32[256,1536]{1,0:T(8,128)}, f32[256,512]{1,0:T(8,128)}, /*in...) custom-call(f32[256,1536]{1,0:T(8,128)} %get-tuple-element.56.refs_0, ...), custom_call_target="tpu_custom_call" | custom-call | tf_op jit(solution)/shard_map/finish/pallas_call | solution.py:1122

commit v5 on v4

--- a/solution.py
+++ b/solution.py
@@ -226,6 +226,25 @@
     if gath is not None:
         for hop in range(n - 1, 0, -1):
             gath.send(hop, f - hop, within(f - hop))
+
+
+def staggered(k, starts, scat, gath, finish, n):
+    ages = [(k - start, p) for p, start in enumerate(starts)]
+    for age, p in ages:
+        if age == 2:
+            finish(p)
+            if gath is not None:
+                gath.send(0, p)
+    for age, p in ages:
+        if age == 1:
+            scat.pass_on(1, p)
+    for age, p in ages:
+        if age == 0:
+            scat.pass_on(0, p)
+    if gath is not None:
+        for age, p in ages:
+            if 3 <= age <= n + 1:
+                gath.send(age - 2, p)
 
 
 class Square:
@@ -276,6 +295,32 @@
         for term in (dot(A[part, :, cols], B[part], 0, 0), dot(sib_a(part), sib_b[part], 0, 0)):
             total = term if total is None else total + term
     return total
+
+
+PLAN = dict(
+    branch_starts=(0, 1, 4, 5), back_starts=(0, 1, 4, 5),
+    after=dict(
+        start=(('input', 0), ('input', 1), ('input', 2), ('input', 3), ('cot0', 0)),
+        out0=(('input', 4), ('input', 5), ('cot0', 1), ('cot0', 2)),
+        attend10=(('branch', 0), ('branch', 1), ('branch', 2), ('cot0', 3)),
+        attend11=(('branch', 3),),
+        out1=(('cot0', 4), ('cot1', 0)),
+        act=(('branch', 4), ('branch', 5), ('branch', 6)),
+        feed01=(('cot1', 1),),
+        feed03=(('branch', 7),),
+        feed05=(('branch', 8), ('cot1', 2)),
+        feed06=(('branch', 9), ('branch', 10), ('cot1', 3), ('cot1', 4)),
+        feed10=(('back', 0),),
+        feed11=(('back', 1), ('back', 2)),
+        feed14=(('back', 3),),
+        work4=(('back', 4),),
+        work6=(('back', 5), ('back', 6)),
+        work9=(('back', 7), ('mlp', 0)),
+        work11=(('back', 8),),
+        work12=(('mlp', 1),),
+        work13=(('back', 9), ('back', 10), ('mlp', 2), ('mlp', 3), ('mlp', 4)),
+    ),
+)
 
 
 def middle_kernel(n, C, S, W, HD, docs, push, *refs):
@@ -360,32 +405,46 @@
         dact[:, lanes(2 * part + 1, HD)] = jnp.sin(angle) * sign
         dact[:, lanes(table_lanes // R + part, R)] = jnp.where(both(col <= row, col >= first_wide), 0.0, masked_score)
 
-    cot_from = HALVES + n - 1
-
-    def cot_low(t):
-        @when(t == cot_from)
-        def _():
-            for p in range(HALVES):
-                gc.send(0, p)
-
+    def input_step(k):
         for hop in range(n - 1, 0, -1):
-            p = t - cot_from - 1 - hop
-            gc.send(hop, p, both(p >= 0, p < HALVES))
-
-    def first_step(t):
+            if 0 <= k + 1 - hop < P_:
+                g1.send(hop, k + 1 - hop)
+        if k + 2 < P_:
+            g1.send(0, k + 2)
+
+    def cot_step(part, k):
+        if k == 0:
+            for h in range(HALVES):
+                gc.send(0, part * HALVES + h)
         for hop in range(n - 1, 0, -1):
-            p = t - hop
-            g1.send(hop, p, both(p >= 0, p < P_))
-
-        @when(t + 1 < P_)
-        def _():
-            g1.send(0, t + 1)
-
-        cot_low(t)
-
-    half_in = HALVES + n - 2
-    all_in = P_ + n - 2
-    tiles(half_in, lambda i: first_step(i + 1))
+            if 0 <= k - hop < HALVES:
+                gc.send(hop, part * HALVES + k - hop)
+
+    def mlp_step(k):
+        if k == 0:
+            for j in range(nd):
+                sbufm[0, :, lanes(j, TN)] = dot(act[0], wdown[:, lanes(j, TN)], 1, 0).astype(BF16)
+            for h in range(HALVES):
+                sm.originate(h)
+        else:
+            staggered(k - 1, tuple(range(HALVES)), sm, None, mlp_done, n)
+
+    def mlp_done(p):
+        sm.final(p, acc)
+        part, rr = mid_row(p)
+        out_ref[part, rr] = middle_ref[part, rr] + acc[...]
+
+    steps = dict(
+        input=input_step, cot0=functools.partial(cot_step, 0), cot1=functools.partial(cot_step, 1), mlp=mlp_step,
+        branch=lambda k: staggered(k, PLAN["branch_starts"], s1, g2, after_attention, n),
+        back=lambda k: staggered(k, PLAN["back_starts"], s2, g3, after_feed, n))
+    assert (n, C, HALVES, KH, nt, nd) == (4, 2, 2, 2, 3, 4)
+
+    def run(place):
+        for kind, k in PLAN["after"].get(place, ()):
+            steps[kind](k)
+
+    run("start")
     for load in loads[2:5]:
         load.wait()
 
@@ -421,6 +480,8 @@
             (mixv.at[part], mix_hbm.at[part]), (dbf.at[part], normed_hbm.at[part]))))[lo:hi]]
 
     def out_project(part):
+        if part == 0:
+            loads[5].wait()
         for save in saves(part, 0, 2):
             save.wait()
 
@@ -441,67 +502,39 @@
         middle_ref[part, rr] = middle
         g2.at(n2f, z, p)[...] = (middle * rms_scale(middle) * gain).astype(BF16)
 
-    def phase_one(k):
-        chain(k, 0, P_, s1, g2, after_attention, n)
-        cot_low(all_in + 1 + k)
-
-    def cot_high(e):
-        @when(e == 0)
-        def _():
-            for h in range(HALVES):
-                gc.send(0, HALVES + h)
-
-        step = jnp.where(e < 4, e - 1, e - 2)
-        for hop in range(n - 1, 0, -1):
-            p = HALVES + step - hop
-            gc.send(hop, p, both(e != 4, step > 0, p >= HALVES, p < P_))
-
     def dact_tile(part, j):
         dact[:, lanes(j, TN)] = dot(cotf[part], wdown[rows_at(j, TN), :], 1, 1)
 
     project(0)
-    for k in range(max(KH, all_in - half_in)):
-        if half_in + 1 + k <= all_in:
-            first_step(half_in + 1 + k)
-        if k < KH:
-            attend(0, k)
-    for save in saves(0):
-        save.start()
+    run("project0")
+    for k in range(KH):
+        attend(0, k)
+        if k == KH - 1:
+            for save in saves(0):
+                save.start()
+        run("attend0%d" % k)
+    out_project(0)
+    run("out0")
     project(1)
     loads[8].start()
-    loads[5].wait()
-    out_project(0)
+    run("project1")
     for k in range(KH):
         attend(1, k)
         if k == KH - 1:
             for save in saves(1):
                 save.start()
-        if k < 2:
-            phase_one(k)
-    for k in range(KH, 2):
-        phase_one(k)
+        run("attend1%d" % k)
     out_project(1)
-    first_in = HALVES + n + 1
-    ready = max(2, cot_from + HALVES + n - 2 - all_in)
+    run("out1")
     loads[6].wait()
     for part in range(C):
         for save in saves(part, 2, 6):
             save.wait()
-
-    def early(k):
-        phase_one(2 + k)
-
-        @when(both(2 + k >= ready, 2 + k < ready + nt))
-        def _():
-            dact_tile(0, 2 + k - ready)
-
-    tiles(first_in - 2, early)
-    for j in range(max(first_in - ready, 0), nt):
-        dact_tile(0, j)
+    tiles(nt, lambda j: dact_tile(0, j))
+    run("act")
     loads[7].wait()
     loads[8].wait()
     g1.drain()
-    late = P_ + n + 1 - first_in
     if push:
         core = w % 2
         mate = w + 1 - 2 * core
@@ -522,23 +555,15 @@
         g3.at(dbf, z, p)[...] = dmid.astype(BF16)
 
     gaing_ref[...] = jnp.zeros_like(gaing_ref)
-    early_steps = (2, 5)
-    assert nt + nd == 7 and HALVES + n - 1 == 5 and late == 2
 
     def feed(part):
-        def service(e):
-            @when(both(part == 0, e % 2 == 1, e // 2 < late))
-            def _():
-                phase_one(first_in + e // 2)
-
-            @when(part == 0)
-            def _():
-                cot_high(e)
-
-            for step, at in enumerate(early_steps):
-                @when(both(part > 0, e == at))
-                def _():
-                    chain(step, 0, P_, s2, g3, after_feed, n)
+        def service(e, only=range(nt + nd - 1)):
+            for which in range(C):
+                for at in only:
+                    if "feed%d%d" % (which, at) in PLAN["after"]:
+                        @when(both(part == which, e == at))
+                        def _():
+                            run("feed%d%d" % (which, at))
 
         def gate_tile(j):
             @when(part > 0)
@@ -573,31 +598,13 @@
 
         for h in range(HALVES):
             s2.originate(part * HALVES + h)
+        service(nt + nd - 1, (nt + nd - 1,))
 
     tiles(C, feed)
-
-    def tail(k):
-        chain(k, 0, P_, s2, g3, after_feed, n)
 
     def mlp_sums(part):
         for j in range(nd):
             sbufm[part, :, lanes(j, TN)] = dot(act[part], wdown[:, lanes(j, TN)], 1, 0).astype(BF16)
-
-    def mlp_step(k):
-        chain(k, 0, HALVES, sm, None, mlp_done, n)
-
-    def mlp_done(p):
-        sm.final(p, acc)
-        part, rr = mid_row(p)
-        out_ref[part, rr] = middle_ref[part, rr] + acc[...]
-
-    begin, steps = len(early_steps), P_ + n + 1
-    mlp_begun = 5
-
-    def mlp_start():
-        mlp_sums(0)
-        for h in range(HALVES):
-            sm.originate(h)
 
     def mix_back(part):
         dmix_ref[part] = dot(dbf[part], wout[...], 1, 1).astype(BF16)
@@ -673,27 +680,19 @@
                 stage32[...] = block(n2f, du, q)
                 own_copy(own_up, 2).start()
 
-        work = [[(down_block, 0), (down_block, 1)], [(down_block, 2), (down_block, 3)],
-                [(gate_block, 0), (gate_block, 1)], [(gate_block, 2), (down.pass_on,)],
-                [(gate_block, 3), (up_block, 0), (up_block, 1)], [(up_block, 2), (gate.pass_on,), (mix_back, 0)],
-                [(up_block, 3), (mlp_sums, 1)]]
+        work = [[(down_block, q)] for q in range(4)] + [[(gate_block, q)] for q in range(3)] + [
+            [(down.pass_on,), (gate_block, 3)], [(up_block, 0)], [(up_block, 1)], [(gate.pass_on,), (up_block, 2)], [(up_block, 3)]]
     else:
         outs = [pltpu.make_async_copy(a, b, osem.at[6 + i]) for i, (a, b) in enumerate(
             ((n2f, n2_hbm), (cotf, cot_hbm), (act, act_hbm), (dg, dg_hbm), (du, du_hbm)))]
         for out in outs:
             out.start()
-        work = [[] for _ in range(steps - begin - 1)] + [[(mlp_sums, 1), (mix_back, 0)]]
-    assert len(work) == steps - begin
-    for k in range(begin, steps):
-        tail(k)
-        if k == mlp_begun - 1:
-            mlp_start()
-        if k >= mlp_begun:
-            mlp_step(k - mlp_begun)
-        for piece in work[k - begin]:
+        work = [[] for _ in range(12)]
+    work += [[(mlp_sums, 1)], [(mix_back, 0)]]
+    for place, pieces in enumerate(work):
+        for piece in pieces:
             piece[0](*piece[1:])
-    for k in range(steps - mlp_begun, HALVES + 2):
-        mlp_step(k)
+        run("work%d" % place)
     ends = [pltpu.make_async_copy(a, b, osem.at[i]) for i, (a, b) in enumerate(
         ((sbufm, mlp_hbm), (dbf, db_hbm), (middle_ref, middle_hbm), (dmid_ref, dmid_hbm), (out_ref, out_hbm), (dmix_ref, dmix_hbm)))]
     for end in ends[:5]:

time: 297 us -> 280 us (0.943)
  Pallas kernels: 296 us -> 279 us
    pallas_call x1, Pallas kernels: 214 us -> 197 us  [local(): pl.pallas_call(functools.partial(middle_kernel, n, C, S, W, HD, docs, pus...]
where the time goes in v5:
time: 280 us
  Pallas kernels  279 us (100%)
    pallas_call x1, Pallas kernels, local(): pl.pallas_call(functools.partial(middle_kernel, n, C, S, W, HD, docs, pus...  197 us
    pallas_call x1, Pallas kernels, local(): pl.pallas_call(functools.partial(last_kernel, n, C, S, W, HD, push), name...  73.7 us
    pallas_call x1, Pallas kernels, local(): pl.pallas_call(finish_kernel, name='finish', grid=(grid,), out_shape=[sds...  8.54 us

profile of v5, /device:TPU:0, one launch (start us, length us, event | category | flops | bytes accessed | tf_op | source)
XLA Modules:
  0.0 279.9 jit_solution(13165571588400129184)
XLA Ops:
  0.6 196.9 %middle.1 = (f32[2,256,768]{2,1,0:T(8,128)}, f32[2,256,1024]{2,1,0:T(8,128)}, bf16[2,256,1024]{2,1,0:T(8,128)(2,1)}, f32[2,256,256]{2,1,0:T(8,128)}, bf16[2,256,...) custom-call(s32[2,4]{1,0:T(2,128)} %bitcast.12, ...), custom_call_target="tpu_custom_call" | custom-call | tf_op jit(solution)/shard_map/middle/pallas_call | solution.py:1060
  197.5 73.7 %last.1 = (f32[1,64,2048]{2,1,0:T(8,128)}, f32[2,64,2048]{2,1,0:T(8,128)}, f32[2048]{0:T(1024)}, f32[2048]{0:T(1024)}, f32[128]{0:T(128)}, /*index=5*/f32[128]{0...) custom-call(bf16[2048]{0:T(1024)(128)(2,1)} %refs_0_.1, ...), custom_call_target="tpu_custom_call" | custom-call | tf_op jit(solution)/shard_map/last/pallas_call | solution.py:1098
  271.2 8.5 %finish.1 = (f32[1536,256]{1,0:T(8,128)}, f32[512,256]{1,0:T(8,128)}, f32[256,1536]{1,0:T(8,128)}, f32[256,1536]{1,0:T(8,128)}, f32[256,512]{1,0:T(8,128)}, /*in...) custom-call(f32[256,1536]{1,0:T(8,128)} %get-tuple-element.56.refs_0, ...), custom_call_target="tpu_custom_call" | custom-call | tf_op jit(solution)/shard_map/finish/pallas_call | solution.py:1121

commit v6 on v5

--- a/solution.py
+++ b/solution.py
@@ -371,11 +371,11 @@
     for load in loads[:8]:
         load.start()
     gain, again, qgain, kgain, freq = [row_of(v) for v in (gain_ref, attn_gain_ref, qg_ref, kg_ref, freq_ref)]
+    barrier(n, W if push else 0)
     loads[0].wait()
     for part in range(C):
         x = x_ref[part].astype(F32)
         dbf[part, rows_at(z, S)] = (x * rms_scale(x) * again).astype(BF16)
-    barrier(n, W if push else 0)
     g1 = Gather(n, C, S, dbf, g1s, g1r)
     gc = Gather(n, C, S, cotf, cs, cr)
     g2 = Gather(n, C, S, n2f, g2s, g2r)
@@ -636,7 +636,7 @@
             return pltpu.make_async_copy(stage32, dst, ssem32.at[index])
 
         def up_copy(q):
-            return pltpu.make_async_copy(stage_u.at[q % 2], blk_up.at[q], osem.at[6 + q])
+            return pltpu.make_async_copy(stage_u.at[q % 2], blk_up.at[q], osem.at[7 + q])
 
         def arrive(*pairs):
             for part in range(C):
@@ -683,23 +683,34 @@
         work = [[(down_block, q)] for q in range(4)] + [[(gate_block, q)] for q in range(3)] + [
             [(down.pass_on,), (gate_block, 3)], [(up_block, 0)], [(up_block, 1)], [(gate.pass_on,), (up_block, 2)], [(up_block, 3)]]
     else:
-        outs = [pltpu.make_async_copy(a, b, osem.at[6 + i]) for i, (a, b) in enumerate(
+        outs = [pltpu.make_async_copy(a, b, osem.at[7 + i]) for i, (a, b) in enumerate(
             ((n2f, n2_hbm), (cotf, cot_hbm), (act, act_hbm), (dg, dg_hbm), (du, du_hbm)))]
         for out in outs:
             out.start()
         work = [[] for _ in range(12)]
-    work += [[(mlp_sums, 1)], [(mix_back, 0)]]
+    ends = [pltpu.make_async_copy(a, b, osem.at[i]) for i, (a, b) in enumerate(
+        ((middle_ref, middle_hbm), (sbufm.at[1], mlp_hbm.at[0]), (dbf.at[0], db_hbm.at[0]), (dbf.at[1], db_hbm.at[1]),
+         (dmid_ref, dmid_hbm), (out_ref, out_hbm), (dmix_ref, dmix_hbm)))]
+    ends[0].start()
+
+    def second_mlp_sums():
+        mlp_sums(1)
+        ends[1].start()
+
+    def first_mix_back():
+        mix_back(0)
+        ends[2].start()
+
+    work += [[(second_mlp_sums,)], [(first_mix_back,)]]
     for place, pieces in enumerate(work):
         for piece in pieces:
             piece[0](*piece[1:])
         run("work%d" % place)
-    ends = [pltpu.make_async_copy(a, b, osem.at[i]) for i, (a, b) in enumerate(
-        ((sbufm, mlp_hbm), (dbf, db_hbm), (middle_ref, middle_hbm), (dmid_ref, dmid_hbm), (out_ref, out_hbm), (dmix_ref, dmix_hbm)))]
-    for end in ends[:5]:
+    for end in ends[3:6]:
         end.start()
     for part in range(1, C):
         mix_back(part)
-    ends[5].start()
+    ends[6].start()
     gc.drain()
     g2.drain()
     g3.drain()
@@ -754,14 +765,23 @@
     P_ = C * HALVES
     rows = S // HALVES
     w, z = lax.axis_index("wide"), lax.axis_index("narrow")
-    loads = [pltpu.make_async_copy(a, b, lsem.at[i]) for i, (a, b) in enumerate(zip(sources, held[:12]))]
-    for load in loads:
+    targets = (sbufm.at[1:2],) + tuple(held[1:12])
+    loads = [pltpu.make_async_copy(a, b, lsem.at[i]) for i, (a, b) in enumerate(zip(sources, targets))]
+    loads[0].start()
+    if push:
+        stage_up = squares[0]
+        blocks = [pltpu.make_async_copy(blk_up.at[q], stage_up.at[q], lsem.at[15 + q]) for q in range(3)]
+        for q in range(3):
+            blocks[q].start()
+    for load in loads[1:6]:
         load.start()
     if push:
         extra = [pltpu.make_async_copy(a, b, lsem.at[12 + i]) for i, (a, b) in enumerate(
             ((mix_hbm, mixv), (db_hbm, dbv), (normed_hbm, normv)))]
         for load in extra:
             load.start()
+    for load in loads[6:]:
+        load.start()
     barrier(n, W)
     sm = Scatter(n, C, S, sbufm, sbufm, rbufm, sms, smr)
     s3 = Scatter(n, C, S, partial, sbuf, rbuf, s3s, s3r)
@@ -772,10 +792,7 @@
         up_sums, out_sums, qkv_sums = [
             Square(squares[i], squares[i + 1], recv, squares[i + 2], squares[i + 3])
             for i, recv in ((0, recv_up), (4, recv_out), (8, recv_qkv))]
-        stage_up, stage_out, stage_qkv = squares[0], squares[4], squares[8]
-        blocks = [pltpu.make_async_copy(blk_up.at[q], stage_up.at[q], lsem.at[15 + q]) for q in range(3)]
-        for q in range(3):
-            blocks[q].start()
+        stage_out, stage_qkv = squares[4], squares[8]
 
         def swap(index, src, dst, part):
             return remote(src.at[part], dst.at[part], sib_ss.at[index, part], sib_rs.at[index, part], mate, z)
@@ -787,11 +804,16 @@
         for q in range(3):
             blocks[q].wait()
             up_sums.put(q)
-        for load in extra:
+
+    def rest_in():
+        for load in loads[6:]:
             load.wait()
-        for part in range(C):
-            for index, (a, b) in enumerate(((mixv, sib_mix), (dbv, sib_db), (normv, sib_norm))):
-                swap(index, a, b, part).start()
+        if push:
+            for load in extra:
+                load.wait()
+            for part in range(C):
+                for index, (a, b) in enumerate(((mixv, sib_mix), (dbv, sib_db), (normv, sib_norm))):
+                    swap(index, a, b, part).start()
 
     def piece_row(p):
         return p // HALVES, rows_at(p % HALVES, rows)
@@ -815,7 +837,7 @@
 
     gains[...] = jnp.zeros_like(gains)
     scale = HD ** (-0.5)
-    for load in loads[1:]:
+    for load in loads[1:6]:
         load.wait()
 
     def unit(part, k):
@@ -845,16 +867,6 @@
         dproj[part, :, lanes(QC // HD + k, HD)] = unturned(dk * scale, raws[part, :, lanes(QC // HD + k, HD)], kgain, 2)
         dproj[part, :, lanes(QC // HD + KH + k, HD)] = dv.astype(BF16)
 
-    per_part = KH + 1
-
-    def between(e):
-        chain(e, HALVES, P_, sm, None, mlp_done, n)
-        chain(e - per_part, 0, HALVES, s3, None, grad_done, n)
-        if push:
-            @when(e == per_part)
-            def _():
-                up_sums.pass_on()
-
     if push:
         def block(A, B, sib_a, sib_b, owner):
             cols = lanes(owner, width)
@@ -883,10 +895,31 @@
             else:
                 own_qkv[...] = block(normv, dproj, sib_norm, sib_dproj, w)
 
+    def grad_step(k):
+        staggered(k, tuple(range(P_)), s3, None, grad_done, n)
+
+    def mlp_step(k):
+        chain(k, HALVES, P_, sm, None, mlp_done, n)
+
+    assert (n, C, HALVES, KH) == (4, 2, 2, 2)
+
     def backward(part):
         def heads(k, carry):
             unit(part, k)
-            between(part * per_part + k)
+
+            @when(both(part == 0, k == 0))
+            def _():
+                rest_in()
+
+            @when(both(part == 0, k == KH - 1))
+            def _():
+                mlp_step(0)
+
+            if push:
+                @when(both(part == 1, k == 0))
+                def _():
+                    up_sums.pass_on()
+
             return carry
 
         lax.fori_loop(0, KH, heads, 0)
@@ -903,32 +936,30 @@
         lax.fori_loop(0, nd, back_tile, 0)
         for h in range(HALVES):
             s3.originate(part * HALVES + h)
-        between(part * per_part + KH)
-        if push:
-            @when(part == 0)
-            def _():
+
+        @when(part == 0)
+        def _():
+            if push:
                 for q in range(3):
                     out_block(q)
+            mlp_step(1)
+            mlp_step(2)
+
+        @when(part == 1)
+        def _():
+            grad_step(0)
 
     def both_parts(part, carry):
         backward(part)
         return carry
 
     lax.fori_loop(0, C, both_parts, 0)
-    done = C * per_part
-    for e in range(done, max(HALVES + 2, per_part + HALVES + 2)):
-        between(e)
-    steps = HALVES + 2
-    if push:
-        work = [[(qkv_block, 0), (out_sums.pass_on,)], [(qkv_block, 1), (qkv_block, 2)], [(qkv_block, 3)],
-                [(out_block, 3), (qkv_sums.pass_on,)]]
-        assert len(work) == steps
-    else:
-        work = [[]] * steps
-    for k in range(steps):
-        chain(k, HALVES, P_, s3, None, grad_done, n)
-        for piece in work[k]:
-            piece[0](*piece[1:])
+    tail = [lambda: mlp_step(3), lambda: grad_step(1), lambda: grad_step(2), lambda: grad_step(3)]
+    if push:
+        tail = [lambda: qkv_block(0), lambda: qkv_block(1), tail[0], lambda: qkv_block(2), tail[1], out_sums.pass_on,
+                lambda: out_block(3), lambda: qkv_block(3), tail[2], tail[3], qkv_sums.pass_on]
+    for piece in tail + [lambda: grad_step(4), lambda: grad_step(5)]:
+        piece()
     if not push:
         out = pltpu.make_async_copy(dproj, dproj_hbm, lsem.at[16])
         out.start()
@@ -1038,7 +1069,7 @@
     full, wide_rows = sds((C, R, D), BF16), sds((C, R, FC), BF16)
     kept = [sds((C, R, QC + KC), F32), sds((C, R, QH * R), F32), sds((C, R, PC), BF16), sds((C, R, 2 * HD), F32),
             sds((C, R, QC), BF16), full]
-    outs = kept + [sds((C, S, D), F32), sds((C, S, D), F32), sds((1, D), F32), sds((C, R, QC), BF16), full, full, sds((1, S, D), F32)]
+    outs = kept + [sds((C, S, D), F32), sds((C, S, D), F32), sds((1, D), F32), sds((C, R, QC), BF16), full, sds((1, R, D), BF16), sds((1, S, D), F32)]
     specs = [hbm] * 8 + [vm] + [hbm] * 4
     line = lambda: [VM((C, R, D), BF16), VM((C, R + S, D), BF16)]
     scratch = (
@@ -1047,7 +1078,7 @@
         + [VM((C, R, D), BF16)] * 3 + [VM((C, R, D), F32)] + line()
         + [VM((C, R, D), BF16), VM((R, FC), F32)] + [VM((C, R, FC), BF16)] * 3 + [VM((S // HALVES, D), F32)]
         + [dma((9,)), gsem(), gsem(), gsem(), gsem(), dma((n, P_)), dma((2, n, P_)), gsem(), gsem(), dma((n, P_)), dma((2, n, P_)),
-           gsem(), gsem(), dma((n, P_)), dma((2, n, P_)), dma((11,)), dma((6, C))]
+           gsem(), gsem(), dma((n, P_)), dma((2, n, P_)), dma((12,)), dma((6, C))]
     )
     if push:
         sums, own = sds((2, width, FC), BF16), sds((width, FC), F32)
@@ -1069,7 +1100,7 @@
     args = [attn_gain, query_gain, key_gain, gmlp, mlp_sums, raws, rots, prob, tabs, d_mix, w_query, w_key, w_value,
             middle, d_middle, x_own]
     in_specs = [vm] * 4 + [hbm] * 12
-    held = [VM(v.shape, v.dtype) for v in args[4:]] + [VM((1, S, D), F32), VM((C, S, D), F32)]
+    held = [VM((C, R, D), BF16)] + [VM(v.shape, v.dtype) for v in args[5:]] + [VM((1, S, D), F32), VM((C, S, D), F32)]
     own_rows = sds((C, S, D), F32)
     outs = [sds((1, S, D), F32), own_rows, sds((D,), F32), sds((D,), F32), sds((HD,), F32), sds((HD,), F32)]
     specs = [hbm] * 2 + [vm] * 4

time: 280 us -> 272 us (0.971)
  Pallas kernels: 279 us -> 271 us
    pallas_call x1, Pallas kernels: 73.7 us -> 68.8 us  [local(): pl.pallas_call(functools.partial(last_kernel, n, C, S, W, HD, push), name...]
    pallas_call x1, Pallas kernels: 197 us -> 194 us  [local(): pl.pallas_call(functools.partial(middle_kernel, n, C, S, W, HD, docs, pus...]
where the time goes in v6:
time: 272 us
  Pallas kernels  271 us (100%)
    pallas_call x1, Pallas kernels, local(): pl.pallas_call(functools.partial(middle_kernel, n, C, S, W, HD, docs, pus...  194 us
    pallas_call x1, Pallas kernels, local(): pl.pallas_call(functools.partial(last_kernel, n, C, S, W, HD, push), name...  68.8 us
    pallas_call x1, Pallas kernels, local(): pl.pallas_call(finish_kernel, name='finish', grid=(grid,), out_shape=[sds...  8.54 us

profile of v6, /device:TPU:0, one launch (start us, length us, event | category | flops | bytes accessed | tf_op | source)
XLA Modules:
  0.0 272.1 jit_solution(10037608377841407555)
XLA Ops:
  0.6 193.9 %middle.1 = (f32[2,256,768]{2,1,0:T(8,128)}, f32[2,256,1024]{2,1,0:T(8,128)}, bf16[2,256,1024]{2,1,0:T(8,128)(2,1)}, f32[2,256,256]{2,1,0:T(8,128)}, bf16[2,256,...) custom-call(s32[2,4]{1,0:T(2,128)} %bitcast.12, ...), custom_call_target="tpu_custom_call" | custom-call | tf_op jit(solution)/shard_map/middle/pallas_call | solution.py:1091
  194.5 68.8 %last.1 = (f32[1,64,2048]{2,1,0:T(8,128)}, f32[2,64,2048]{2,1,0:T(8,128)}, f32[2048]{0:T(1024)}, f32[2048]{0:T(1024)}, f32[128]{0:T(128)}, /*index=5*/f32[128]{0...) custom-call(bf16[2048]{0:T(1024)(128)(2,1)} %refs_0_.1, ...), custom_call_target="tpu_custom_call" | custom-call | tf_op jit(solution)/shard_map/last/pallas_call | solution.py:1129
  263.3 8.5 %finish.1 = (f32[1536,256]{1,0:T(8,128)}, f32[512,256]{1,0:T(8,128)}, f32[256,1536]{1,0:T(8,128)}, f32[256,1536]{1,0:T(8,128)}, f32[256,512]{1,0:T(8,128)}, /*in...) custom-call(f32[256,1536]{1,0:T(8,128)} %get-tuple-element.56.refs_0, ...), custom_call_target="tpu_custom_call" | custom-call | tf_op jit(solution)/shard_map/finish/pallas_call | solution.py:1152

commit v7 on v6

--- a/solution.py
+++ b/solution.py
@@ -298,27 +298,31 @@
 
 
 PLAN = dict(
-    branch_starts=(0, 1, 4, 5), back_starts=(0, 1, 4, 5),
+    branch_starts=(0, 1, 5, 6), back_starts=(0, 1, 5, 6),
     after=dict(
         start=(('input', 0), ('input', 1), ('input', 2), ('input', 3), ('cot0', 0)),
-        out0=(('input', 4), ('input', 5), ('cot0', 1), ('cot0', 2)),
-        attend10=(('branch', 0), ('branch', 1), ('branch', 2), ('cot0', 3)),
-        attend11=(('branch', 3),),
-        out1=(('cot0', 4), ('cot1', 0)),
-        act=(('branch', 4), ('branch', 5), ('branch', 6)),
-        feed01=(('cot1', 1),),
-        feed03=(('branch', 7),),
-        feed05=(('branch', 8), ('cot1', 2)),
-        feed06=(('branch', 9), ('branch', 10), ('cot1', 3), ('cot1', 4)),
+        attend01=(('input', 4),),
+        out0=(('input', 5), ('cot0', 1), ('cot0', 2), ('cot1', 0)),
+        project1=(('branch', 0),),
+        attend10=(('branch', 1), ('branch', 2)),
+        attend11=(('branch', 3), ('cot1', 1)),
+        out1=(('cot0', 3), ('cot0', 4)),
+        act=(('branch', 4), ('branch', 5), ('branch', 6), ('branch', 7)),
+        feed00=(('cot1', 2),),
+        feed03=(('branch', 8),),
+        feed04=(('cot1', 3),),
+        feed06=(('branch', 9), ('branch', 10), ('branch', 11), ('cot1', 4)),
         feed10=(('back', 0),),
         feed11=(('back', 1), ('back', 2)),
         feed14=(('back', 3),),
-        work4=(('back', 4),),
-        work6=(('back', 5), ('back', 6)),
-        work9=(('back', 7), ('mlp', 0)),
-        work11=(('back', 8),),
-        work12=(('mlp', 1),),
-        work13=(('back', 9), ('back', 10), ('mlp', 2), ('mlp', 3), ('mlp', 4)),
+        work1=(('back', 4),),
+        work3=(('back', 5), ('back', 6), ('back', 7)),
+        work5=(('back', 8), ('mlp', 0)),
+        work7=(('back', 9),),
+        work10=(('back', 10), ('mlp', 1)),
+        work11=(('mlp', 2), ('mlp', 3)),
+        work12=(('back', 11),),
+        work13=(('mlp', 4),),
     ),
 )
 
@@ -339,8 +343,8 @@
      dact, act, dg, du, acc, wsem, g1s, g1r, cs, cr, s1s, s1r, g2s, g2r, s2s, s2r, g3s, g3r, sms, smr, osem, vsem) = rest[:40]
     rest = rest[40:]
     if push:
-        (stage_d, stage_g, stage_u, transit_d, transit_g, stage32, cols_sib, b_sib, sib_ss, sib_rs,
-         down_ss, down_rs, gate_ss, gate_rs, lsem, ssem32) = rest
+        (stage_d, stage_g, stage_u, transit_d, transit_g, stage_own, cols_sib, b_sib, sib_ss, sib_rs,
+         down_ss, down_rs, gate_ss, gate_rs, lsem, own_sem) = rest
     R = n * S
     D = x_ref.shape[2]
     FC = wgate.shape[1]
@@ -606,8 +610,8 @@
         for j in range(nd):
             sbufm[part, :, lanes(j, TN)] = dot(act[part], wdown[:, lanes(j, TN)], 1, 0).astype(BF16)
 
-    def mix_back(part):
-        dmix_ref[part] = dot(dbf[part], wout[...], 1, 1).astype(BF16)
+    def mix_back():
+        dmix_ref[0] = dot(dbf[0], wout[...], 1, 1).astype(BF16)
 
     if push:
         width = D // W
@@ -633,7 +637,7 @@
             return weight_block(A, B, lambda part: cols_sib[q, part], b_sib, lanes((owners + (w,))[q], width))
 
         def own_copy(dst, index):
-            return pltpu.make_async_copy(stage32, dst, ssem32.at[index])
+            return pltpu.make_async_copy(stage_own, dst, own_sem.at[index])
 
         def up_copy(q):
             return pltpu.make_async_copy(stage_u.at[q % 2], blk_up.at[q], osem.at[7 + q])
@@ -651,7 +655,7 @@
                 stage_d[q] = block(cotf, act, q).astype(BF16)
                 down.put(q)
             else:
-                stage32[...] = block(cotf, act, q)
+                stage_own[...] = block(cotf, act, q).astype(BF16)
                 own_copy(own_down, 0).start()
 
         def gate_block(q):
@@ -663,7 +667,7 @@
                 gate.put(q)
             else:
                 own_copy(own_down, 0).wait()
-                stage32[...] = block(n2f, dg, q)
+                stage_own[...] = block(n2f, dg, q).astype(BF16)
                 own_copy(own_gate, 1).start()
 
         def up_block(q):
@@ -677,7 +681,7 @@
                 up_copy(q).start()
             else:
                 own_copy(own_gate, 1).wait()
-                stage32[...] = block(n2f, du, q)
+                stage_own[...] = block(n2f, du, q).astype(BF16)
                 own_copy(own_up, 2).start()
 
         work = [[(down_block, q)] for q in range(4)] + [[(gate_block, q)] for q in range(3)] + [
@@ -698,8 +702,9 @@
         ends[1].start()
 
     def first_mix_back():
-        mix_back(0)
+        mix_back()
         ends[2].start()
+        ends[6].start()
 
     work += [[(second_mlp_sums,)], [(first_mix_back,)]]
     for place, pieces in enumerate(work):
@@ -708,9 +713,6 @@
         run("work%d" % place)
     for end in ends[3:6]:
         end.start()
-    for part in range(1, C):
-        mix_back(part)
-    ends[6].start()
     gc.drain()
     g2.drain()
     g3.drain()
@@ -734,29 +736,29 @@
 
 def last_kernel(n, C, S, W, HD, push, *refs):
     gain_ref, qg_ref, kg_ref, gmlp_ref = refs[:4]
-    sources = refs[4:16]
-    rest = list(refs[16:])
-    if push:
-        mix_hbm, db_hbm, normed_hbm, blk_up = rest[:4]
-        rest = rest[4:]
+    sources = refs[4:18]
+    rest = list(refs[18:])
+    if push:
+        mix_hbm, normed_hbm, blk_up = rest[:3]
+        rest = rest[3:]
     out_hbm, in_hbm, ga_ref, gm_ref, gq_ref, gk_ref = rest[:6]
     rest = rest[6:]
     if push:
-        recv_up, recv_out, recv_qkv, own_out, own_qkv = rest[:5]
+        recv_up, recv_out, recv_qkv, own_out_hbm, own_qkv_hbm = rest[:5]
         rest = rest[5:]
     else:
         dproj_hbm = rest[0]
         rest = rest[1:]
-    held = rest[:14]
-    (sbufm, raws, rots, prob_ref, tabs, dmix_ref, wq, wk, wv, middle_ref, dmid_ref, x_ref) = held[:12]
-    out_ref, in_ref = held[12:14]
-    rest = rest[14:]
+    held = rest[:16]
+    (sbufm, raws, rots, prob_ref, tabs, dmix_ref, wq, wk, wv, middle_ref, dmid_ref, x_ref, dbv, wout) = held[:14]
+    out_ref, in_ref = held[14:16]
+    rest = rest[16:]
     (dproj, partial, sbuf, rbuf, rbufm, acc, gains, small, small_two,
      lsem, s3s, s3r, sms, smr, gs1, gr1, gs2, gr2, osem) = rest[:19]
     rest = rest[19:]
     if push:
-        (mixv, dbv, normv, sib_mix, sib_db, sib_norm, sib_dproj, sib_ss, sib_rs) = rest[:9]
-        squares = rest[9:]
+        (mixv, normv, sib_mix, sib_db, sib_norm, sib_dproj, sib_ss, sib_rs, own_out, own_qkv) = rest[:10]
+        squares = rest[10:]
     R, D = n * S, x_ref.shape[2]
     QC, KC = wq.shape[1], wk.shape[1]
     G, KH = QC // KC, KC // HD
@@ -765,19 +767,19 @@
     P_ = C * HALVES
     rows = S // HALVES
     w, z = lax.axis_index("wide"), lax.axis_index("narrow")
-    targets = (sbufm.at[1:2],) + tuple(held[1:12])
+    targets = (sbufm.at[1:2],) + tuple(held[1:5]) + (dmix_ref.at[0:1],) + tuple(held[6:14])
     loads = [pltpu.make_async_copy(a, b, lsem.at[i]) for i, (a, b) in enumerate(zip(sources, targets))]
     loads[0].start()
     if push:
         stage_up = squares[0]
-        blocks = [pltpu.make_async_copy(blk_up.at[q], stage_up.at[q], lsem.at[15 + q]) for q in range(3)]
+        blocks = [pltpu.make_async_copy(blk_up.at[q], stage_up.at[q], lsem.at[16 + q]) for q in range(3)]
         for q in range(3):
             blocks[q].start()
     for load in loads[1:6]:
         load.start()
     if push:
-        extra = [pltpu.make_async_copy(a, b, lsem.at[12 + i]) for i, (a, b) in enumerate(
-            ((mix_hbm, mixv), (db_hbm, dbv), (normed_hbm, normv)))]
+        extra = [pltpu.make_async_copy(a, b, lsem.at[14 + i]) for i, (a, b) in enumerate(
+            ((mix_hbm, mixv), (normed_hbm, normv)))]
         for load in extra:
             load.start()
     for load in loads[6:]:
@@ -872,6 +874,9 @@
             cols = lanes(owner, width)
             return weight_block(A, B, lambda part: sib_a[part, :, cols], sib_b, cols)
 
+        own_copies = [pltpu.make_async_copy(a, b, osem.at[2 + i]) for i, (a, b) in enumerate(
+            ((own_out, own_out_hbm), (own_qkv, own_qkv_hbm)))]
+
         def arrive(*pairs):
             for part in range(C):
                 for index, dst in pairs:
@@ -884,7 +889,8 @@
                 stage_out[q] = block(dbv, mixv, sib_db, sib_mix, out_sums.owners[q]).astype(BF16)
                 out_sums.put(q)
             else:
-                own_out[...] = block(dbv, mixv, sib_db, sib_mix, w)
+                own_out[...] = block(dbv, mixv, sib_db, sib_mix, w).astype(BF16)
+                own_copies[0].start()
 
         def qkv_block(q):
             if q == 0:
@@ -893,7 +899,8 @@
                 stage_qkv[q] = block(normv, dproj, sib_norm, sib_dproj, qkv_sums.owners[q]).astype(BF16)
                 qkv_sums.put(q)
             else:
-                own_qkv[...] = block(normv, dproj, sib_norm, sib_dproj, w)
+                own_qkv[...] = block(normv, dproj, sib_norm, sib_dproj, w).astype(BF16)
+                own_copies[1].start()
 
     def grad_step(k):
         staggered(k, tuple(range(P_)), s3, None, grad_done, n)
@@ -904,6 +911,10 @@
     assert (n, C, HALVES, KH) == (4, 2, 2, 2)
 
     def backward(part):
+        @when(part == 1)
+        def _():
+            dmix_ref[1] = dot(dbv[1], wout[...], 1, 1).astype(BF16)
+
         def heads(k, carry):
             unit(part, k)
 
@@ -961,7 +972,7 @@
     for piece in tail + [lambda: grad_step(4), lambda: grad_step(5)]:
         piece()
     if not push:
-        out = pltpu.make_async_copy(dproj, dproj_hbm, lsem.at[16])
+        out = pltpu.make_async_copy(dproj, dproj_hbm, lsem.at[14])
         out.start()
     ends = [pltpu.make_async_copy(a, b, osem.at[i]) for i, (a, b) in enumerate(((out_ref, out_hbm), (in_ref, in_hbm)))]
     for end in ends:
@@ -1009,6 +1020,8 @@
                 swap(index, a, b, part).wait_send()
         for sums in (up_sums, out_sums, qkv_sums):
             sums.drain()
+        for copy in own_copies:
+            copy.wait()
     else:
         out.wait()
 
@@ -1021,7 +1034,7 @@
     out_ref[0], out_ref[1] = low[0], high[0]
 
     def total(own, parts):
-        value = own[...]
+        value = own[...].astype(F32)
         for i in range(parts.shape[0]):
             value = value + parts[i].astype(F32)
         return value
@@ -1069,11 +1082,11 @@
     full, wide_rows = sds((C, R, D), BF16), sds((C, R, FC), BF16)
     kept = [sds((C, R, QC + KC), F32), sds((C, R, QH * R), F32), sds((C, R, PC), BF16), sds((C, R, 2 * HD), F32),
             sds((C, R, QC), BF16), full]
-    outs = kept + [sds((C, S, D), F32), sds((C, S, D), F32), sds((1, D), F32), sds((C, R, QC), BF16), full, sds((1, R, D), BF16), sds((1, S, D), F32)]
+    outs = kept + [sds((C, S, D), F32), sds((C, S, D), F32), sds((1, D), F32), sds((1, R, QC), BF16), full, sds((1, R, D), BF16), sds((1, S, D), F32)]
     specs = [hbm] * 8 + [vm] + [hbm] * 4
     line = lambda: [VM((C, R, D), BF16), VM((C, R + S, D), BF16)]
     scratch = (
-        [VM((C, S, D), BF16), VM((C, S, D), BF16), VM((C, S, D), F32), VM((C, S, D), F32), VM((1, S, D), F32), VM((C, R, QC), BF16)]
+        [VM((C, S, D), BF16), VM((C, S, D), BF16), VM((C, S, D), F32), VM((C, S, D), F32), VM((1, S, D), F32), VM((1, R, QC), BF16)]
         + [VM((C, R, QC), BF16), VM(w_out.shape, BF16), VM(w_gate.shape, BF16), VM(w_up.shape, BF16), VM(w_down.shape, BF16)]
         + [VM((C, R, D), BF16)] * 3 + [VM((C, R, D), F32)] + line()
         + [VM((C, R, D), BF16), VM((R, FC), F32)] + [VM((C, R, FC), BF16)] * 3 + [VM((S // HALVES, D), F32)]
@@ -1081,10 +1094,10 @@
            gsem(), gsem(), dma((n, P_)), dma((2, n, P_)), dma((12,)), dma((6, C))]
     )
     if push:
-        sums, own = sds((2, width, FC), BF16), sds((width, FC), F32)
+        sums, own = sds((2, width, FC), BF16), sds((width, FC), BF16)
         outs += [full, full, wide_rows, wide_rows, wide_rows, sums, sums, sds((3, width, FC), BF16), own, own, own]
         scratch += [VM((3, width, FC), BF16), VM((3, width, FC), BF16), VM((2, width, FC), BF16), VM((width, FC), BF16),
-                    VM((width, FC), BF16), VM((width, FC), F32), VM((4, C, R, width), BF16), VM((C, R, FC), BF16),
+                    VM((width, FC), BF16), VM((width, FC), BF16), VM((4, C, R, width), BF16), VM((C, R, FC), BF16),
                     dma((5, C)), dma((5, C)), dma((6,)), dma((6,)), dma((6,)), dma((6,)), dma((2, 4, C)), dma((3,))]
     else:
         outs += [full, full, wide_rows, wide_rows, wide_rows]
@@ -1098,9 +1111,10 @@
     middle, d_middle, gmlp, d_mix, db_full, mlp_sums, out_low = res[:7]
 
     args = [attn_gain, query_gain, key_gain, gmlp, mlp_sums, raws, rots, prob, tabs, d_mix, w_query, w_key, w_value,
-            middle, d_middle, x_own]
-    in_specs = [vm] * 4 + [hbm] * 12
-    held = [VM((C, R, D), BF16)] + [VM(v.shape, v.dtype) for v in args[5:]] + [VM((1, S, D), F32), VM((C, S, D), F32)]
+            middle, d_middle, x_own, db_full, w_out]
+    in_specs = [vm] * 4 + [hbm] * 14
+    held = [VM((C, R, D), BF16)] + [VM(v.shape, v.dtype) for v in args[5:9]] + [VM((C, R, QC), BF16)]
+    held += [VM(v.shape, v.dtype) for v in args[10:]] + [VM((1, S, D), F32), VM((C, S, D), F32)]
     own_rows = sds((C, S, D), F32)
     outs = [sds((1, S, D), F32), own_rows, sds((D,), F32), sds((D,), F32), sds((HD,), F32), sds((HD,), F32)]
     specs = [hbm] * 2 + [vm] * 4
@@ -1108,19 +1122,19 @@
     scratch = (
         held + [VM((C, R, PC), BF16), VM((C, R, D), F32)]
         + line() + line()[1:] + [VM((S // HALVES, D), F32), VM((8, D), F32), VM((W, 1, L), F32), VM((n, 1, L), F32)]
-        + [dma((18,)), dma((n, P_)), dma((2, n, P_)), dma((n, P_)), dma((2, n, P_)), dma((W,)), dma((W,)), dma((n,)), dma((n,)),
-           dma((2,))]
+        + [dma((19,)), dma((n, P_)), dma((2, n, P_)), dma((n, P_)), dma((2, n, P_)), dma((W,)), dma((W,)), dma((n,)), dma((n,)),
+           dma((4,))]
     )
     if push:
         sib_n2, sib_cot, sib_act, sib_dg, sib_du, recv_down, recv_gate, blk_up, own_down, own_gate, own_up = res[7:]
-        args += [mix, db_full, normed_full, blk_up]
-        in_specs += [hbm] * 4
+        args += [mix, normed_full, blk_up]
+        in_specs += [hbm] * 3
         outs += [sds((2, width, FC), BF16)] + [sds((2, width, QC), BF16), sds((2, width, PC), BF16),
-                                                       sds((width, QC), F32), sds((width, PC), F32)]
-        specs += [hbm] * 3 + [vm] * 2
-        scratch += [VM((C, R, QC), BF16), VM((C, R, D), BF16), VM((C, R, D), BF16)]
+                                                       sds((width, QC), BF16), sds((width, PC), BF16)]
+        specs += [hbm] * 5
+        scratch += [VM((C, R, QC), BF16), VM((C, R, D), BF16)]
         scratch += [VM((C, R, QC), BF16), VM((C, R, D), BF16), VM((C, R, D), BF16), VM((C, R, PC), BF16)]
-        scratch += [dma((4, C)), dma((4, C))]
+        scratch += [dma((4, C)), dma((4, C)), VM((width, QC), BF16), VM((width, PC), BF16)]
         for cols in (FC, QC, PC):
             scratch += [VM((3, width, cols), BF16), VM((width, cols), BF16), dma((6,)), dma((6,))]
     else:

time: 272 us -> 271 us (level)
  no operation moved by 1% of the time
where the time goes in v7:
time: 271 us
  Pallas kernels  270 us (100%)
    pallas_call x1, Pallas kernels, local(): pl.pallas_call(functools.partial(middle_kernel, n, C, S, W, HD, docs, pus...  193 us
    pallas_call x1, Pallas kernels, local(): pl.pallas_call(functools.partial(last_kernel, n, C, S, W, HD, push), name...  68.8 us
    pallas_call x1, Pallas kernels, local(): pl.pallas_call(finish_kernel, name='finish', grid=(grid,), out_shape=[sds...  7.88 us

profile of v7, /device:TPU:0, one launch (start us, length us, event | category | flops | bytes accessed | tf_op | source)
XLA Modules:
  0.0 271.0 jit_solution(587310148653308404)
XLA Ops:
  0.6 193.5 %middle.1 = (f32[2,256,768]{2,1,0:T(8,128)}, f32[2,256,1024]{2,1,0:T(8,128)}, bf16[2,256,1024]{2,1,0:T(8,128)(2,1)}, f32[2,256,256]{2,1,0:T(8,128)}, bf16[2,256,...) custom-call(s32[2,4]{1,0:T(2,128)} %bitcast.12, ...), custom_call_target="tpu_custom_call" | custom-call | tf_op jit(solution)/shard_map/middle/pallas_call | solution.py:1104
  194.1 68.8 %last.1 = (f32[1,64,2048]{2,1,0:T(8,128)}, f32[2,64,2048]{2,1,0:T(8,128)}, f32[2048]{0:T(1024)}, f32[2048]{0:T(1024)}, f32[128]{0:T(128)}, /*index=5*/f32[128]{0...) custom-call(bf16[2048]{0:T(1024)(128)(2,1)} %refs_0_.1, ...), custom_call_target="tpu_custom_call" | custom-call | tf_op jit(solution)/shard_map/last/pallas_call | solution.py:1143
  262.9 7.9 %finish.1 = (f32[1536,256]{1,0:T(8,128)}, f32[512,256]{1,0:T(8,128)}, f32[256,1536]{1,0:T(8,128)}, f32[256,1536]{1,0:T(8,128)}, f32[256,512]{1,0:T(8,128)}, /*in...) custom-call(bf16[256,1536]{1,0:T(8,128)(2,1)} %get-tuple-element.56., ...), custom_call_target="tpu_custom_call" | custom-call | tf_op jit(solution)/shard_map/finish/pallas_call | solution.py:1166

commit v8 on v7

--- a/solution.py
+++ b/solution.py
@@ -753,9 +753,9 @@
     (sbufm, raws, rots, prob_ref, tabs, dmix_ref, wq, wk, wv, middle_ref, dmid_ref, x_ref, dbv, wout) = held[:14]
     out_ref, in_ref = held[14:16]
     rest = rest[16:]
-    (dproj, partial, sbuf, rbuf, rbufm, acc, gains, small, small_two,
-     lsem, s3s, s3r, sms, smr, gs1, gr1, gs2, gr2, osem) = rest[:19]
-    rest = rest[19:]
+    (dproj, partial, sbuf, rbuf, rbufm, acc, gains, small, small_two, others, others_two,
+     lsem, s3s, s3r, sms, smr, gs1, gr1, gs2, gr2, osem) = rest[:21]
+    rest = rest[21:]
     if push:
         (mixv, normv, sib_mix, sib_db, sib_norm, sib_dproj, sib_ss, sib_rs, own_out, own_qkv) = rest[:10]
         squares = rest[10:]
@@ -902,6 +902,49 @@
                 own_qkv[...] = block(normv, dproj, sib_norm, sib_dproj, w).astype(BF16)
                 own_copies[1].start()
 
+    def to_wide(ref, index, s):
+        return remote(ref.at[w], ref.at[w], gs1.at[index, s], gr1.at[index, s], lax.rem(w + s, W), z)
+
+    def to_narrow(ref, index, s):
+        return remote(ref.at[z], ref.at[z], gs2.at[index, s], gr2.at[index, s], w, lax.rem(z + s, n))
+
+    def send_wide(ref, index):
+        for s in range(1, W):
+            to_wide(ref, index, s).start()
+
+    def send_narrow(ref, two, index):
+        for s in range(1, W):
+            to_wide(ref, index, s).wait_recv()
+        total = ref[0]
+        for s in range(1, W):
+            total = total + ref[s]
+        two[z] = total
+        for s in range(1, n):
+            to_narrow(two, index, s).start()
+
+    def summed(two, index):
+        for s in range(1, n):
+            to_narrow(two, index, s).wait_recv()
+        total = two[0]
+        for s in range(1, n):
+            total = total + two[s]
+        return total
+
+    def exchange(ref, two, index, value):
+        ref[w] = value
+        send_wide(ref, index)
+        send_narrow(ref, two, index)
+        return summed(two, index)
+
+    def early_gains(stage):
+        if stage == 0:
+            others[w, :, 0:D] = gmlp_ref[...]
+            others[w, :, D:D + HD] = gains[1:2, :HD]
+            others[w, :, D + HD:D + 2 * HD] = gains[2:3, :HD]
+            send_wide(others, 1)
+            return None
+        return summed(others_two, 1)
+
     def grad_step(k):
         staggered(k, tuple(range(P_)), s3, None, grad_done, n)
 
@@ -969,7 +1012,8 @@
     if push:
         tail = [lambda: qkv_block(0), lambda: qkv_block(1), tail[0], lambda: qkv_block(2), tail[1], out_sums.pass_on,
                 lambda: out_block(3), lambda: qkv_block(3), tail[2], tail[3], qkv_sums.pass_on]
-    for piece in tail + [lambda: grad_step(4), lambda: grad_step(5)]:
+    early_gains(0)
+    for piece in tail + [lambda: send_narrow(others, others_two, 1), lambda: grad_step(4), lambda: grad_step(5)]:
         piece()
     if not push:
         out = pltpu.make_async_copy(dproj, dproj_hbm, lsem.at[14])
@@ -977,39 +1021,16 @@
     ends = [pltpu.make_async_copy(a, b, osem.at[i]) for i, (a, b) in enumerate(((out_ref, out_hbm), (in_ref, in_hbm)))]
     for end in ends:
         end.start()
-    L = 2 * D + 2 * HD
-    small[w, :, 0:D] = gains[0:1, :]
-    small[w, :, D:2 * D] = gmlp_ref[...]
-    small[w, :, 2 * D:2 * D + HD] = gains[1:2, :HD]
-    small[w, :, 2 * D + HD:L] = gains[2:3, :HD]
-
-    def to_wide(s):
-        return remote(small.at[w], small.at[w], gs1.at[s], gr1.at[s], lax.rem(w + s, W), z)
-
-    def to_narrow(s):
-        return remote(small_two.at[z], small_two.at[z], gs2.at[s], gr2.at[s], w, lax.rem(z + s, n))
-
-    for s in range(1, W):
-        to_wide(s).start()
-    for s in range(1, W):
-        to_wide(s).wait_recv()
-    total = small[0]
-    for s in range(1, W):
-        total = total + small[s]
-    small_two[z] = total
-    for s in range(1, n):
-        to_narrow(s).start()
-    for s in range(1, n):
-        to_narrow(s).wait_recv()
-    total = small_two[0]
-    for s in range(1, n):
-        total = total + small_two[s]
-    for ref, lo, hi in ((ga_ref, 0, D), (gm_ref, D, 2 * D), (gq_ref, 2 * D, 2 * D + HD), (gk_ref, 2 * D + HD, L)):
-        ref[...] = total[:, lo:hi].reshape(hi - lo)
-    for s in range(1, W):
-        to_wide(s).wait_send()
-    for s in range(1, n):
-        to_narrow(s).wait_send()
+    finish_others = early_gains(1)
+    attn = exchange(small, small_two, 0, gains[0:1, :])
+    for ref, lo, hi in ((gm_ref, 0, D), (gq_ref, D, D + HD), (gk_ref, D + HD, D + 2 * HD)):
+        ref[...] = finish_others[:, lo:hi].reshape(hi - lo)
+    ga_ref[...] = attn.reshape(D)
+    for index, (first, second) in enumerate(((small, small_two), (others, others_two))):
+        for s in range(1, W):
+            to_wide(first, index, s).wait_send()
+        for s in range(1, n):
+            to_narrow(second, index, s).wait_send()
     sm.drain(HALVES, P_)
     s3.drain()
     for end in ends:
@@ -1062,7 +1083,7 @@
     FC = w_gate.shape[1]
     docs = document_lengths.shape[2]
     P_ = C * HALVES
-    grid = 4
+    grid = 2
     push = (W == 8 and (D // W) % 128 == 0 and FC % (128 * grid) == 0 and QC % (128 * grid) == 0
             and S % (8 * grid) == 0)
     assert C == 2
@@ -1118,11 +1139,11 @@
     own_rows = sds((C, S, D), F32)
     outs = [sds((1, S, D), F32), own_rows, sds((D,), F32), sds((D,), F32), sds((HD,), F32), sds((HD,), F32)]
     specs = [hbm] * 2 + [vm] * 4
-    L = 2 * D + 2 * HD
+    L = D + 2 * HD
     scratch = (
         held + [VM((C, R, PC), BF16), VM((C, R, D), F32)]
-        + line() + line()[1:] + [VM((S // HALVES, D), F32), VM((8, D), F32), VM((W, 1, L), F32), VM((n, 1, L), F32)]
-        + [dma((19,)), dma((n, P_)), dma((2, n, P_)), dma((n, P_)), dma((2, n, P_)), dma((W,)), dma((W,)), dma((n,)), dma((n,)),
+        + line() + line()[1:] + [VM((S // HALVES, D), F32), VM((8, D), F32), VM((W, 1, D), F32), VM((n, 1, D), F32), VM((W, 1, L), F32), VM((n, 1, L), F32)]
+        + [dma((19,)), dma((n, P_)), dma((2, n, P_)), dma((n, P_)), dma((2, n, P_)), dma((2, W)), dma((2, W)), dma((2, n)), dma((2, n)),
            dma((4,))]
     )
     if push:

time: 271 us -> 271 us (level)
  no operation moved by 1% of the time
where the time goes in v8:
time: 271 us
  Pallas kernels  270 us (100%)
    pallas_call x1, Pallas kernels, local(): pl.pallas_call(functools.partial(middle_kernel, n, C, S, W, HD, docs, pus...  193 us
    pallas_call x1, Pallas kernels, local(): pl.pallas_call(functools.partial(last_kernel, n, C, S, W, HD, push), name...  68.7 us
    pallas_call x1, Pallas kernels, local(): pl.pallas_call(finish_kernel, name='finish', grid=(grid,), out_shape=[sds...  7.58 us

profile of v8, /device:TPU:0, one launch (start us, length us, event | category | flops | bytes accessed | tf_op | source)
XLA Modules:
  0.0 270.6 jit_solution(3037029907650731973)
XLA Ops:
  0.6 193.5 %middle.1 = (f32[2,256,768]{2,1,0:T(8,128)}, f32[2,256,1024]{2,1,0:T(8,128)}, bf16[2,256,1024]{2,1,0:T(8,128)(2,1)}, f32[2,256,256]{2,1,0:T(8,128)}, bf16[2,256,...) custom-call(s32[2,4]{1,0:T(2,128)} %bitcast.12, ...), custom_call_target="tpu_custom_call" | custom-call | tf_op jit(solution)/shard_map/middle/pallas_call | solution.py:1125
  194.1 68.7 %last.1 = (f32[1,64,2048]{2,1,0:T(8,128)}, f32[2,64,2048]{2,1,0:T(8,128)}, f32[2048]{0:T(1024)}, f32[2048]{0:T(1024)}, f32[128]{0:T(128)}, /*index=5*/f32[128]{0...) custom-call(bf16[2048]{0:T(1024)(128)(2,1)} %refs_0_.1, ...), custom_call_target="tpu_custom_call" | custom-call | tf_op jit(solution)/shard_map/last/pallas_call | solution.py:1164
  262.8 7.6 %finish.1 = (f32[1536,256]{1,0:T(8,128)}, f32[512,256]{1,0:T(8,128)}, f32[256,1536]{1,0:T(8,128)}, f32[256,1536]{1,0:T(8,128)}, f32[256,512]{1,0:T(8,128)}, /*in...) custom-call(bf16[256,1536]{1,0:T(8,128)(2,1)} %get-tuple-element.56., ...), custom_call_target="tpu_custom_call" | custom-call | tf_op jit(solution)/shard_map/finish/pallas_call | solution.py:1187
